TPU v7x, 32 devices: a whole 2x2x4 slice. The times are simulated.
32 devices in a mesh: patch: 16 (over z, x, core), sample: 2 (over y).
Axes of the slice: x: 2, y: 2, z: 4, core: 2. Of those that a mesh axis runs over, the one named last changes fastest.
Arguments:
- nodes: bfloat16 [8, 8192, 512], P('sample', 'patch'), may hold values from -6 to 6
- neighbours: int32 [8192, 16], P('patch'), may hold values from 0 to 767
- send_rows: int32 [64, 64], P('patch'), may hold values from 0 to 511
- noise_code: float32 [8, 16], P('sample'), may hold values from -5 to 5
- w_query: bfloat16 [512, 512], P(('patch', 'sample')), may hold values from -0.25 to 0.25
- w_key: bfloat16 [512, 512], P(('patch', 'sample')), may hold values from -0.25 to 0.25
- w_value: bfloat16 [512, 512], P(('patch', 'sample')), may hold values from -0.25 to 0.25
- w_out: bfloat16 [512, 512], P(('patch', 'sample')), may hold values from -0.5 to 0.5
- w_up: bfloat16 [512, 2048], P(('patch', 'sample')), may hold values from -0.25 to 0.25
- b_up: bfloat16 [2048], P(('patch', 'sample')), may hold values from -3 to 3
- w_down: bfloat16 [2048, 512], P(('patch', 'sample')), may hold values from -0.1875 to 0.1875
- b_down: bfloat16 [512], P(('patch', 'sample')), may hold values from -3 to 3
- cond_weight: bfloat16 [16, 2048], P(None, ('patch', 'sample')), may hold values from -1 to 1
- cond_bias: bfloat16 [2048], P(('patch', 'sample')), may hold values from -2 to 2
- cotangent: bfloat16 [8, 8192, 512], P('sample', 'patch'), may hold values from -6 to 6
Outputs:
- out_nodes: bfloat16 [8, 8192, 512], P('sample', 'patch')
- grad_nodes: float32 [8, 8192, 512], P('sample', 'patch')
- grad_query: float32 [512, 512], P(('patch', 'sample'))
- grad_key: float32 [512, 512], P(('patch', 'sample'))
- grad_value: float32 [512, 512], P(('patch', 'sample'))
- grad_out: float32 [512, 512], P(('patch', 'sample'))
- grad_up: float32 [512, 2048], P(('patch', 'sample'))
- grad_b_up: float32 [2048], P(('patch', 'sample'))
- grad_down: float32 [2048, 512], P(('patch', 'sample'))
- grad_b_down: float32 [512], P(('patch', 'sample'))
- grad_cond_weight: float32 [16, 2048], P(None, ('patch', 'sample'))
- grad_cond_bias: float32 [2048], P(('patch', 'sample'))
Inputs may be any that keep to these rules, and one draw needn't show every extreme that they name: `send_rows`: row 4 q + b lists local node numbers of patch q; repeats are allowed.
All inputs are finite; a program needn't handle non-finite values.
Results may differ from a plain program's by a relative error of at most 0.014.
The roundings to bfloat16 on the way count: a program that leaves them out, or rounds other values in their place, can miss the bound.
Values may be sent and summed in bfloat16 or wider, within the bound.
No kernel may reach another device: no remote copies, remote signals or barrier semaphores. Data moves between devices by JAX's collectives and lax.ppermute only.
A program may use at most 320 MiB of HBM per device.

v0:
```python
import math

import jax
import jax.numpy as jnp
from jax import lax
from jax.experimental import pallas as pl
from jax.experimental.pallas import tpu as pltpu
from jax.sharding import PartitionSpec as P


HEAD = 128
STRIDE = 4
BLOCK = 16
AXES = ("patch", "sample")
EPSILON = 1e-05
F32 = jnp.float32
BF16 = jnp.bfloat16
MIB = 1024 * 1024


def product(left, right):
    return jnp.dot(left, right, preferred_element_type=F32)


def product_t(left, right):
    return lax.dot_general(left, right, (((1,), (1,)), ((), ())), preferred_element_type=F32)


def from_behind(block, distance):
    count = lax.axis_size("patch")
    return lax.ppermute(block, "patch", [((i - distance) % count, i) for i in range(count)])


def swap(block, bits, devices):
    return lax.ppermute(block, AXES, [(i, i ^ bits) for i in range(devices)])


def stage_groups(devices):
    bits = [1 << i for i in reversed(range(devices.bit_length() - 1)) if (1 << i) != 2]
    groups = [bits[i : i + 2] for i in range(0, len(bits), 2)]
    return [combos(g) for g in groups] + [[2]]


def combos(group):
    if len(group) == 1:
        return [group[0]]
    high, low = group
    return [low, high, low | high]


def relative(k, devices):
    shift, out = 0, 0
    for group in stage_groups(devices):
        if len(group) == 1:
            out = out | (((k >> shift) & 1) * group[0])
            shift += 1
        else:
            out = out | (((k >> shift) & 1) * group[0]) | (((k >> (shift + 1)) & 1) * group[1])
            shift += 2
    return out


def join_kernel(*refs):
    at = 0
    for ref in refs[:-1]:
        refs[-1][at : at + ref.shape[0]] = ref[...]
        at += ref.shape[0]


def join(pieces):
    count = sum(piece.shape[0] for piece in pieces)
    return pl.pallas_call(
        join_kernel,
        out_shape=jax.ShapeDtypeStruct((count,) + pieces[0].shape[1:], pieces[0].dtype),
        compiler_params=plain(8),
    )(*pieces)


def after(value, *others):
    return lax.optimization_barrier((value,) + others)[0]


def layer_normalize(values):
    centre = jnp.mean(values, axis=-1, keepdims=True)
    centred = values - centre
    inverse = lax.rsqrt(jnp.mean(centred * centred, axis=-1, keepdims=True) + EPSILON)
    return centred * inverse, inverse


def norm_back(grad_hat, normed, inverse):
    first = jnp.mean(grad_hat, axis=-1, keepdims=True)
    second = jnp.mean(grad_hat * normed, axis=-1, keepdims=True)
    return inverse * (grad_hat - first - normed * second)


def whole(shape):
    return pl.BlockSpec(shape, lambda *_: (0,) * len(shape))


def once(shape):
    return pl.BlockSpec(shape, lambda *_: (0,) * len(shape), pipeline_mode=pl.Buffered(1))


def per_sample(shape, begin=0):
    return pl.BlockSpec((1,) + shape, lambda s, *_: (s + begin,) + (0,) * len(shape))


def anywhere():
    return pl.BlockSpec(memory_space=pl.ANY)


def params(limit, axes=1):
    return pltpu.CompilerParams(
        dimension_semantics=("arbitrary",) * axes, vmem_limit_bytes=limit * MIB
    )


def plain(limit):
    return pltpu.CompilerParams(vmem_limit_bytes=limit * MIB)


def bias_kernel(nbr_ref, bias_ref):
    table, count = bias_ref.shape
    height = 2 * BLOCK
    row = lax.broadcasted_iota(jnp.int32, (height, count), 0)
    slots = nbr_ref[...]

    def block(i, _):
        begin = pl.multiple_of(i * height, height)
        total = jnp.zeros((height, count), F32)
        for j in range(slots.shape[0]):
            total = total + jnp.where(row == slots[j : j + 1, :] - begin, 1.0, 0.0)
        bias_ref[pl.ds(begin, height), :] = jnp.where(
            total > 0.0, jnp.log2(jnp.maximum(total, 1.0)), -1e30
        )
        return 0

    lax.fori_loop(0, table // height, block, 0)


def slot_bias(neighbours, table):
    return pl.pallas_call(
        bias_kernel,
        out_shape=jax.ShapeDtypeStruct((table, neighbours.shape[0]), F32),
        compiler_params=plain(8),
    )(neighbours.T)


def pick_rows(nodes_ref, send_ref, out_refs):
    samples, count, _ = nodes_ref.shape
    each = send_ref.shape[1]
    lanes = lax.broadcasted_iota(jnp.int32, (each, count), 1)
    columns = send_ref[...].T
    for d, out_ref in enumerate(out_refs):
        chosen = jnp.where(lanes == columns[:, d : d + 1], 1.0, 0.0).astype(BF16)
        for s in range(samples):
            out_ref[s] = product(chosen, nodes_ref[s]).astype(BF16)


def blocks_of(ref):
    height, width = ref.shape
    for r in range(0, height, BLOCK):
        for c in range(0, width, 128):
            yield slice(r, r + BLOCK), slice(c, c + 128)


def pack_shards(weights, first_ref, second_ref):
    wq, wk, wv, cw, cb, wo, wu, bu, wd, bd = weights
    for source, ref in (((wq, wk, wv), first_ref), ((wu, wd, wo), second_ref)):
        at = 0
        for part in source:
            for rows, cols in blocks_of(part):
                ref[0, at : at + BLOCK, :] = part[rows, cols]
                at += BLOCK
        ref[0, at : at + BLOCK, :] = jnp.zeros((BLOCK, 128), BF16)
    at = first_ref.shape[1] - BLOCK
    first_ref[0, at : at + BLOCK, 0 : cw.shape[1]] = cw[...]
    first_ref[0, at : at + 1, cb.shape[1] :] = cb[...]
    at = second_ref.shape[1] - BLOCK
    for row, part in enumerate((bu, bd)):
        step = part.shape[1]
        for c in range(0, 128, step):
            second_ref[0, at + row : at + row + 1, c : c + step] = part[...]


def begin_kernel(*refs, ways, given):
    nodes_ref, send_ref = refs[:2]
    weights, out_refs = refs[2 : 2 + given], refs[2 + given : 2 + given + ways]
    pick_rows(nodes_ref, send_ref, out_refs)
    if weights:
        pack_shards(weights, *refs[-2:])


def begin(nodes, send_rows, weights=()):
    samples, _, width = nodes.shape
    ways, each = send_rows.shape
    weights = [w if w.ndim == 2 else w[None] for w in weights]
    shards = []
    if weights:
        wq, wk, wv, _, _, wo, wu, _, wd, _ = weights
        for group in ((wq, wk, wv), (wo, wu, wd)):
            rows = sum(w.size for w in group) // 128 + BLOCK
            shards.append(jax.ShapeDtypeStruct((1, rows, 128), BF16))
    return pl.pallas_call(
        lambda *refs: begin_kernel(*refs, ways=ways, given=len(weights)),
        out_shape=[jax.ShapeDtypeStruct((samples, each, width), BF16)] * ways + shards,
        compiler_params=plain(60),
    )(nodes, send_rows, *weights)


def spread(rows, step, width):
    reps = jnp.concatenate([rows] * (width // 128), axis=1)
    lane = lax.broadcasted_iota(jnp.int32, reps.shape, 1)
    row = lax.broadcasted_iota(jnp.int32, reps.shape, 0)
    return jnp.sum(jnp.where(lane // step == row, reps, 0.0), axis=0, keepdims=True)


def place(source, k, shard, targets):
    at = 0
    for ref, height in targets:
        for r in range(0, height, BLOCK):
            rows = pl.ds(pl.multiple_of(shard * height + r, BLOCK), BLOCK)
            for c in range(0, ref.shape[1], 128):
                ref[rows, c : c + 128] = source[k, at : at + BLOCK, :]
                at += BLOCK
    return at


def for_shards(pieces, take, arriving=()):
    at = 0
    for n, ref in enumerate(pieces):
        if arriving:
            arriving[n].wait()

        def step(i, _, ref=ref, at=at):
            take(at + i, ref, i)
            return 0

        lax.fori_loop(0, ref.shape[0], step, 0, unroll=2)
        at += ref.shape[0]


def place_first(me_ref, pieces, code_ref, wq_ref, wk_ref, wv_ref, mod_ref, raw):
    devices = sum(ref.shape[0] for ref in pieces)
    samples = code_ref.shape[0]
    width = wq_ref.shape[1]
    step = 4 * width // devices
    lane = lax.broadcasted_iota(jnp.int32, (BLOCK, 128), 1)
    columns = code_ref[...].T
    code = [jnp.where(lane < 64, columns[:, s : s + 1], 1.0) for s in range(samples)]

    def take(k, source, i):
        shard = me_ref[0] ^ relative(k, devices)
        targets = ((wq_ref, BLOCK), (wk_ref, BLOCK), (wv_ref, BLOCK))
        at = place(source, i, shard, targets)
        cond = source[i, at : at + BLOCK, :].astype(F32)
        for s in range(samples):
            value = jnp.sum(cond * code[s], axis=0, keepdims=True)
            raw[s, pl.ds(shard, 1), :] = value + pltpu.roll(value, 64, 1)

    for_shards(pieces, take)
    each = devices // 4
    for s in range(samples):
        for kind in range(4):
            value = spread(raw[s, kind * each : (kind + 1) * each, :], step, width)
            mod_ref[s, kind : kind + 1, :] = value + 1.0 if kind % 2 == 0 else value


def place_second(me_ref, pieces, arriving, wo_ref, wu_ref, wd_ref, bu_ref, bd_ref, raw):
    devices = sum(ref.shape[0] for ref in pieces)
    width = wo_ref.shape[1]
    hidden = wu_ref.shape[1]

    def take(k, source, i):
        shard = me_ref[0] ^ relative(k, devices)
        targets = ((wu_ref, BLOCK), (wd_ref, hidden // devices), (wo_ref, BLOCK))
        at = place(source, i, shard, targets)
        extra = source[i, at : at + BLOCK, :].astype(F32)
        raw[0, pl.ds(shard, 1), :] = extra[0:1]
        raw[1, pl.ds(shard, 1), :] = extra[1:2]

    for_shards(pieces, take, arriving)
    each = devices // (hidden // width)
    for c in range(hidden // width):
        bu_ref[:, c * width : (c + 1) * width] = spread(
            raw[0, c * each : (c + 1) * each, :], hidden // devices, width
        )
    bd_ref[...] = spread(raw[1], width // devices, width)


def packs(width, devices):
    return width == devices * BLOCK


def gather_plain(wq, wk, wv, cond_weight, cond_bias, noise_code, wo, wu, bu, wd, bd):
    def full(x, axis=0):
        return lax.all_gather(x, AXES, axis=axis, tiled=True)

    mod = jnp.dot(
        noise_code, full(cond_weight, 1).astype(F32), precision=lax.Precision.HIGHEST
    ) + full(cond_bias).astype(F32)
    mod = mod.reshape(noise_code.shape[0], 4, wq.shape[1])
    mod = mod + jnp.array([1.0, 0.0, 1.0, 0.0], F32)[:, None]
    first = (full(wq), full(wk), full(wv), mod)
    biases = (full(bu)[None].astype(F32), full(bd)[None].astype(F32))
    return first, (full(wo), full(wu), full(wd)) + biases


def scatter_plain(sums, axes):
    return [
        lax.psum_scatter(x, AXES, scatter_dimension=axis, tiled=True)
        for x, axis in zip(sums, axes)
    ]


def add_kernel(own_ref, far_ref, *out_refs):
    size = out_refs[0].shape[0]
    for i, out_ref in enumerate(out_refs):
        part = slice(i * size, (i + 1) * size)
        out_ref[...] = own_ref[part] + far_ref[part]


def add_halves(own_half, far_half, parts):
    count, rows, lanes = own_half.shape
    return pl.pallas_call(
        add_kernel,
        out_shape=[jax.ShapeDtypeStruct((count // parts, rows, lanes), BF16)] * parts,
        compiler_params=plain(16),
    )(own_half, far_half)


def add_more_kernel(*refs):
    sources, outs = refs[: -refs[0].shape[0]], refs[-refs[0].shape[0] :]
    for i, out_ref in enumerate(outs):
        total = sources[0][i].astype(F32)
        for ref in sources[1:]:
            total = total + ref[i].astype(F32)
        out_ref[0] = total.astype(BF16)


def add_pieces(pieces):
    count, rows, lanes = pieces[0].shape
    return pl.pallas_call(
        add_more_kernel,
        out_shape=[jax.ShapeDtypeStruct((1, rows, lanes), BF16)] * count,
        compiler_params=plain(8),
    )(*pieces)


def last_kernel(*refs, pieces, first):
    me_ref = refs[0]
    sources, outs = refs[1 : 1 + pieces], refs[1 + pieces :]
    position = me_ref[0]

    def total(at, height):
        value = sources[0][0, at : at + height, :].astype(F32)
        for ref in sources[1:]:
            value = value + ref[0, at : at + height, :].astype(F32)
        return value

    at = 0
    for ref in outs[:3]:
        for rows, cols in blocks_of(ref):
            ref[rows, cols] = total(at, BLOCK)
            at += BLOCK
    if first:
        cond = total(at, BLOCK)
        step = outs[3].shape[1]
        begin = lax.rem(position * step, 128)
        outs[3][...] = pltpu.roll(cond, 128 - begin, 1)[:, 0:step]
        bias = total(at + BLOCK, BLOCK)
        outs[4][...] = pltpu.roll(bias, 128 - begin, 1)[0:1, 0:step]
    else:
        last = total(at, BLOCK)
        for row, ref in enumerate(outs[3:]):
            step = ref.shape[1]
            begin = lax.rem(position * step, 128)
            ref[...] = pltpu.roll(last, 128 - begin, 1)[row : row + 1, 0:step]


def last_sum(me, pieces, shapes, first):
    return pl.pallas_call(
        lambda *refs: last_kernel(*refs, pieces=len(pieces), first=first),
        out_shape=[jax.ShapeDtypeStruct(shape, F32) for shape in shapes],
        in_specs=[smem()] + [pl.BlockSpec(memory_space=pltpu.VMEM)] * len(pieces),
        compiler_params=plain(60),
    )(me, *pieces)


def smem():
    return pl.BlockSpec(memory_space=pltpu.SMEM)


def attend_kernel(*refs, pieces):
    nodes_ref, h0, h1, h2, h3, bias_ref = refs[:6]
    buffers, sems = refs[-7:-1], refs[-1]
    act_buf, q_buf, k_buf, v_buf, p_buf, att_buf = buffers
    s, last = pl.program_id(0), pl.num_programs(0) - 1
    if pieces:
        me_ref, code_ref = refs[6:8]
        shards = refs[8 : 8 + pieces]
        wq_ref, wk_ref, wv_ref, mod_ref = refs[8 + pieces : 12 + pieces]
        raw = refs[18 + pieces]
        outs = refs[12 + pieces : 18 + pieces]

        @pl.when(s == 0)
        def _():
            place_first(me_ref, shards, code_ref, wq_ref, wk_ref, wv_ref, mod_ref, raw)

        at = s
    else:
        mod_ref, wq_ref, wk_ref, wv_ref = refs[6:10]
        outs = refs[10:16]
        at = 0
    heads_count = p_buf.shape[1]
    slot = lax.rem(s, 2)

    def copies(sample, place, arrays, some_heads):
        made = [(buffers[i].at[place], outs[i].at[sample], sems.at[place, i]) for i in arrays]
        for h in some_heads:
            made.append((p_buf.at[place, h], outs[4].at[sample, h], sems.at[place, 6 + h]))
        return [pltpu.make_async_copy(*parts) for parts in made]

    def wait_for(sample, place):
        for copy in copies(sample, place, (0, 1, 2, 3, 5), range(heads_count)):
            copy.wait()

    @pl.when(s > 1)
    def _():
        wait_for(s - 2, slot)

    count, _ = nodes_ref.shape[1:]
    each = h0.shape[1]
    scale, shift = mod_ref[at, 0:1, :], mod_ref[at, 1:2, :]

    def activate(rows):
        hat, _ = layer_normalize(rows.astype(F32))
        return (hat * scale + shift).astype(BF16)

    act_buf[slot, 0:count, :] = activate(nodes_ref[0])
    for d, ref in enumerate((h0, h1, h2, h3)):
        begin = count + d * each
        act_buf[slot, begin : begin + each, :] = activate(ref[0])
    act = act_buf[slot]
    for copy in copies(s, slot, (0,), ()):
        copy.start()
    factor = math.log2(math.e) * HEAD ** (-0.5)
    heads = [slice(h * HEAD, (h + 1) * HEAD) for h in range(heads_count)]

    def project(h):
        if h % 2 or h >= heads_count:
            return
        cols = slice(h * HEAD, min(h + 2, heads_count) * HEAD)
        q_buf[slot, :, cols] = product(act[0:count], wq_ref[:, cols]).astype(BF16)
        k_buf[slot, :, cols] = product(act, wk_ref[:, cols]).astype(BF16)
        v_buf[slot, :, cols] = product(act, wv_ref[:, cols]).astype(BF16)

    def score(cols):
        return product_t(k_buf[slot, :, cols], q_buf[slot, :, cols])

    early = max(heads_count - 3, 0)
    project(0)
    following = score(heads[0])
    for h, cols in enumerate(heads):
        scores = following
        project(h + 2)
        if h + 1 < heads_count:
            following = score(heads[h + 1])
        scores = scores * factor + bias_ref[...]
        top = jnp.max(scores, axis=0, keepdims=True)
        expo = jnp.exp2(scores - top)
        total = jnp.sum(expo, axis=0, keepdims=True)
        probs = (expo * (1.0 / total)).astype(BF16)
        p_buf[slot, h] = probs
        att_buf[slot, :, cols] = product(v_buf[slot, :, cols].T, probs).T.astype(BF16)
        if h == early:
            for copy in copies(s, slot, (1, 2, 3), range(early + 1)):
                copy.start()
    for copy in copies(s, slot, (5,), range(early + 1, heads_count)):
        copy.start()

    @pl.when(s == last)
    def _():
        wait_for(s, slot)

        @pl.when(s > 0)
        def _():
            wait_for(s - 1, 1 - slot)


def attend(nodes, halos, bias, weights=None, shards=None):
    samples, count, width = nodes.shape
    table = bias.shape[0]
    heads = width // HEAD
    each = halos[0].shape[1]
    square = jax.ShapeDtypeStruct((width, width), BF16)
    mod_shape = jax.ShapeDtypeStruct((samples, 4, width), F32)
    tile = per_sample
    in_specs = [tile((count, width))] + [tile((each, width))] * 4 + [once((table, count))]
    args = [nodes, *halos, bias]
    out_specs, out_shape, scratch = [], [], []
    if shards is None:
        wq, wk, wv, mod = weights
        in_specs += [tile((4, width))] + [once((width, width))] * 3
        args += [mod, wq, wk, wv]
    else:
        me, code, *pieces = shards
        in_specs += [smem(), once(code.shape)] + [once(x.shape) for x in pieces]
        args += [me, code] + pieces
        out_specs += [once((width, width))] * 3 + [once(mod_shape.shape)]
        out_shape += [square] * 3 + [mod_shape]
        devices = sum(x.shape[0] for x in pieces)
        scratch = [pltpu.VMEM((samples, devices, 128), F32)]
    tables = [(table, width), (count, width), (table, width), (table, width)]
    tables += [(heads, table, count), (count, width)]
    first = 0 if shards is None else len(shards) - 2
    return pl.pallas_call(
        lambda *refs: attend_kernel(*refs, pieces=first),
        grid=(samples,),
        in_specs=in_specs,
        out_specs=out_specs + [anywhere()] * len(tables),
        out_shape=out_shape + [jax.ShapeDtypeStruct((samples,) + t, BF16) for t in tables],
        scratch_shapes=scratch
        + [pltpu.VMEM((2,) + t, BF16) for t in tables]
        + [pltpu.SemaphoreType.DMA((2, 6 + heads))],
        compiler_params=params(60),
    )(*args)


def feed_kernel(*refs, shards):
    me_ref, nodes_ref, att_ref, cot_ref, mod_ref = refs[:5]
    scratch = 6 + (10 + shards if shards else 0)
    up_acc, down_acc, wo_acc, bu_acc, bd_acc, down_rows = refs[len(refs) - 6 :]
    if shards:
        pieces = refs[5 : 5 + shards]
        *piece_bufs, low_buf, high_buf, in_sems, out_sems = refs[-scratch:-12]
        wo_ref, wu_ref, wd_ref, bu_ref, bd_ref, raw = refs[-12:-6]
        outs = refs[5 + shards : -scratch]

        @pl.when(pl.program_id(0) == 0)
        def _():
            arriving = [
                pltpu.make_async_copy(piece, buf, in_sems.at[i])
                for i, (piece, buf) in enumerate(zip(pieces, piece_bufs))
            ]
            for copy in arriving:
                copy.start()
            place_second(
                me_ref, piece_bufs, arriving, wo_ref, wu_ref, wd_ref, bu_ref, bd_ref, raw
            )

    else:
        wo_ref, wu_ref, wd_ref, bu_ref, bd_ref = refs[5:10]
        outs = refs[10:-scratch]
    out_ref, gmid_ref, gatt_ref, gmod_ref = outs[:4]
    sums = outs[4:]
    s = pl.program_id(0)
    count, width = nodes_ref.shape[1:]
    hidden_size = wu_ref.shape[1]
    wide = hidden_size // width

    def add_to(ref, cols, value):
        ref[:, cols] = jnp.where(s == 0, 0.0, ref[:, cols]) + value

    scale, shift = mod_ref[0, 2:3, :], mod_ref[0, 3:4, :]
    blocks = [slice(c * width, (c + 1) * width) for c in range(wide)]
    attended = att_ref[0]
    cot = cot_ref[0]
    middle = nodes_ref[0].astype(F32) + product(attended, wo_ref[...])
    cot_t = cot.T
    grad_ahead = product_t(cot, wd_ref[blocks[0], :])
    add_to(bd_acc, slice(0, width), jnp.sum(cot.astype(F32), axis=0, keepdims=True))
    hat, inverse = layer_normalize(middle)
    act = (hat * scale + shift).astype(BF16)
    act_t = act.T
    result = middle + bd_ref[...]
    grad_act = jnp.zeros((count, width), F32)

    pre_ahead = product(act, wu_ref[:, blocks[0]])
    ready = None
    for c, cols in enumerate(blocks):
        pre, grad_hidden = pre_ahead, grad_ahead
        if c + 1 < wide:
            pre_ahead = product(act, wu_ref[:, blocks[c + 1]])
            grad_ahead = product_t(cot, wd_ref[blocks[c + 1], :])
        if ready:
            old, hidden, low_pre = ready
            result = result + product(hidden, wd_ref[old, :])
            grad_act = grad_act + product_t(low_pre, wu_ref[:, old])
            add_to(down_acc, old, product(cot_t, hidden))
            add_to(up_acc, old, product(act_t, low_pre))
        pre = pre + bu_ref[:, cols]
        gate = 0.5 * jnp.tanh(0.5 * pre) + 0.5
        value = pre * gate
        low_pre = (grad_hidden * (gate + value * (1.0 - gate))).astype(BF16)
        add_to(bu_acc, cols, jnp.sum(low_pre.astype(F32), axis=0, keepdims=True))
        ready = (cols, value.astype(BF16), low_pre)
    old, hidden, low_pre = ready
    grad_act = grad_act + product_t(low_pre, wu_ref[:, old])
    result = result + product(hidden, wd_ref[old, :])
    add_to(down_acc, old, product(cot_t, hidden))
    add_to(up_acc, old, product(act_t, low_pre))
    grad_middle = cot.astype(F32) + norm_back(grad_act * scale, hat, inverse)
    gmid_ref[0] = grad_middle
    branch = grad_middle.astype(BF16)
    out_ref[0] = result.astype(BF16)
    gmod_ref[0, 0:1, :] = jnp.sum(grad_act * hat, axis=0, keepdims=True)
    gmod_ref[0, 1:2, :] = jnp.sum(grad_act, axis=0, keepdims=True)
    gatt_ref[0] = product_t(branch, wo_ref[...]).astype(BF16)
    add_to(wo_acc, slice(0, width), product(attended.T, branch))

    @pl.when(s == pl.num_programs(0) - 1)
    def _():
        for c in range(wide):
            cols = slice(c * width, (c + 1) * width)
            down_rows[cols, :] = down_acc[:, cols].T
        if len(sums) > 2:
            for ref, value in zip(sums, (up_acc, down_rows, wo_acc, bu_acc, bd_acc)):
                ref[...] = value[...]
            return
        half = low_buf.shape[0]
        devices = 2 * half
        down = hidden_size // devices
        leaving = []

        for part, ref in ((1, high_buf), (0, low_buf)):

            def pack(i, _, part=part, ref=ref):
                shard = me_ref[0] ^ relative(i + part * half, devices)
                rows = pl.ds(pl.multiple_of(shard * BLOCK, BLOCK), BLOCK)
                at = 0
                for c in range(0, hidden_size, 128):
                    ref[i, at : at + BLOCK, :] = up_acc[rows, c : c + 128].astype(BF16)
                    at += BLOCK
                for r in range(0, down, BLOCK):
                    some = pl.ds(pl.multiple_of(shard * down + r, BLOCK), BLOCK)
                    for c in range(0, width, 128):
                        ref[i, at : at + BLOCK, :] = down_rows[some, c : c + 128].astype(BF16)
                        at += BLOCK
                for c in range(0, width, 128):
                    ref[i, at : at + BLOCK, :] = wo_acc[rows, c : c + 128].astype(BF16)
                    at += BLOCK
                up_tile = pl.multiple_of(((shard * down) // 128) * 128, 128)
                down_tile = pl.multiple_of(((shard * (width // devices)) // 128) * 128, 128)
                row = lax.broadcasted_iota(jnp.int32, (BLOCK, 128), 0)
                ref[i, at : at + BLOCK, :] = jnp.where(
                    row == 0, bu_acc[:, pl.ds(up_tile, 128)], bd_acc[:, pl.ds(down_tile, 128)]
                ).astype(BF16)
                return 0

            quarter = half // 4
            for q in range(4):
                some = slice(q * quarter, (q + 1) * quarter)
                lax.fori_loop(some.start, some.stop, pack, 0, unroll=2)
                leaving.append(
                    pltpu.make_async_copy(
                        ref.at[some], sums[part].at[some], out_sems.at[part, q]
                    )
                )
                leaving[-1].start()
        for copy in leaving:
            copy.wait()


def feed(me, nodes, attended, cot, mod, hidden, devices, weights=None, shards=None):
    samples, count, width = nodes.shape
    tile = per_sample((count, width))
    scratch = [
        pltpu.VMEM((width, hidden), F32),
        pltpu.VMEM((width, hidden), F32),
        pltpu.VMEM((width, width), F32),
        pltpu.VMEM((1, hidden), F32),
        pltpu.VMEM((1, width), F32),
        pltpu.VMEM((hidden, width), F32),
    ]
    if shards:
        rows = shards[0].shape[1]
        sums = [jax.ShapeDtypeStruct((devices // 2, rows, 128), BF16)] * 2
        extra = list(shards)
        scratch = [pltpu.VMEM(x.shape, BF16) for x in extra + sums] + [
            pltpu.SemaphoreType.DMA((len(extra),)),
            pltpu.SemaphoreType.DMA((2, 4)),
            pltpu.VMEM((width, width), BF16),
            pltpu.VMEM((width, hidden), BF16),
            pltpu.VMEM((hidden, width), BF16),
            pltpu.VMEM((1, hidden), F32),
            pltpu.VMEM((1, width), F32),
            pltpu.VMEM((2, devices, 128), F32),
        ] + scratch
    else:
        shapes = ((width, hidden), (hidden, width), (width, width), (1, hidden), (1, width))
        sums = [jax.ShapeDtypeStruct(shape, F32) for shape in shapes]
        extra = list(weights)
    return pl.pallas_call(
        lambda *refs: feed_kernel(*refs, shards=len(shards or ())),
        grid=(samples,),
        in_specs=[smem(), tile, tile, tile, per_sample((4, width))]
        + [anywhere() if shards else once(x.shape) for x in extra],
        out_specs=[tile, tile, tile, per_sample((2, width))]
        + [anywhere() if shards else once(x.shape) for x in sums],
        out_shape=[
            jax.ShapeDtypeStruct((samples, count, width), BF16),
            jax.ShapeDtypeStruct((samples, count, width), F32),
            jax.ShapeDtypeStruct((samples, count, width), BF16),
            jax.ShapeDtypeStruct((samples, 2, width), F32),
        ]
        + sums,
        scratch_shapes=scratch,
        compiler_params=params(60),
    )(me, nodes, attended, cot, mod, *extra)


def attend_back_kernel(*refs, started, last, begin):
    me_ref, nodes_ref, h0, h1, h2, h3, code_ref, gmod_ref = refs[:8]
    act_ref, q_ref, k_ref, v_ref, p_ref, gatt_ref, wq_ref, wk_ref, wv_ref = refs[8:17]
    gmid_ref, mod_ref = refs[17:19]
    rest = refs[19:]
    if started:
        before, rest = rest[:5], rest[10:]
    base_ref, b0, b1, b2, b3 = rest[:5]
    gq, gk, gv, p_buf, p_sems, sum_sems = rest[-6:]
    if last:
        outs = rest[5:-11]
        sums = q_acc, k_acc, v_acc, cond_acc, bias_acc = rest[-11:-6]
    else:
        sums = q_acc, k_acc, v_acc, cond_acc, bias_acc = rest[5:10]
    s, steps = pl.program_id(0), pl.num_programs(0)
    slot = lax.rem(s, 2)

    def fetch(step, h):
        place = lax.rem(step, 2)
        return pltpu.make_async_copy(
            p_ref.at[begin + step, h], p_buf.at[place, h], p_sems.at[place, h]
        )

    def carry():
        return [
            pltpu.make_async_copy(old, new, sum_sems.at[i])
            for i, (old, new) in enumerate(zip(before, sums))
        ]

    @pl.when(s == 0)
    def _():
        for h in range(p_buf.shape[1]):
            fetch(s, h).start()
        if started:
            for copy in carry():
                copy.start()

    @pl.when(s + 1 < steps)
    def _():
        for h in range(p_buf.shape[1]):
            fetch(s + 1, h).start()

    def add_to(ref, cols, value):
        old = ref[:, cols]
        ref[:, cols] = (old if started else jnp.where(s == 0, 0.0, old)) + value

    count, width = nodes_ref.shape[1:]
    each = h0.shape[1]
    inv_root = HEAD ** (-0.5)

    heads = [slice(h * HEAD, (h + 1) * HEAD) for h in range(width // HEAD)]

    def grad_of_probs(cols):
        return product_t(v_ref[0, :, cols], gatt_ref[0, :, cols])

    def spread_back(cols, grad_scores):
        gk[:, cols] = (product(grad_scores, q_ref[0, :, cols]) * inv_root).astype(BF16)
        gq[:, cols] = (product(k_ref[0, :, cols].T, grad_scores) * inv_root).T.astype(BF16)

    act_t = act_ref[0].T

    def weigh(h):
        cols = slice(h * HEAD, (h + 2) * HEAD)
        add_to(q_acc, cols, product(act_t[:, 0:count], gq[:, cols]))
        add_to(k_acc, cols, product(act_t, gk[:, cols]))
        add_to(v_acc, cols, product(act_t, gv[:, cols]))

    following = grad_of_probs(heads[0])
    hat, inverse = layer_normalize(nodes_ref[0].astype(F32))
    ready = None
    for h, cols in enumerate(heads):
        grad_probs = following
        if h + 1 < len(heads):
            following = grad_of_probs(heads[h + 1])
        if h % 2 == 0:
            for i in range(h, min(h + 2, len(heads))):
                fetch(s, i).wait()
        if h == 2 and started:

            @pl.when(s == 0)
            def _():
                for copy in carry():
                    copy.wait()

        gv[:, cols] = product(p_buf[slot, h], gatt_ref[0, :, cols]).astype(BF16)
        if ready:
            spread_back(*ready)
        if h == 2:
            weigh(0)
        probs = p_buf[slot, h].astype(F32)
        inner = jnp.sum(probs * grad_probs, axis=0, keepdims=True)
        ready = (cols, (probs * (grad_probs - inner)).astype(BF16))
    spread_back(*ready)

    grad_act = (
        product_t(gq[...], wq_ref[...])
        + product_t(gk[0:count, :], wk_ref[...])
        + product_t(gv[0:count, :], wv_ref[...])
    )
    grad_far = product_t(gk[count:, :], wk_ref[...]) + product_t(gv[count:, :], wv_ref[...])
    for h in range(2, len(heads), 2):
        weigh(h)
    base_ref[0] = gmid_ref[0] + norm_back(grad_act * mod_ref[0, 0:1, :], hat, inverse)
    scale_sum = jnp.sum(grad_act * hat, axis=0, keepdims=True)
    shift_sum = jnp.sum(grad_act, axis=0, keepdims=True)
    for d, (far, back) in enumerate(zip((h0, h1, h2, h3), (b0, b1, b2, b3))):
        part = grad_far[d * each : (d + 1) * each]
        far_hat, _ = layer_normalize(far[0].astype(F32))
        scale_sum = scale_sum + jnp.sum(part * far_hat, axis=0, keepdims=True)
        shift_sum = shift_sum + jnp.sum(part, axis=0, keepdims=True)
        back[0] = part.astype(BF16)
    kinds = (scale_sum, shift_sum, gmod_ref[0, 0:1, :], gmod_ref[0, 1:2, :])
    columns = code_ref[...].T
    mine = lax.broadcasted_iota(jnp.int32, columns.shape, 1) == s + begin
    code = jnp.sum(jnp.where(mine, columns, 0.0), axis=1, keepdims=True)
    for kind, value in enumerate(kinds):
        cols = slice(kind * width, (kind + 1) * width)
        add_to(cond_acc, cols, code * value)
        add_to(bias_acc, cols, value)
    if not last:
        return

    @pl.when(s == pl.num_programs(0) - 1)
    def _():
        if len(outs) > 2:
            for ref, value in zip(outs, sums):
                ref[...] = value[...]
            return
        half = outs[0].shape[0]
        devices = 2 * half
        for part, ref in enumerate(outs):

            def pack(i, _, part=part, ref=ref):
                shard = me_ref[0] ^ relative(i + part * half, devices)
                rows = pl.ds(pl.multiple_of(shard * BLOCK, BLOCK), BLOCK)
                at = 0
                for value in (q_acc, k_acc, v_acc):
                    for c in range(0, width, 128):
                        ref[i, at : at + BLOCK, :] = value[rows, c : c + 128].astype(BF16)
                        at += BLOCK
                tile = pl.multiple_of(((shard * (4 * width // devices)) // 128) * 128, 128)
                ref[i, at : at + BLOCK, :] = cond_acc[:, pl.ds(tile, 128)].astype(BF16)
                at += BLOCK
                ref[i, at : at + BLOCK, :] = jnp.broadcast_to(
                    bias_acc[:, pl.ds(tile, 128)], (BLOCK, 128)
                ).astype(BF16)
                return 0

            lax.fori_loop(0, half, pack, 0, unroll=2)


def attend_back(
    me,
    nodes,
    halos,
    noise_code,
    gmod,
    saved,
    gatt,
    wq,
    wk,
    wv,
    gmid,
    mod,
    devices,
    begin,
    steps,
    carried=(),
):
    samples, count, width = nodes.shape
    act, queries, keys, values, probs = saved
    table = act.shape[1]
    heads = width // HEAD
    each = halos[0].shape[1]
    half = devices // 2
    codes = noise_code.shape[1]
    last = begin + steps == samples
    shapes = [(width, width)] * 3 + [(codes, 4 * width), (1, 4 * width)]
    sums = [jax.ShapeDtypeStruct(shape, F32) for shape in shapes]
    scratch = [
        pltpu.VMEM((count, width), BF16),
        pltpu.VMEM((table, width), BF16),
        pltpu.VMEM((table, width), BF16),
        pltpu.VMEM((2, heads, table, count), BF16),
        pltpu.SemaphoreType.DMA((2, heads)),
        pltpu.SemaphoreType.DMA((5,)),
    ]
    if last:
        scratch = [pltpu.VMEM(shape, F32) for shape in shapes] + scratch
        if packs(width, devices):
            rows = 3 * BLOCK * width // 128 + 2 * BLOCK
            sums = [jax.ShapeDtypeStruct((half, rows, 128), BF16)] * 2

    def tile(*shape):
        return per_sample(shape, begin)

    args = [me, nodes, *halos, noise_code, gmod, act, queries, keys, values, probs, gatt, wq, wk, wv]
    args += [gmid, mod]
    aliases = {len(args) + 5 + i: i for i in range(5)} if carried else {}
    return pl.pallas_call(
        lambda *refs: attend_back_kernel(*refs, started=bool(carried), last=last, begin=begin),
        grid=(steps,),
        in_specs=[smem(), tile(count, width)]
        + [tile(each, width)] * 4
        + [once(noise_code.shape), tile(2, width)]
        + [tile(table, width), tile(count, width), tile(table, width), tile(table, width)]
        + [anywhere(), tile(count, width)]
        + [once((width, width))] * 3
        + [tile(count, width), tile(4, width)]
        + ([anywhere()] * 5 + [anywhere()] * 5 if carried else []),
        out_specs=[tile(count, width)]
        + [tile(each, width)] * 4
        + [once(x.shape) for x in sums],
        out_shape=[jax.ShapeDtypeStruct((samples, count, width), F32)]
        + [jax.ShapeDtypeStruct((samples, each, width), BF16)] * 4
        + sums,
        scratch_shapes=scratch,
        input_output_aliases=aliases,
        compiler_params=params(46),
    )(*args, *carried)


def finish_kernel(nodes_ref, base_ref, b0, b1, b2, b3, send_ref, mod_ref, out_ref, far):
    count = nodes_ref.shape[1]
    each = b0.shape[1]
    row = lax.broadcasted_iota(jnp.int32, (count, 4 * each), 0)
    chosen = jnp.where(row == send_ref[...], 1.0, 0.0).astype(BF16)
    for d, ref in enumerate((b0, b1, b2, b3)):
        far[d * each : (d + 1) * each, :] = ref[0]
    grad_act = product(chosen, far[...])
    hat, inverse = layer_normalize(nodes_ref[0].astype(F32))
    out_ref[0] = base_ref[0] + norm_back(grad_act * mod_ref[0, 0:1, :], hat, inverse)


def finish(nodes, base, backs, send_rows, mod):
    samples, count, width = nodes.shape
    each = backs[0].shape[1]
    picks = send_rows.size
    tile = per_sample((count, width))
    return pl.pallas_call(
        finish_kernel,
        grid=(samples,),
        in_specs=[tile, tile]
        + [per_sample((each, width))] * 4
        + [whole((1, picks)), per_sample((4, width))],
        out_specs=tile,
        out_shape=jax.ShapeDtypeStruct((samples, count, width), F32),
        scratch_shapes=[pltpu.VMEM((picks, width), BF16)],
        compiler_params=params(16),
    )(nodes, base, *backs, send_rows.reshape(1, picks), mod)


def layer(
    nodes,
    neighbours,
    send_rows,
    noise_code,
    w_query,
    w_key,
    w_value,
    w_out,
    w_up,
    b_up,
    w_down,
    b_down,
    cond_weight,
    cond_bias,
    cotangent,
):
    devices = lax.axis_size("patch") * lax.axis_size("sample")
    position = lax.axis_index("patch") * lax.axis_size("sample") + lax.axis_index("sample")
    me = position.astype(jnp.int32).reshape(1)
    width = nodes.shape[2]
    hidden = w_up.shape[1]
    offsets = (1, -1, STRIDE, -STRIDE)

    samples, count, _ = nodes.shape
    table = count + send_rows.size
    if not packs(width, devices):
        return plain_body(
            me,
            nodes,
            neighbours,
            send_rows,
            noise_code,
            (w_query, w_key, w_value, cond_weight, cond_bias, noise_code),
            (w_out, w_up, b_up, w_down, b_down),
            cotangent,
            devices,
        )
    z_side, plane, (core,) = stage_groups(devices)

    def swaps(pieces, group):
        return [swap(x, c, devices) for x, c in zip(pieces, group)]

    def cores(pieces):
        return [swap(x, core, devices) for x in pieces]

    def shifts(blocks, sign):
        return [from_behind(x, sign * o) for x, o in zip(blocks, offsets)]

    *sends, first, second = begin(
        nodes,
        send_rows,
        (w_query, w_key, w_value, cond_weight, cond_bias, w_out, w_up, b_up, w_down, b_down),
    )
    far = swaps([first] * 3, z_side)
    far_second = swaps([second] * 3, z_side)
    bias = slot_bias(neighbours, table)
    halos = shifts([after(x, bias) for x in sends], 1)
    held = join([first] + far)
    low_first = [held] + swaps([held] * 3, plane)
    high_first = cores(low_first)
    held_second = join([second] + far_second)
    low_second = [held_second] + swaps([held_second] * 3, plane)
    wq, wk, wv, mod, *saved, attended = attend(
        nodes, halos, bias, shards=[me, noise_code] + low_first + high_first
    )
    high_second = cores(low_second)
    result, gmid, gatt, gmod, low_feed, high_feed = feed(
        me,
        nodes,
        attended,
        cotangent,
        mod,
        hidden,
        devices,
        shards=low_second + high_second,
    )
    back = (me, nodes, halos, noise_code, gmod, saved, gatt, wq, wk, wv, gmid, mod, devices)
    (got_feed,) = cores([high_feed])
    *arrays, s0, s1, s2, s3, s4 = attend_back(*back, 0, 1)
    own_feed, *parts = add_halves(low_feed, got_feed, 4)
    feed_far = swaps(parts, plane)
    carried = (after(s0, own_feed), s1, s2, s3, s4, *arrays)
    base, *rest = attend_back(*back, 1, samples - 1, carried)
    low_proj, high_proj = rest[4:]
    (got_proj,) = cores([high_proj])
    own_feed, *parts = add_pieces([own_feed] + feed_far)
    feed_last = swaps(parts, z_side)
    own_proj, *parts = add_halves(low_proj, got_proj, 4)
    proj_far = swaps(parts, plane)
    backs = shifts(rest[:4], -1)
    own_proj, *parts = add_pieces([own_proj] + proj_far)
    proj_last = swaps(parts, z_side)
    grad_nodes = finish(nodes, base, backs, send_rows, mod)
    down, thin = hidden // devices, width // devices
    grad_up, grad_down, grad_out, grad_b_up, grad_b_down = last_sum(
        me,
        [own_feed] + feed_last,
        ((BLOCK, hidden), (down, width), (BLOCK, width), (1, down), (1, thin)),
        False,
    )
    step = 4 * width // devices
    grad_query, grad_key, grad_value, grad_cond, grad_cond_bias = last_sum(
        me,
        [own_proj] + proj_last,
        ((BLOCK, width),) * 3 + ((BLOCK, step), (1, step)),
        True,
    )
    grad_b_up, grad_b_down, grad_cond_bias = grad_b_up[0], grad_b_down[0], grad_cond_bias[0]
    return (
        result,
        grad_nodes,
        grad_query,
        grad_key,
        grad_value,
        grad_out,
        grad_up,
        grad_b_up,
        grad_down,
        grad_b_down,
        grad_cond,
        grad_cond_bias,
    )


def plain_body(
    me, nodes, neighbours, send_rows, noise_code, first, second, cotangent, devices
):
    samples, count, _ = nodes.shape
    hidden = second[1].shape[1]
    offsets = (1, -1, STRIDE, -STRIDE)
    bias = slot_bias(neighbours, count + send_rows.size)
    sends = begin(nodes, send_rows)
    halos = [from_behind(block, offset) for block, offset in zip(sends, offsets)]
    (wq, wk, wv, mod), weights = gather_plain(*first, *second)
    *saved, attended = attend(nodes, halos, bias, weights=(wq, wk, wv, mod))
    result, gmid, gatt, gmod, *sums = feed(
        me, nodes, attended, cotangent, mod, hidden, devices, weights=weights
    )
    sums[3:] = [x[0] for x in sums[3:]]
    grad_up, grad_down, grad_out, grad_b_up, grad_b_down = scatter_plain(sums, (0,) * 5)
    base, *rest = attend_back(
        me, nodes, halos, noise_code, gmod, saved, gatt, wq, wk, wv, gmid, mod, devices, 0, samples
    )
    backs = [from_behind(block, -offset) for block, offset in zip(rest[:4], offsets)]
    rest[-1] = rest[-1][0]
    grad_query, grad_key, grad_value, grad_cond, grad_cond_bias = scatter_plain(
        rest[4:], (0, 0, 0, 1, 0)
    )
    grad_nodes = finish(nodes, base, backs, send_rows, mod)
    return (
        result,
        grad_nodes,
        grad_query,
        grad_key,
        grad_value,
        grad_out,
        grad_up,
        grad_b_up,
        grad_down,
        grad_b_down,
        grad_cond,
        grad_cond_bias,
    )


def solution(mesh):
    both = P(("patch", "sample"), None)
    flat = P(("patch", "sample"))
    split = P("sample", "patch", None)
    cond = P(None, ("patch", "sample"))
    return jax.shard_map(
        layer,
        mesh=mesh,
        in_specs=(
            split,
            P("patch", None),
            P("patch", None),
            P("sample", None),
            both,
            both,
            both,
            both,
            both,
            flat,
            both,
            flat,
            cond,
            flat,
            split,
        ),
        out_specs=(split, split, both, both, both, both, both, flat, both, flat, cond, flat),
        check_vma=False,
    )
```

profile of v0, /device:TPU:0, one launch (start us, length us, event | category | flops | bytes accessed | tf_op | source)
XLA Modules:
  0.0 274.4 jit_solution(7675150982222725459)
XLA Ops:
  0.6 4.2 %shard_map.238 = (bf16[4,64,512]{2,1,0:T(8,128)(2,1)}, bf16[4,64,512]{2,1,0:T(8,128)(2,1)}, bf16[4,64,512]{2,1,0:T(8,128)(2,1)}, bf16[4,64,512]{2,1,0:T(8,128)(2...) custom-call(bf16[4,512,512]{2,1,0:T(8,128)(2,1)} %nodes_ref.1, s32[4,64]{1,0:T(4,128)} %refs_1_.4, ...), custom_call_target="tpu_custom_call" | custom-call | tf_op jit(solution)/shard_map/pallas_call | solution.py:204
  4.8 3.1 %collective-permute-start.4 = (bf16[1,208,128]{2,1,0:T(8,128)(2,1)}, bf16[1,208,128]{2,1,0:T(8,128)(2,1)S(1)}, u32[]{:S(2)}, u32[]{:S(2)}) collective-permute-start(bf16[1,208,128]{2,1,0:T(8,128)(2,1)} %get-tuple-element.90.refs_0_), channel_id=1, source_target_pairs={{0,8},{1,9},{2,10},{3,11},{4,12},{5,13},{6,14},{7,15},{8,0},{9,1},... | collective-permute-start | bytes 159752 | tf_op jit(solution)/shard_map/ppermute | solution.py:35
  8.8 3.7 %shard_map.239.refs_5_ = f32[768,512]{1,0:T(8,128)S(1)} custom-call(s32[16,512]{1,0:T(8,128)S(1)} %bitcast.8), custom_call_target="tpu_custom_call" | custom-call | tf_op jit(solution)/shard_map/pallas_call | solution.py:142
  13.7 4.4 %collective-permute-start.1 = (bf16[4,64,512]{2,1,0:T(8,128)(2,1)}, bf16[4,64,512]{2,1,0:T(8,128)(2,1)S(1)}, u32[]{:S(2)}, u32[]{:S(2)}) collective-permute-start(bf16[4,64,512]{2,1,0:T(8,128)(2,1)} %get-tuple-element.85), channel_id=1, source_target_pairs={{2,0},{4,2},{6,4},{8,6},{10,8},{12,10},{14,12},{16,14},{18,16},{20... | collective-permute-start | bytes 786440 | tf_op jit(solution)/shard_map/ppermute | solution.py:31
  19.3 1.8 collective-permute-start.15
  21.0 8.8 %collective-permute-done.5.refs_2_ = bf16[1,208,128]{2,1,0:T(8,128)(2,1)S(1)} collective-permute-done((bf16[1,208,128]{2,1,0:T(8,128)(2,1)}, bf16[1,208,128]{2,1,0:T(8,128)(2,1)S(1)}, u32[]{:S(2)}, u32[]{:S(2)}) %collective-permute-start.5) | collective-permute-done | bytes 53280 | tf_op jit(solution)/shard_map/ppermute | solution.py:35
  32.2 2.9 %collective-permute-start.3 = (bf16[4,64,512]{2,1,0:T(8,128)(2,1)}, bf16[4,64,512]{2,1,0:T(8,128)(2,1)S(1)}, u32[]{:S(2)}, u32[]{:S(2)}) collective-permute-start(bf16[4,64,512]{2,1,0:T(8,128)(2,1)} %get-tuple-element.89), channel_id=1, source_target_pairs={{8,0},{10,2},{12,4},{14,6},{16,8},{18,10},{20,12},{22,14},{24,16},... | collective-permute-start | bytes 786440 | tf_op jit(solution)/shard_map/ppermute | solution.py:31
  35.1 3.5 %collective-permute-done.16.refs_3_ = bf16[1,592,128]{2,1,0:T(8,128)(2,1)S(1)} collective-permute-done((bf16[1,592,128]{2,1,0:T(8,128)(2,1)}, bf16[1,592,128]{2,1,0:T(8,128)(2,1)S(1)}, u32[]{:S(2)}, u32[]{:S(2)}) %collective-permute-start.16) | collective-permute-done | bytes 151584 | tf_op jit(solution)/shard_map/ppermute | solution.py:35
  41.1 8.5 %collective-permute-done.6.refs_3_ = bf16[1,208,128]{2,1,0:T(8,128)(2,1)S(1)} collective-permute-done((bf16[1,208,128]{2,1,0:T(8,128)(2,1)}, bf16[1,208,128]{2,1,0:T(8,128)(2,1)S(1)}, u32[]{:S(2)}, u32[]{:S(2)}) %collective-permute-start.6) | collective-permute-done | bytes 53280 | tf_op jit(solution)/shard_map/ppermute | solution.py:35
  51.1 1.9 collective-permute-start.19
  53.1 1.6 collective-permute-start.7
  54.8 27.6 %collective-permute-done.7.refs_9_ = bf16[4,208,128]{2,1,0:T(8,128)(2,1)S(1)} collective-permute-done((bf16[4,208,128]{2,1,0:T(8,128)(2,1)S(1)}, bf16[4,208,128]{2,1,0:T(8,128)(2,1)S(1)}, u32[]{:S(2)}, u32[]{:S(2)}) %collective-permute-start.7) | collective-permute-done | bytes 213024 | tf_op jit(solution)/shard_map/ppermute | solution.py:35
  82.4 2.0 collective-permute-done.8.refs_10_
  84.5 4.8 %collective-permute-done.9.refs_11_ = bf16[4,208,128]{2,1,0:T(8,128)(2,1)} collective-permute-done((bf16[4,208,128]{2,1,0:T(8,128)(2,1)S(1)}, bf16[4,208,128]{2,1,0:T(8,128)(2,1)}, u32[]{:S(2)}, u32[]{:S(2)}) %collective-permute-start.9) | collective-permute-done | bytes 213024 | tf_op jit(solution)/shard_map/ppermute | solution.py:35
  90.9 3.6 %collective-permute-done.12.refs_14_ = bf16[4,208,128]{2,1,0:T(8,128)(2,1)S(1)} collective-permute-done((bf16[4,208,128]{2,1,0:T(8,128)(2,1)S(1)}, bf16[4,208,128]{2,1,0:T(8,128)(2,1)S(1)}, u32[]{:S(2)}, u32[]{:S(2)}) %collective-permute-start.12) | collective-permute-done | bytes 213024 | tf_op jit(solution)/shard_map/ppermute | solution.py:35
  96.4 23.2 %shard_map.241 = (bf16[512,512]{1,0:T(8,128)(2,1)}, bf16[512,512]{1,0:T(8,128)(2,1)}, bf16[512,512]{1,0:T(8,128)(2,1)}, f32[4,4,512]{2,1,0:T(4,128)}, bf16[4,768...) custom-call(bf16[4,512,512]{2,1,0:T(8,128)(2,1)} %nodes_ref.1, ...), custom_call_target="tpu_custom_call" | custom-call | tf_op jit(solution)/shard_map/pallas_call | solution.py:517
  119.8 43.9 %shard_map.243 = (bf16[4,512,512]{2,1,0:T(8,128)(2,1)}, f32[4,512,512]{2,1,0:T(8,128)}, bf16[4,512,512]{2,1,0:T(8,128)(2,1)}, f32[4,2,512]{2,1,0:T(2,128)}, bf16...) custom-call(s32[1]{0:T(128)} %bitcast.refs_6_.refs_0_, bf16[4,512,512]{2,1,0:T(8,128)(2,1)} %nodes_ref.1, ...), custom_call_target="tpu_custom_call" | custom-call | tf_op jit(solution)/shard_map/pallas_call | solution.py:694
  164.8 10.3 %shard_map.244 = (f32[4,512,512]{2,1,0:T(8,128)}, bf16[4,64,512]{2,1,0:T(8,128)(2,1)S(1)}, bf16[4,64,512]{2,1,0:T(8,128)(2,1)S(1)}, bf16[4,64,512]{2,1,0:T(8,128...) custom-call(s32[1]{0:T(128)} %bitcast.refs_6_.refs_0_, ...), custom_call_target="tpu_custom_call" | custom-call | tf_op jit(solution)/shard_map/pallas_call | solution.py:912
  176.1 25.7 %shard_map.246 = (f32[4,512,512]{2,1,0:T(8,128)}, bf16[4,64,512]{2,1,0:T(8,128)(2,1)S(1)}, bf16[4,64,512]{2,1,0:T(8,128)(2,1)S(1)}, bf16[4,64,512]{2,1,0:T(8,128...) custom-call(s32[1]{0:T(128)} %bitcast.refs_6_.refs_0_, ...), custom_call_target="tpu_custom_call", output_to_operand_aliasing={{0}: (24, {}), {1}: (25, {}), {2}: (26, {}), {3}: (27, {}),... | custom-call | tf_op jit(solution)/shard_map/pallas_call | solution.py:912
  203.7 2.0 collective-permute-start.38
  206.4 3.3 %collective-permute-done.25.b0 = bf16[4,64,512]{2,1,0:T(8,128)(2,1)S(1)} collective-permute-done((bf16[4,64,512]{2,1,0:T(8,128)(2,1)S(1)}, bf16[4,64,512]{2,1,0:T(8,128)(2,1)S(1)}, u32[]{:S(2)}, u32[]{:S(2)}) %collective-permute-start.25) | collective-permute-done | bytes 262176 | tf_op jit(solution)/shard_map/ppermute | solution.py:31
  211.1 3.2 %collective-permute-done.26.b1 = bf16[4,64,512]{2,1,0:T(8,128)(2,1)S(1)} collective-permute-done((bf16[4,64,512]{2,1,0:T(8,128)(2,1)S(1)}, bf16[4,64,512]{2,1,0:T(8,128)(2,1)S(1)}, u32[]{:S(2)}, u32[]{:S(2)}) %collective-permute-start.26) | collective-permute-done | bytes 262176 | tf_op jit(solution)/shard_map/ppermute | solution.py:31
  214.4 23.8 %collective-permute-start.31 = (bf16[4,224,128]{2,1,0:T(8,128)(2,1)S(1)}, bf16[4,224,128]{2,1,0:T(8,128)(2,1)S(1)}, u32[]{:S(2)}, u32[]{:S(2)}) collective-permute-start(bf16[4,224,128]{2,1,0:T(8,128)(2,1)S(1)} %get-tuple-element.129), channel_id=1, source_target_pairs={{0,4},{1,5},{2,6},{3,7},{4,0},{5,1},{6,2},{7,3},{8,12},{9,13},{10,... | collective-permute-start | bytes 688136 | tf_op jit(solution)/shard_map/ppermute | solution.py:35
  242.2 2.5 collective-permute-start.39
  244.7 4.2 %collective-permute-start.40 = (bf16[1,592,128]{2,1,0:T(8,128)(2,1)S(1)}, bf16[1,592,128]{2,1,0:T(8,128)(2,1)}, u32[]{:S(2)}, u32[]{:S(2)}) collective-permute-start(bf16[1,592,128]{2,1,0:T(8,128)(2,1)S(1)} %get-tuple-element.143), channel_id=1, source_target_pairs={{0,16},{1,17},{2,18},{3,19},{4,20},{5,21},{6,22},{7,23},{8,24},{9,... | collective-permute-start | bytes 454664 | tf_op jit(solution)/shard_map/ppermute | solution.py:35
  251.8 4.0 %collective-permute-start.33 = (bf16[1,224,128]{2,1,0:T(8,128)(2,1)}, bf16[1,224,128]{2,1,0:T(8,128)(2,1)}, u32[]{:S(2)}, u32[]{:S(2)}) collective-permute-start(bf16[1,224,128]{2,1,0:T(8,128)(2,1)} %get-tuple-element.132), channel_id=1, source_target_pairs={{0,8},{1,9},{2,10},{3,11},{4,12},{5,13},{6,14},{7,15},{8,0},{9,1},... | collective-permute-start | bytes 172040 | tf_op jit(solution)/shard_map/ppermute | solution.py:35
  255.8 1.7 collective-permute-done.28.b3
  257.5 3.0 %collective-permute-done.39.refs_2_ = bf16[1,592,128]{2,1,0:T(8,128)(2,1)S(1)} collective-permute-done((bf16[1,592,128]{2,1,0:T(8,128)(2,1)S(1)}, bf16[1,592,128]{2,1,0:T(8,128)(2,1)S(1)}, u32[]{:S(2)}, u32[]{:S(2)}) %collective-permute-start.39) | collective-permute-done | bytes 151584 | tf_op jit(solution)/shard_map/ppermute | solution.py:35
  261.2 3.1 %collective-permute-start.35 = (bf16[1,224,128]{2,1,0:T(8,128)(2,1)S(1)}, bf16[1,224,128]{2,1,0:T(8,128)(2,1)}, u32[]{:S(2)}, u32[]{:S(2)}) collective-permute-start(bf16[1,224,128]{2,1,0:T(8,128)(2,1)S(1)} %get-tuple-element.134), channel_id=1, source_target_pairs={{0,24},{1,25},{2,26},{3,27},{4,28},{5,29},{6,30},{7,31},{8,16},{9,... | collective-permute-start | bytes 172040 | tf_op jit(solution)/shard_map/ppermute | solution.py:35
  264.5 2.2 copy-done.1
  266.7 4.2 %shard_map.247 = f32[4,512,512]{2,1,0:T(8,128)} custom-call(bf16[4,512,512]{2,1,0:T(8,128)(2,1)S(1)} %copy-done, f32[4,512,512]{2,1,0:T(8,128)S(1)} %copy-done.1, bf16[4,64,512]{2,1,0:T(8,128)(2,1)S(1)} %collective-permute-done.25.b0, bf16[4,64,512]{2,1,0:T(8,128)(2,1)S(1)} %collective-permute-done.26.b1, ...), custom_call_target="tpu_custom_call" | custom-call | tf_op jit(solution)/shard_map/pallas_call | solution.py:952
  270.8 1.9 shard_map.252
  (138 shorter events, 28.5 us)
Async XLA Ops:
  4.8 14.5 %collective-permute-start.4 = (bf16[1,208,128]{2,1,0:T(8,128)(2,1)}, bf16[1,208,128]{2,1,0:T(8,128)(2,1)S(1)}, u32[]{:S(2)}, u32[]{:S(2)}) collective-permute-start(bf16[1,208,128]{2,1,0:T(8,128)(2,1)} %get-tuple-element.90.refs_0_), channel_id=1, source_target_pairs={{0,8},{1,9},{2,10},{3,11},{4,12},{5,13},{6,14},{7,15},{8,0},{9,1},... | collective-permute-start | bytes 159752 | tf_op jit(solution)/shard_map/ppermute | solution.py:35
  7.9 23.3 %collective-permute-start.14 = (bf16[1,592,128]{2,1,0:T(8,128)(2,1)}, bf16[1,592,128]{2,1,0:T(8,128)(2,1)S(1)}, u32[]{:S(2)}, u32[]{:S(2)}) collective-permute-start(bf16[1,592,128]{2,1,0:T(8,128)(2,1)} %get-tuple-element.93.refs_0_), channel_id=1, source_target_pairs={{0,8},{1,9},{2,10},{3,11},{4,12},{5,13},{6,14},{7,15},{8,0},{9,1},... | collective-permute-start | bytes 454664 | tf_op jit(solution)/shard_map/ppermute | solution.py:35
  13.7 37.4 %collective-permute-start = (bf16[4,64,512]{2,1,0:T(8,128)(2,1)}, bf16[4,64,512]{2,1,0:T(8,128)(2,1)S(1)}, u32[]{:S(2)}, u32[]{:S(2)}) collective-permute-start(bf16[4,64,512]{2,1,0:T(8,128)(2,1)} %get-tuple-element.83), channel_id=1, source_target_pairs={{30,0},{0,2},{2,4},{4,6},{6,8},{8,10},{10,12},{12,14},{14,16},{16,... | collective-permute-start | bytes 786440 | tf_op jit(solution)/shard_map/ppermute | solution.py:31
  13.7 37.4 %collective-permute-start.1 = (bf16[4,64,512]{2,1,0:T(8,128)(2,1)}, bf16[4,64,512]{2,1,0:T(8,128)(2,1)S(1)}, u32[]{:S(2)}, u32[]{:S(2)}) collective-permute-start(bf16[4,64,512]{2,1,0:T(8,128)(2,1)} %get-tuple-element.85), channel_id=1, source_target_pairs={{2,0},{4,2},{6,4},{8,6},{10,8},{12,10},{14,12},{16,14},{18,16},{20... | collective-permute-start | bytes 786440 | tf_op jit(solution)/shard_map/ppermute | solution.py:31
  18.1 11.7 %collective-permute-start.5 = (bf16[1,208,128]{2,1,0:T(8,128)(2,1)}, bf16[1,208,128]{2,1,0:T(8,128)(2,1)S(1)}, u32[]{:S(2)}, u32[]{:S(2)}) collective-permute-start(bf16[1,208,128]{2,1,0:T(8,128)(2,1)} %get-tuple-element.90.refs_0_), channel_id=1, source_target_pairs={{0,16},{1,17},{2,18},{3,19},{4,20},{5,21},{6,22},{7,23},{8,24},{9,... | collective-permute-start | bytes 159752 | tf_op jit(solution)/shard_map/ppermute | solution.py:35
  19.3 12.9 %collective-permute-start.15 = (bf16[1,592,128]{2,1,0:T(8,128)(2,1)}, bf16[1,592,128]{2,1,0:T(8,128)(2,1)S(1)}, u32[]{:S(2)}, u32[]{:S(2)}) collective-permute-start(bf16[1,592,128]{2,1,0:T(8,128)(2,1)} %get-tuple-element.93.refs_0_), channel_id=1, source_target_pairs={{0,16},{1,17},{2,18},{3,19},{4,20},{5,21},{6,22},{7,23},{8,24},{9,... | collective-permute-start | bytes 454664 | tf_op jit(solution)/shard_map/ppermute | solution.py:35
  31.3 21.8 %collective-permute-start.2 = (bf16[4,64,512]{2,1,0:T(8,128)(2,1)}, bf16[4,64,512]{2,1,0:T(8,128)(2,1)S(1)}, u32[]{:S(2)}, u32[]{:S(2)}) collective-permute-start(bf16[4,64,512]{2,1,0:T(8,128)(2,1)} %get-tuple-element.87), channel_id=1, source_target_pairs={{24,0},{26,2},{28,4},{30,6},{0,8},{2,10},{4,12},{6,14},{8,16},{10,... | collective-permute-start | bytes 786440 | tf_op jit(solution)/shard_map/ppermute | solution.py:31
  32.2 22.5 %collective-permute-start.3 = (bf16[4,64,512]{2,1,0:T(8,128)(2,1)}, bf16[4,64,512]{2,1,0:T(8,128)(2,1)S(1)}, u32[]{:S(2)}, u32[]{:S(2)}) collective-permute-start(bf16[4,64,512]{2,1,0:T(8,128)(2,1)} %get-tuple-element.89), channel_id=1, source_target_pairs={{8,0},{10,2},{12,4},{14,6},{16,8},{18,10},{20,12},{22,14},{24,16},... | collective-permute-start | bytes 786440 | tf_op jit(solution)/shard_map/ppermute | solution.py:31
  49.6 40.3 %collective-permute-start.17 = (bf16[4,592,128]{2,1,0:T(8,128)(2,1)S(1)}, bf16[4,592,128]{2,1,0:T(8,128)(2,1)S(1)}, u32[]{:S(2)}, u32[]{:S(2)}) collective-permute-start(bf16[4,592,128]{2,1,0:T(8,128)(2,1)S(1)} %shard_map.242.refs_5_), channel_id=1, source_target_pairs={{0,1},{1,0},{2,3},{3,2},{4,5},{5,4},{6,7},{7,6},{8,9},{9,8},{10,11... | collective-permute-start | bytes 1818632 | tf_op jit(solution)/shard_map/ppermute | solution.py:35
  51.1 38.8 %collective-permute-start.18 = (bf16[4,592,128]{2,1,0:T(8,128)(2,1)S(1)}, bf16[4,592,128]{2,1,0:T(8,128)(2,1)S(1)}, u32[]{:S(2)}, u32[]{:S(2)}) collective-permute-start(bf16[4,592,128]{2,1,0:T(8,128)(2,1)S(1)} %shard_map.242.refs_5_), channel_id=1, source_target_pairs={{0,4},{1,5},{2,6},{3,7},{4,0},{5,1},{6,2},{7,3},{8,12},{9,13},{10,... | collective-permute-start | bytes 1818632 | tf_op jit(solution)/shard_map/ppermute | solution.py:35
  51.1 39.2 %collective-permute-start.19 = (bf16[4,592,128]{2,1,0:T(8,128)(2,1)S(1)}, bf16[4,592,128]{2,1,0:T(8,128)(2,1)}, u32[]{:S(2)}, u32[]{:S(2)}) collective-permute-start(bf16[4,592,128]{2,1,0:T(8,128)(2,1)S(1)} %shard_map.242.refs_5_), channel_id=1, source_target_pairs={{0,5},{1,4},{2,7},{3,6},{4,1},{5,0},{6,3},{7,2},{8,13},{9,12},{10,... | collective-permute-start | bytes 1818632 | tf_op jit(solution)/shard_map/ppermute | solution.py:35
  53.1 29.3 %collective-permute-start.7 = (bf16[4,208,128]{2,1,0:T(8,128)(2,1)S(1)}, bf16[4,208,128]{2,1,0:T(8,128)(2,1)S(1)}, u32[]{:S(2)}, u32[]{:S(2)}) collective-permute-start(bf16[4,208,128]{2,1,0:T(8,128)(2,1)S(1)} %shard_map.240.refs_8_), channel_id=1, source_target_pairs={{0,1},{1,0},{2,3},{3,2},{4,5},{5,4},{6,7},{7,6},{8,9},{9,8},{10,11... | collective-permute-start | bytes 638984 | tf_op jit(solution)/shard_map/ppermute | solution.py:35
  54.7 29.8 %collective-permute-start.8 = (bf16[4,208,128]{2,1,0:T(8,128)(2,1)S(1)}, bf16[4,208,128]{2,1,0:T(8,128)(2,1)S(1)}, u32[]{:S(2)}, u32[]{:S(2)}) collective-permute-start(bf16[4,208,128]{2,1,0:T(8,128)(2,1)S(1)} %shard_map.240.refs_8_), channel_id=1, source_target_pairs={{0,4},{1,5},{2,6},{3,7},{4,0},{5,1},{6,2},{7,3},{8,12},{9,13},{10,... | collective-permute-start | bytes 638984 | tf_op jit(solution)/shard_map/ppermute | solution.py:35
  89.3 30.4 %collective-permute-start.20 = (bf16[4,592,128]{2,1,0:T(8,128)(2,1)S(1)}, bf16[4,592,128]{2,1,0:T(8,128)(2,1)}, u32[]{:S(2)}, u32[]{:S(2)}) collective-permute-start(bf16[4,592,128]{2,1,0:T(8,128)(2,1)S(1)} %shard_map.242.refs_5_), channel_id=1, source_target_pairs={{0,2},{1,3},{2,0},{3,1},{4,6},{5,7},{6,4},{7,5},{8,10},{9,11},{10,... | collective-permute-start | bytes 1818632 | tf_op jit(solution)/shard_map/ppermute | solution.py:35
  89.8 29.9 %collective-permute-start.21 = (bf16[4,592,128]{2,1,0:T(8,128)(2,1)S(1)}, bf16[4,592,128]{2,1,0:T(8,128)(2,1)}, u32[]{:S(2)}, u32[]{:S(2)}) collective-permute-start(bf16[4,592,128]{2,1,0:T(8,128)(2,1)S(1)} %collective-permute-done.17.refs_6_), channel_id=1, source_target_pairs={{0,2},{1,3},{2,0},{3,1},{4,6},{5,7},{6,4},{7,5},{8,10},{9,11},{10,... | collective-permute-start | bytes 1818632 | tf_op jit(solution)/shard_map/ppermute | solution.py:35
  89.9 29.8 %collective-permute-start.22 = (bf16[4,592,128]{2,1,0:T(8,128)(2,1)S(1)}, bf16[4,592,128]{2,1,0:T(8,128)(2,1)}, u32[]{:S(2)}, u32[]{:S(2)}) collective-permute-start(bf16[4,592,128]{2,1,0:T(8,128)(2,1)S(1)} %collective-permute-done.18.refs_7_), channel_id=1, source_target_pairs={{0,2},{1,3},{2,0},{3,1},{4,6},{5,7},{6,4},{7,5},{8,10},{9,11},{10,... | collective-permute-start | bytes 1818632 | tf_op jit(solution)/shard_map/ppermute | solution.py:35
  90.3 29.4 %collective-permute-start.23 = (bf16[4,592,128]{2,1,0:T(8,128)(2,1)}, bf16[4,592,128]{2,1,0:T(8,128)(2,1)}, u32[]{:S(2)}, u32[]{:S(2)}) collective-permute-start(bf16[4,592,128]{2,1,0:T(8,128)(2,1)} %collective-permute-done.19.refs_8_), channel_id=1, source_target_pairs={{0,2},{1,3},{2,0},{3,1},{4,6},{5,7},{6,4},{7,5},{8,10},{9,11},{10,... | collective-permute-start | bytes 1818632 | tf_op jit(solution)/shard_map/ppermute | solution.py:35
  163.7 11.4 %collective-permute-start.24 = (bf16[16,592,128]{2,1,0:T(8,128)(2,1)}, bf16[16,592,128]{2,1,0:T(8,128)(2,1)S(1)}, u32[]{:S(2)}, u32[]{:S(2)}) collective-permute-start(bf16[16,592,128]{2,1,0:T(8,128)(2,1)} %get-tuple-element.108), channel_id=1, source_target_pairs={{0,2},{1,3},{2,0},{3,1},{4,6},{5,7},{6,4},{7,5},{8,10},{9,11},{10,... | collective-permute-start | bytes 7274504 | tf_op jit(solution)/shard_map/ppermute | solution.py:35
  202.2 35.9 %collective-permute-start.36 = (bf16[4,592,128]{2,1,0:T(8,128)(2,1)S(1)}, bf16[4,592,128]{2,1,0:T(8,128)(2,1)S(1)}, u32[]{:S(2)}, u32[]{:S(2)}) collective-permute-start(bf16[4,592,128]{2,1,0:T(8,128)(2,1)S(1)} %get-tuple-element.138), channel_id=1, source_target_pairs={{0,1},{1,0},{2,3},{3,2},{4,5},{5,4},{6,7},{7,6},{8,9},{9,8},{10,11... | collective-permute-start | bytes 1818632 | tf_op jit(solution)/shard_map/ppermute | solution.py:35
  203.7 35.2 %collective-permute-start.37 = (bf16[4,592,128]{2,1,0:T(8,128)(2,1)S(1)}, bf16[4,592,128]{2,1,0:T(8,128)(2,1)S(1)}, u32[]{:S(2)}, u32[]{:S(2)}) collective-permute-start(bf16[4,592,128]{2,1,0:T(8,128)(2,1)S(1)} %get-tuple-element.139), channel_id=1, source_target_pairs={{0,4},{1,5},{2,6},{3,7},{4,0},{5,1},{6,2},{7,3},{8,12},{9,13},{10,... | collective-permute-start | bytes 1818632 | tf_op jit(solution)/shard_map/ppermute | solution.py:35
  203.7 36.5 %collective-permute-start.38 = (bf16[4,592,128]{2,1,0:T(8,128)(2,1)S(1)}, bf16[4,592,128]{2,1,0:T(8,128)(2,1)S(1)}, u32[]{:S(2)}, u32[]{:S(2)}) collective-permute-start(bf16[4,592,128]{2,1,0:T(8,128)(2,1)S(1)} %get-tuple-element.140), channel_id=1, source_target_pairs={{0,5},{1,4},{2,7},{3,6},{4,1},{5,0},{6,3},{7,2},{8,13},{9,12},{10,... | collective-permute-start | bytes 1818632 | tf_op jit(solution)/shard_map/ppermute | solution.py:35
  209.7 32.5 %collective-permute-start.30 = (bf16[4,224,128]{2,1,0:T(8,128)(2,1)S(1)}, bf16[4,224,128]{2,1,0:T(8,128)(2,1)S(1)}, u32[]{:S(2)}, u32[]{:S(2)}) collective-permute-start(bf16[4,224,128]{2,1,0:T(8,128)(2,1)S(1)} %get-tuple-element.128), channel_id=1, source_target_pairs={{0,1},{1,0},{2,3},{3,2},{4,5},{5,4},{6,7},{7,6},{8,9},{9,8},{10,11... | collective-permute-start | bytes 688136 | tf_op jit(solution)/shard_map/ppermute | solution.py:35
  214.4 30.3 %collective-permute-start.31 = (bf16[4,224,128]{2,1,0:T(8,128)(2,1)S(1)}, bf16[4,224,128]{2,1,0:T(8,128)(2,1)S(1)}, u32[]{:S(2)}, u32[]{:S(2)}) collective-permute-start(bf16[4,224,128]{2,1,0:T(8,128)(2,1)S(1)} %get-tuple-element.129), channel_id=1, source_target_pairs={{0,4},{1,5},{2,6},{3,7},{4,0},{5,1},{6,2},{7,3},{8,12},{9,13},{10,... | collective-permute-start | bytes 688136 | tf_op jit(solution)/shard_map/ppermute | solution.py:35
  238.1 11.0 %collective-permute-start.32 = (bf16[4,224,128]{2,1,0:T(8,128)(2,1)S(1)}, bf16[4,224,128]{2,1,0:T(8,128)(2,1)S(1)}, u32[]{:S(2)}, u32[]{:S(2)}) collective-permute-start(bf16[4,224,128]{2,1,0:T(8,128)(2,1)S(1)} %get-tuple-element.130), channel_id=1, source_target_pairs={{0,5},{1,4},{2,7},{3,6},{4,1},{5,0},{6,3},{7,2},{8,13},{9,12},{10,... | collective-permute-start | bytes 688136 | tf_op jit(solution)/shard_map/ppermute | solution.py:35
  238.9 12.9 %collective-permute-start.27 = (bf16[4,64,512]{2,1,0:T(8,128)(2,1)S(1)}, bf16[4,64,512]{2,1,0:T(8,128)(2,1)S(1)}, u32[]{:S(2)}, u32[]{:S(2)}) collective-permute-start(bf16[4,64,512]{2,1,0:T(8,128)(2,1)S(1)} %get-tuple-element.123), channel_id=1, source_target_pairs={{8,0},{10,2},{12,4},{14,6},{16,8},{18,10},{20,12},{22,14},{24,16},... | collective-permute-start | bytes 786440 | tf_op jit(solution)/shard_map/ppermute | solution.py:31
  240.3 17.3 %collective-permute-start.28 = (bf16[4,64,512]{2,1,0:T(8,128)(2,1)S(1)}, bf16[4,64,512]{2,1,0:T(8,128)(2,1)S(1)}, u32[]{:S(2)}, u32[]{:S(2)}) collective-permute-start(bf16[4,64,512]{2,1,0:T(8,128)(2,1)S(1)} %get-tuple-element.124), channel_id=1, source_target_pairs={{24,0},{26,2},{28,4},{30,6},{0,8},{2,10},{4,12},{6,14},{8,16},{10,... | collective-permute-start | bytes 786440 | tf_op jit(solution)/shard_map/ppermute | solution.py:31
  242.2 18.4 %collective-permute-start.39 = (bf16[1,592,128]{2,1,0:T(8,128)(2,1)S(1)}, bf16[1,592,128]{2,1,0:T(8,128)(2,1)S(1)}, u32[]{:S(2)}, u32[]{:S(2)}) collective-permute-start(bf16[1,592,128]{2,1,0:T(8,128)(2,1)S(1)} %get-tuple-element.142), channel_id=1, source_target_pairs={{0,8},{1,9},{2,10},{3,11},{4,12},{5,13},{6,14},{7,15},{8,0},{9,1},... | collective-permute-start | bytes 454664 | tf_op jit(solution)/shard_map/ppermute | solution.py:35
  244.7 26.1 %collective-permute-start.40 = (bf16[1,592,128]{2,1,0:T(8,128)(2,1)S(1)}, bf16[1,592,128]{2,1,0:T(8,128)(2,1)}, u32[]{:S(2)}, u32[]{:S(2)}) collective-permute-start(bf16[1,592,128]{2,1,0:T(8,128)(2,1)S(1)} %get-tuple-element.143), channel_id=1, source_target_pairs={{0,16},{1,17},{2,18},{3,19},{4,20},{5,21},{6,22},{7,23},{8,24},{9,... | collective-permute-start | bytes 454664 | tf_op jit(solution)/shard_map/ppermute | solution.py:35
  249.2 21.6 %collective-permute-start.41 = (bf16[1,592,128]{2,1,0:T(8,128)(2,1)S(1)}, bf16[1,592,128]{2,1,0:T(8,128)(2,1)}, u32[]{:S(2)}, u32[]{:S(2)}) collective-permute-start(bf16[1,592,128]{2,1,0:T(8,128)(2,1)S(1)} %get-tuple-element.144), channel_id=1, source_target_pairs={{0,24},{1,25},{2,26},{3,27},{4,28},{5,29},{6,30},{7,31},{8,16},{9,... | collective-permute-start | bytes 454664 | tf_op jit(solution)/shard_map/ppermute | solution.py:35
  251.8 20.8 %collective-permute-start.33 = (bf16[1,224,128]{2,1,0:T(8,128)(2,1)}, bf16[1,224,128]{2,1,0:T(8,128)(2,1)}, u32[]{:S(2)}, u32[]{:S(2)}) collective-permute-start(bf16[1,224,128]{2,1,0:T(8,128)(2,1)} %get-tuple-element.132), channel_id=1, source_target_pairs={{0,8},{1,9},{2,10},{3,11},{4,12},{5,13},{6,14},{7,15},{8,0},{9,1},... | collective-permute-start | bytes 172040 | tf_op jit(solution)/shard_map/ppermute | solution.py:35
  257.5 15.3 %collective-permute-start.34 = (bf16[1,224,128]{2,1,0:T(8,128)(2,1)}, bf16[1,224,128]{2,1,0:T(8,128)(2,1)}, u32[]{:S(2)}, u32[]{:S(2)}) collective-permute-start(bf16[1,224,128]{2,1,0:T(8,128)(2,1)} %get-tuple-element.133), channel_id=1, source_target_pairs={{0,16},{1,17},{2,18},{3,19},{4,20},{5,21},{6,22},{7,23},{8,24},{9,... | collective-permute-start | bytes 172040 | tf_op jit(solution)/shard_map/ppermute | solution.py:35
  261.2 11.6 %collective-permute-start.35 = (bf16[1,224,128]{2,1,0:T(8,128)(2,1)S(1)}, bf16[1,224,128]{2,1,0:T(8,128)(2,1)}, u32[]{:S(2)}, u32[]{:S(2)}) collective-permute-start(bf16[1,224,128]{2,1,0:T(8,128)(2,1)S(1)} %get-tuple-element.134), channel_id=1, source_target_pairs={{0,24},{1,25},{2,26},{3,27},{4,28},{5,29},{6,30},{7,31},{8,16},{9,... | collective-permute-start | bytes 172040 | tf_op jit(solution)/shard_map/ppermute | solution.py:35
  (45 other events, 1044.6 us)
where the time goes:
time: 275 us; the launch traced here: 274 us
  Pallas kernels  120 us (44%)
  waiting for transfers between devices  73.2 us (27%)
  starting transfers between devices  71.6 us (26%)
  local copies, waits for them, and re-layouts  8.07 us (3%)
    ppermute x34, waiting for transfers between devices, swap(): return lax.ppermute(block, AXES, [(i, i ^ bits) for i in range(devices)])  64.9 us
    ppermute x34, starting transfers between devices, swap(): return lax.ppermute(block, AXES, [(i, i ^ bits) for i in range(devices)])  60.9 us
    pallas_call x1, Pallas kernels, feed(): pl.pallas_call(lambda *refs: feed_kernel(*refs, shards=len(shards or ()))...  43.9 us
    pallas_call x2, Pallas kernels, attend_back(): pl.pallas_call(lambda *refs: attend_back_kernel(*refs, started=bool(carri...  36 us
    pallas_call x1, Pallas kernels, attend(): pl.pallas_call(lambda *refs: attend_kernel(*refs, pieces=first), grid=(sa...  23.2 us
    ppermute x8, starting transfers between devices, from_behind(): lax.ppermute(block, 'patch', [((i - distance) % count, i) for i in range(...  10.8 us
    ppermute x8, waiting for transfers between devices, from_behind(): lax.ppermute(block, 'patch', [((i - distance) % count, i) for i in range(...  8.25 us
    unnamed x70, local copies, waits for them, and re-layouts  7.99 us
  transfers between devices with their start and end apart: 42, of which 16 were waited for; matrix products, arithmetic and copies ran while one was open for 0% of the time, Pallas kernels for 16%

commit v1 on v0

--- a/solution.py
+++ b/solution.py
@@ -16,6 +16,7 @@
 F32 = jnp.float32
 BF16 = jnp.bfloat16
 MIB = 1024 * 1024
+EMIT_LIMIT = 20
 
 
 def product(left, right):
@@ -347,44 +348,47 @@
     )(*pieces)
 
 
-def last_kernel(*refs, pieces, first):
-    me_ref = refs[0]
-    sources, outs = refs[1 : 1 + pieces], refs[1 + pieces :]
+def last_kernel(me_ref, *refs, pieces):
+    feed_refs, proj_refs = refs[: pieces[0]], refs[pieces[0] : sum(pieces)]
+    outs = refs[sum(pieces) :]
     position = me_ref[0]
 
-    def total(at, height):
-        value = sources[0][0, at : at + height, :].astype(F32)
+    def total(sources, at):
+        value = sources[0][0, at : at + BLOCK, :].astype(F32)
         for ref in sources[1:]:
-            value = value + ref[0, at : at + height, :].astype(F32)
+            value = value + ref[0, at : at + BLOCK, :].astype(F32)
         return value
 
-    at = 0
-    for ref in outs[:3]:
-        for rows, cols in blocks_of(ref):
-            ref[rows, cols] = total(at, BLOCK)
-            at += BLOCK
-    if first:
-        cond = total(at, BLOCK)
-        step = outs[3].shape[1]
-        begin = lax.rem(position * step, 128)
-        outs[3][...] = pltpu.roll(cond, 128 - begin, 1)[:, 0:step]
-        bias = total(at + BLOCK, BLOCK)
-        outs[4][...] = pltpu.roll(bias, 128 - begin, 1)[0:1, 0:step]
-    else:
-        last = total(at, BLOCK)
-        for row, ref in enumerate(outs[3:]):
-            step = ref.shape[1]
-            begin = lax.rem(position * step, 128)
-            ref[...] = pltpu.roll(last, 128 - begin, 1)[row : row + 1, 0:step]
-
-
-def last_sum(me, pieces, shapes, first):
+    def own(value, step, row, height):
+        shift = 128 - lax.rem(position * step, 128)
+        return pltpu.roll(value, shift, 1)[row : row + height, 0:step]
+
+    def unpack(sources, refs):
+        at = 0
+        for ref in refs:
+            for rows, cols in blocks_of(ref):
+                ref[rows, cols] = total(sources, at)
+                at += BLOCK
+        return at
+
+    at = unpack(feed_refs, outs[:3])
+    biases = total(feed_refs, at)
+    for row, ref in enumerate(outs[3:5]):
+        ref[...] = own(biases, ref.shape[1], row, 1)
+    at = unpack(proj_refs, outs[5:8])
+    step = outs[8].shape[1]
+    outs[8][...] = own(total(proj_refs, at), step, 0, BLOCK)
+    outs[9][...] = own(total(proj_refs, at + BLOCK), step, 0, 1)
+
+
+def last_sum(me, feed_pieces, proj_pieces, shapes):
+    pieces = (len(feed_pieces), len(proj_pieces))
     return pl.pallas_call(
-        lambda *refs: last_kernel(*refs, pieces=len(pieces), first=first),
+        lambda *refs: last_kernel(*refs, pieces=pieces),
         out_shape=[jax.ShapeDtypeStruct(shape, F32) for shape in shapes],
-        in_specs=[smem()] + [pl.BlockSpec(memory_space=pltpu.VMEM)] * len(pieces),
+        in_specs=[smem()] + [pl.BlockSpec(memory_space=pltpu.VMEM)] * sum(pieces),
         compiler_params=plain(60),
-    )(me, *pieces)
+    )(me, *feed_pieces, *proj_pieces)
 
 
 def smem():
@@ -529,12 +533,13 @@
 
 def feed_kernel(*refs, shards):
     me_ref, nodes_ref, att_ref, cot_ref, mod_ref = refs[:5]
-    scratch = 6 + (10 + shards if shards else 0)
-    up_acc, down_acc, wo_acc, bu_acc, bd_acc, down_rows = refs[len(refs) - 6 :]
+    scratch = 9 + (10 + shards if shards else 0)
+    up_acc, down_acc, wo_acc, bu_acc, bd_acc, down_rows = refs[-9:-3]
+    hid_buf, hid_sems, wd_sem = refs[-3:]
     if shards:
         pieces = refs[5 : 5 + shards]
-        *piece_bufs, low_buf, high_buf, in_sems, out_sems = refs[-scratch:-12]
-        wo_ref, wu_ref, wd_ref, bu_ref, bd_ref, raw = refs[-12:-6]
+        *piece_bufs, low_buf, high_buf, in_sems, out_sems = refs[-scratch:-15]
+        wo_ref, wu_ref, wd_ref, bu_ref, bd_ref, raw = refs[-15:-9]
         outs = refs[5 + shards : -scratch]
 
         @pl.when(pl.program_id(0) == 0)
@@ -552,8 +557,16 @@
     else:
         wo_ref, wu_ref, wd_ref, bu_ref, bd_ref = refs[5:10]
         outs = refs[10:-scratch]
-    out_ref, gmid_ref, gatt_ref, gmod_ref = outs[:4]
-    sums = outs[4:]
+    part_ref, gmid_ref, gatt_ref, gmod_ref, hid_ref = outs[:5]
+    sums = outs[5:]
+    if shards:
+        down_copy = pltpu.make_async_copy(wd_ref, outs[5], wd_sem.at[0])
+        sums = outs[6:]
+
+        @pl.when(pl.program_id(0) == 0)
+        def _():
+            down_copy.start()
+
     s = pl.program_id(0)
     count, width = nodes_ref.shape[1:]
     hidden_size = wu_ref.shape[1]
@@ -561,6 +574,15 @@
 
     def add_to(ref, cols, value):
         ref[:, cols] = jnp.where(s == 0, 0.0, ref[:, cols]) + value
+
+    slot = lax.rem(s, 2)
+
+    def hid_copy(sample, place):
+        return pltpu.make_async_copy(hid_buf.at[place], hid_ref.at[sample], hid_sems.at[place])
+
+    @pl.when(s > 1)
+    def _():
+        hid_copy(s - 2, slot).wait()
 
     scale, shift = mod_ref[0, 2:3, :], mod_ref[0, 3:4, :]
     blocks = [slice(c * width, (c + 1) * width) for c in range(wide)]
@@ -573,7 +595,7 @@
     hat, inverse = layer_normalize(middle)
     act = (hat * scale + shift).astype(BF16)
     act_t = act.T
-    result = middle + bd_ref[...]
+    part_ref[0] = middle + bd_ref[...]
     grad_act = jnp.zeros((count, width), F32)
 
     pre_ahead = product(act, wu_ref[:, blocks[0]])
@@ -585,7 +607,6 @@
             grad_ahead = product_t(cot, wd_ref[blocks[c + 1], :])
         if ready:
             old, hidden, low_pre = ready
-            result = result + product(hidden, wd_ref[old, :])
             grad_act = grad_act + product_t(low_pre, wu_ref[:, old])
             add_to(down_acc, old, product(cot_t, hidden))
             add_to(up_acc, old, product(act_t, low_pre))
@@ -595,15 +616,15 @@
         low_pre = (grad_hidden * (gate + value * (1.0 - gate))).astype(BF16)
         add_to(bu_acc, cols, jnp.sum(low_pre.astype(F32), axis=0, keepdims=True))
         ready = (cols, value.astype(BF16), low_pre)
+        hid_buf[slot, :, cols] = ready[1]
+    hid_copy(s, slot).start()
     old, hidden, low_pre = ready
     grad_act = grad_act + product_t(low_pre, wu_ref[:, old])
-    result = result + product(hidden, wd_ref[old, :])
     add_to(down_acc, old, product(cot_t, hidden))
     add_to(up_acc, old, product(act_t, low_pre))
     grad_middle = cot.astype(F32) + norm_back(grad_act * scale, hat, inverse)
     gmid_ref[0] = grad_middle
     branch = grad_middle.astype(BF16)
-    out_ref[0] = result.astype(BF16)
     gmod_ref[0, 0:1, :] = jnp.sum(grad_act * hat, axis=0, keepdims=True)
     gmod_ref[0, 1:2, :] = jnp.sum(grad_act, axis=0, keepdims=True)
     gatt_ref[0] = product_t(branch, wo_ref[...]).astype(BF16)
@@ -611,6 +632,14 @@
 
     @pl.when(s == pl.num_programs(0) - 1)
     def _():
+        hid_copy(s, slot).wait()
+
+        @pl.when(s > 0)
+        def _():
+            hid_copy(s - 1, 1 - slot).wait()
+
+        if shards:
+            down_copy.wait()
         for c in range(wide):
             cols = slice(c * width, (c + 1) * width)
             down_rows[cols, :] = down_acc[:, cols].T
@@ -672,7 +701,11 @@
         pltpu.VMEM((1, hidden), F32),
         pltpu.VMEM((1, width), F32),
         pltpu.VMEM((hidden, width), F32),
+        pltpu.VMEM((2, count, hidden), BF16),
+        pltpu.SemaphoreType.DMA((2,)),
+        pltpu.SemaphoreType.DMA((1,)),
     ]
+    down = [jax.ShapeDtypeStruct((hidden, width), BF16)] if shards else []
     if shards:
         rows = shards[0].shape[1]
         sums = [jax.ShapeDtypeStruct((devices // 2, rows, 128), BF16)] * 2
@@ -696,18 +729,39 @@
         grid=(samples,),
         in_specs=[smem(), tile, tile, tile, per_sample((4, width))]
         + [anywhere() if shards else once(x.shape) for x in extra],
-        out_specs=[tile, tile, tile, per_sample((2, width))]
+        out_specs=[tile, tile, tile, per_sample((2, width)), anywhere()]
+        + [anywhere()] * len(down)
         + [anywhere() if shards else once(x.shape) for x in sums],
         out_shape=[
-            jax.ShapeDtypeStruct((samples, count, width), BF16),
+            jax.ShapeDtypeStruct((samples, count, width), F32),
             jax.ShapeDtypeStruct((samples, count, width), F32),
             jax.ShapeDtypeStruct((samples, count, width), BF16),
             jax.ShapeDtypeStruct((samples, 2, width), F32),
+            jax.ShapeDtypeStruct((samples, count, hidden), BF16),
         ]
+        + down
         + sums,
         scratch_shapes=scratch,
         compiler_params=params(60),
     )(me, nodes, attended, cot, mod, *extra)
+
+
+def emit_kernel(hid_ref, wd_ref, part_ref, out_ref):
+    out_ref[0] = (part_ref[0] + product(hid_ref[0], wd_ref[...])).astype(BF16)
+
+
+def emit(hid, wd, part):
+    samples, count, width = part.shape
+    hidden = wd.shape[0]
+    tile = per_sample((count, width))
+    return pl.pallas_call(
+        emit_kernel,
+        grid=(samples,),
+        in_specs=[per_sample((count, hidden)), once((hidden, width)), tile],
+        out_specs=tile,
+        out_shape=jax.ShapeDtypeStruct(part.shape, BF16),
+        compiler_params=params(EMIT_LIMIT),
+    )(hid, wd, part)
 
 
 def attend_back_kernel(*refs, started, last, begin):
@@ -1029,7 +1083,7 @@
         nodes, halos, bias, shards=[me, noise_code] + low_first + high_first
     )
     high_second = cores(low_second)
-    result, gmid, gatt, gmod, low_feed, high_feed = feed(
+    part, gmid, gatt, gmod, hid, down_whole, low_feed, high_feed = feed(
         me,
         nodes,
         attended,
@@ -1053,22 +1107,30 @@
     own_proj, *parts = add_halves(low_proj, got_proj, 4)
     proj_far = swaps(parts, plane)
     backs = shifts(rest[:4], -1)
+    result = emit(hid, down_whole, after(part, own_feed))
     own_proj, *parts = add_pieces([own_proj] + proj_far)
     proj_last = swaps(parts, z_side)
     grad_nodes = finish(nodes, base, backs, send_rows, mod)
     down, thin = hidden // devices, width // devices
-    grad_up, grad_down, grad_out, grad_b_up, grad_b_down = last_sum(
+    step = 4 * width // devices
+    (
+        grad_up,
+        grad_down,
+        grad_out,
+        grad_b_up,
+        grad_b_down,
+        grad_query,
+        grad_key,
+        grad_value,
+        grad_cond,
+        grad_cond_bias,
+    ) = last_sum(
         me,
         [own_feed] + feed_last,
-        ((BLOCK, hidden), (down, width), (BLOCK, width), (1, down), (1, thin)),
-        False,
-    )
-    step = 4 * width // devices
-    grad_query, grad_key, grad_value, grad_cond, grad_cond_bias = last_sum(
-        me,
         [own_proj] + proj_last,
-        ((BLOCK, width),) * 3 + ((BLOCK, step), (1, step)),
-        True,
+        ((BLOCK, hidden), (down, width), (BLOCK, width), (1, down), (1, thin))
+        + ((BLOCK, width),) * 3
+        + ((BLOCK, step), (1, step)),
     )
     grad_b_up, grad_b_down, grad_cond_bias = grad_b_up[0], grad_b_down[0], grad_cond_bias[0]
     return (
@@ -1098,9 +1160,10 @@
     halos = [from_behind(block, offset) for block, offset in zip(sends, offsets)]
     (wq, wk, wv, mod), weights = gather_plain(*first, *second)
     *saved, attended = attend(nodes, halos, bias, weights=(wq, wk, wv, mod))
-    result, gmid, gatt, gmod, *sums = feed(
+    part, gmid, gatt, gmod, hid, *sums = feed(
         me, nodes, attended, cotangent, mod, hidden, devices, weights=weights
     )
+    result = emit(hid, weights[2], part)
     sums[3:] = [x[0] for x in sums[3:]]
     grad_up, grad_down, grad_out, grad_b_up, grad_b_down = scatter_plain(sums, (0,) * 5)
     base, *rest = attend_back(

time: 275 us -> 280 us (1.018)
  local copies, waits for them, and re-layouts: 8.07 us -> 11.5 us
    pallas_call x2, Pallas kernels: 3.45 us -> 7.77 us  [the longest x1 5.8 us: emit(): pl.pallas_call(emit_kernel, grid=(samples,), in_specs=[per_sample((count,...]
    unnamed x70 -> x76, local copies, waits for them, and re-layouts: 7.99 us -> 11.4 us
  transfers between devices with their start and end apart: 42 -> 42, of which waited for: 16 -> 15; matrix products, arithmetic and copies ran while one was open for 0% -> 0% of each run, Pallas kernels for 16% -> 17%
where the time goes in v1:
time: 280 us; the launch traced here: 279 us
  Pallas kernels  122 us (44%)
  waiting for transfers between devices  73 us (26%)
  starting transfers between devices  71.6 us (26%)
  local copies, waits for them, and re-layouts  11.5 us (4%)
    ppermute x34, waiting for transfers between devices, swap(): return lax.ppermute(block, AXES, [(i, i ^ bits) for i in range(devices)])  64.7 us
    ppermute x34, starting transfers between devices, swap(): return lax.ppermute(block, AXES, [(i, i ^ bits) for i in range(devices)])  60.9 us
    pallas_call x1, Pallas kernels, feed(): pl.pallas_call(lambda *refs: feed_kernel(*refs, shards=len(shards or ()))...  41.2 us
    pallas_call x2, Pallas kernels, attend_back(): pl.pallas_call(lambda *refs: attend_back_kernel(*refs, started=bool(carri...  36 us
    pallas_call x1, Pallas kernels, attend(): pl.pallas_call(lambda *refs: attend_kernel(*refs, pieces=first), grid=(sa...  23.2 us
    unnamed x76, local copies, waits for them, and re-layouts  11.4 us
    ppermute x8, starting transfers between devices, from_behind(): lax.ppermute(block, 'patch', [((i - distance) % count, i) for i in range(...  10.8 us
    ppermute x8, waiting for transfers between devices, from_behind(): lax.ppermute(block, 'patch', [((i - distance) % count, i) for i in range(...  8.26 us
  transfers between devices with their start and end apart: 42, of which 15 were waited for; matrix products, arithmetic and copies ran while one was open for 0% of the time, Pallas kernels for 17%

profile of v1, /device:TPU:0, one launch (start us, length us, event | category | flops | bytes accessed | tf_op | source)
XLA Modules:
  0.0 279.3 jit_solution(8819241730940896087)
XLA Ops:
  0.6 4.2 %shard_map.238 = (bf16[4,64,512]{2,1,0:T(8,128)(2,1)}, bf16[4,64,512]{2,1,0:T(8,128)(2,1)}, bf16[4,64,512]{2,1,0:T(8,128)(2,1)}, bf16[4,64,512]{2,1,0:T(8,128)(2...) custom-call(bf16[4,512,512]{2,1,0:T(8,128)(2,1)} %nodes_ref.1, s32[4,64]{1,0:T(4,128)} %refs_1_.4, ...), custom_call_target="tpu_custom_call" | custom-call | tf_op jit(solution)/shard_map/pallas_call | solution.py:205
  4.8 3.1 %collective-permute-start.4 = (bf16[1,208,128]{2,1,0:T(8,128)(2,1)}, bf16[1,208,128]{2,1,0:T(8,128)(2,1)S(1)}, u32[]{:S(2)}, u32[]{:S(2)}) collective-permute-start(bf16[1,208,128]{2,1,0:T(8,128)(2,1)} %get-tuple-element.93.refs_0_), channel_id=1, source_target_pairs={{0,8},{1,9},{2,10},{3,11},{4,12},{5,13},{6,14},{7,15},{8,0},{9,1},... | collective-permute-start | bytes 159752 | tf_op jit(solution)/shard_map/ppermute | solution.py:36
  8.8 3.7 %shard_map.239.refs_5_ = f32[768,512]{1,0:T(8,128)S(1)} custom-call(s32[16,512]{1,0:T(8,128)S(1)} %bitcast.8), custom_call_target="tpu_custom_call" | custom-call | tf_op jit(solution)/shard_map/pallas_call | solution.py:143
  13.7 4.4 %collective-permute-start.1 = (bf16[4,64,512]{2,1,0:T(8,128)(2,1)}, bf16[4,64,512]{2,1,0:T(8,128)(2,1)S(1)}, u32[]{:S(2)}, u32[]{:S(2)}) collective-permute-start(bf16[4,64,512]{2,1,0:T(8,128)(2,1)} %get-tuple-element.88), channel_id=1, source_target_pairs={{2,0},{4,2},{6,4},{8,6},{10,8},{12,10},{14,12},{16,14},{18,16},{20... | collective-permute-start | bytes 786440 | tf_op jit(solution)/shard_map/ppermute | solution.py:32
  19.3 1.8 collective-permute-start.15
  21.0 8.8 %collective-permute-done.5.refs_2_ = bf16[1,208,128]{2,1,0:T(8,128)(2,1)S(1)} collective-permute-done((bf16[1,208,128]{2,1,0:T(8,128)(2,1)}, bf16[1,208,128]{2,1,0:T(8,128)(2,1)S(1)}, u32[]{:S(2)}, u32[]{:S(2)}) %collective-permute-start.5) | collective-permute-done | bytes 53280 | tf_op jit(solution)/shard_map/ppermute | solution.py:36
  32.2 2.9 %collective-permute-start.3 = (bf16[4,64,512]{2,1,0:T(8,128)(2,1)}, bf16[4,64,512]{2,1,0:T(8,128)(2,1)S(1)}, u32[]{:S(2)}, u32[]{:S(2)}) collective-permute-start(bf16[4,64,512]{2,1,0:T(8,128)(2,1)} %get-tuple-element.92), channel_id=1, source_target_pairs={{8,0},{10,2},{12,4},{14,6},{16,8},{18,10},{20,12},{22,14},{24,16},... | collective-permute-start | bytes 786440 | tf_op jit(solution)/shard_map/ppermute | solution.py:32
  35.1 3.5 %collective-permute-done.16.refs_3_ = bf16[1,592,128]{2,1,0:T(8,128)(2,1)S(1)} collective-permute-done((bf16[1,592,128]{2,1,0:T(8,128)(2,1)}, bf16[1,592,128]{2,1,0:T(8,128)(2,1)S(1)}, u32[]{:S(2)}, u32[]{:S(2)}) %collective-permute-start.16) | collective-permute-done | bytes 151584 | tf_op jit(solution)/shard_map/ppermute | solution.py:36
  41.1 8.5 %collective-permute-done.6.refs_3_ = bf16[1,208,128]{2,1,0:T(8,128)(2,1)S(1)} collective-permute-done((bf16[1,208,128]{2,1,0:T(8,128)(2,1)}, bf16[1,208,128]{2,1,0:T(8,128)(2,1)S(1)}, u32[]{:S(2)}, u32[]{:S(2)}) %collective-permute-start.6) | collective-permute-done | bytes 53280 | tf_op jit(solution)/shard_map/ppermute | solution.py:36
  51.1 1.9 collective-permute-start.19
  54.8 27.7 %collective-permute-done.7.refs_9_ = bf16[4,208,128]{2,1,0:T(8,128)(2,1)S(1)} collective-permute-done((bf16[4,208,128]{2,1,0:T(8,128)(2,1)S(1)}, bf16[4,208,128]{2,1,0:T(8,128)(2,1)S(1)}, u32[]{:S(2)}, u32[]{:S(2)}) %collective-permute-start.7) | collective-permute-done | bytes 213024 | tf_op jit(solution)/shard_map/ppermute | solution.py:36
  82.4 2.0 collective-permute-done.8.refs_10_
  84.5 4.8 %collective-permute-done.9.refs_11_ = bf16[4,208,128]{2,1,0:T(8,128)(2,1)} collective-permute-done((bf16[4,208,128]{2,1,0:T(8,128)(2,1)S(1)}, bf16[4,208,128]{2,1,0:T(8,128)(2,1)}, u32[]{:S(2)}, u32[]{:S(2)}) %collective-permute-start.9) | collective-permute-done | bytes 213024 | tf_op jit(solution)/shard_map/ppermute | solution.py:36
  90.9 3.6 %collective-permute-done.12.refs_14_ = bf16[4,208,128]{2,1,0:T(8,128)(2,1)S(1)} collective-permute-done((bf16[4,208,128]{2,1,0:T(8,128)(2,1)S(1)}, bf16[4,208,128]{2,1,0:T(8,128)(2,1)S(1)}, u32[]{:S(2)}, u32[]{:S(2)}) %collective-permute-start.12) | collective-permute-done | bytes 213024 | tf_op jit(solution)/shard_map/ppermute | solution.py:36
  96.4 23.2 %shard_map.241 = (bf16[512,512]{1,0:T(8,128)(2,1)}, bf16[512,512]{1,0:T(8,128)(2,1)}, bf16[512,512]{1,0:T(8,128)(2,1)}, f32[4,4,512]{2,1,0:T(4,128)}, bf16[4,768...) custom-call(bf16[4,512,512]{2,1,0:T(8,128)(2,1)} %nodes_ref.1, ...), custom_call_target="tpu_custom_call" | custom-call | tf_op jit(solution)/shard_map/pallas_call | solution.py:521
  119.7 41.2 %shard_map.243 = (f32[4,512,512]{2,1,0:T(8,128)}, f32[4,512,512]{2,1,0:T(8,128)}, bf16[4,512,512]{2,1,0:T(8,128)(2,1)}, f32[4,2,512]{2,1,0:T(2,128)}, bf16[4,512...) custom-call(s32[1]{0:T(128)} %bitcast.refs_6_.refs_0_, ...), custom_call_target="tpu_custom_call" | custom-call | tf_op jit(solution)/shard_map/pallas_call | solution.py:727
  162.0 10.3 %shard_map.247 = (f32[4,512,512]{2,1,0:T(8,128)}, bf16[4,64,512]{2,1,0:T(8,128)(2,1)S(1)}, bf16[4,64,512]{2,1,0:T(8,128)(2,1)S(1)}, bf16[4,64,512]{2,1,0:T(8,128...) custom-call(s32[1]{0:T(128)} %bitcast.refs_6_.refs_0_, ...), custom_call_target="tpu_custom_call" | custom-call | tf_op jit(solution)/shard_map/pallas_call | solution.py:966
  173.3 25.7 %shard_map.248 = (f32[4,512,512]{2,1,0:T(8,128)}, bf16[4,64,512]{2,1,0:T(8,128)(2,1)S(1)}, bf16[4,64,512]{2,1,0:T(8,128)(2,1)S(1)}, bf16[4,64,512]{2,1,0:T(8,128...) custom-call(s32[1]{0:T(128)} %bitcast.refs_6_.refs_0_, ...), custom_call_target="tpu_custom_call", output_to_operand_aliasing={{0}: (24, {}), {1}: (25, {}), {2}: (26, {}), {3}: (27, {}),... | custom-call | tf_op jit(solution)/shard_map/pallas_call | solution.py:966
  200.9 2.0 collective-permute-start.27
  203.6 3.2 %collective-permute-done.28.b0 = bf16[4,64,512]{2,1,0:T(8,128)(2,1)S(1)} collective-permute-done((bf16[4,64,512]{2,1,0:T(8,128)(2,1)S(1)}, bf16[4,64,512]{2,1,0:T(8,128)(2,1)S(1)}, u32[]{:S(2)}, u32[]{:S(2)}) %collective-permute-start.28) | collective-permute-done | bytes 262176 | tf_op jit(solution)/shard_map/ppermute | solution.py:32
  208.3 3.2 %collective-permute-done.29.b1 = bf16[4,64,512]{2,1,0:T(8,128)(2,1)S(1)} collective-permute-done((bf16[4,64,512]{2,1,0:T(8,128)(2,1)S(1)}, bf16[4,64,512]{2,1,0:T(8,128)(2,1)S(1)}, u32[]{:S(2)}, u32[]{:S(2)}) %collective-permute-start.29) | collective-permute-done | bytes 262176 | tf_op jit(solution)/shard_map/ppermute | solution.py:32
  211.5 23.8 %collective-permute-start.37 = (bf16[4,224,128]{2,1,0:T(8,128)(2,1)S(1)}, bf16[4,224,128]{2,1,0:T(8,128)(2,1)S(1)}, u32[]{:S(2)}, u32[]{:S(2)}) collective-permute-start(bf16[4,224,128]{2,1,0:T(8,128)(2,1)S(1)} %get-tuple-element.142), channel_id=1, source_target_pairs={{0,4},{1,5},{2,6},{3,7},{4,0},{5,1},{6,2},{7,3},{8,12},{9,13},{10,... | collective-permute-start | bytes 688136 | tf_op jit(solution)/shard_map/ppermute | solution.py:36
  239.3 2.5 collective-permute-start.32
  241.8 4.2 %collective-permute-start.33 = (bf16[1,592,128]{2,1,0:T(8,128)(2,1)S(1)}, bf16[1,592,128]{2,1,0:T(8,128)(2,1)}, u32[]{:S(2)}, u32[]{:S(2)}) collective-permute-start(bf16[1,592,128]{2,1,0:T(8,128)(2,1)S(1)} %get-tuple-element.136), channel_id=1, source_target_pairs={{0,16},{1,17},{2,18},{3,19},{4,20},{5,21},{6,22},{7,23},{8,24},{9,... | collective-permute-start | bytes 454664 | tf_op jit(solution)/shard_map/ppermute | solution.py:36
  249.0 4.0 %collective-permute-start.39 = (bf16[1,224,128]{2,1,0:T(8,128)(2,1)}, bf16[1,224,128]{2,1,0:T(8,128)(2,1)}, u32[]{:S(2)}, u32[]{:S(2)}) collective-permute-start(bf16[1,224,128]{2,1,0:T(8,128)(2,1)} %get-tuple-element.145), channel_id=1, source_target_pairs={{0,8},{1,9},{2,10},{3,11},{4,12},{5,13},{6,14},{7,15},{8,0},{9,1},... | collective-permute-start | bytes 172040 | tf_op jit(solution)/shard_map/ppermute | solution.py:36
  254.7 3.0 %collective-permute-done.32.refs_2_ = bf16[1,592,128]{2,1,0:T(8,128)(2,1)S(1)} collective-permute-done((bf16[1,592,128]{2,1,0:T(8,128)(2,1)S(1)}, bf16[1,592,128]{2,1,0:T(8,128)(2,1)S(1)}, u32[]{:S(2)}, u32[]{:S(2)}) %collective-permute-start.32) | collective-permute-done | bytes 151584 | tf_op jit(solution)/shard_map/ppermute | solution.py:36
  258.4 3.1 %collective-permute-start.41 = (bf16[1,224,128]{2,1,0:T(8,128)(2,1)S(1)}, bf16[1,224,128]{2,1,0:T(8,128)(2,1)}, u32[]{:S(2)}, u32[]{:S(2)}) collective-permute-start(bf16[1,224,128]{2,1,0:T(8,128)(2,1)S(1)} %get-tuple-element.147), channel_id=1, source_target_pairs={{0,24},{1,25},{2,26},{3,27},{4,28},{5,29},{6,30},{7,31},{8,16},{9,... | collective-permute-start | bytes 172040 | tf_op jit(solution)/shard_map/ppermute | solution.py:36
  261.6 2.2 copy-done.1
  263.8 4.2 %shard_map.249 = f32[4,512,512]{2,1,0:T(8,128)} custom-call(bf16[4,512,512]{2,1,0:T(8,128)(2,1)S(1)} %copy-done, f32[4,512,512]{2,1,0:T(8,128)S(1)} %copy-done.1, bf16[4,64,512]{2,1,0:T(8,128)(2,1)S(1)} %collective-permute-done.28.b0, bf16[4,64,512]{2,1,0:T(8,128)(2,1)S(1)} %collective-permute-done.29.b1, ...), custom_call_target="tpu_custom_call" | custom-call | tf_op jit(solution)/shard_map/pallas_call | solution.py:1006
  268.0 3.4 %copy-done.2 = bf16[4,512,2048]{2,1,0:T(8,128)(2,1)S(1)} copy-done((bf16[4,512,2048]{2,1,0:T(8,128)(2,1)S(1)}, bf16[4,512,2048]{2,1,0:T(8,128)(2,1)}, u32[]{:S(2)}) %copy-start.2) | copy-done | bytes 8388632
  271.3 5.8 %shard_map.246 = bf16[4,512,512]{2,1,0:T(8,128)(2,1)} custom-call(bf16[4,512,2048]{2,1,0:T(8,128)(2,1)S(1)} %copy-done.2, bf16[2048,512]{1,0:T(8,128)(2,1)S(1)} %copy-done.18, f32[4,512,512]{2,1,0:T(8,128)S(1)} %copy-done.4), custom_call_target="tpu_custom_call" | custom-call | tf_op jit(solution)/shard_map/pallas_call | solution.py:757
  277.2 2.0 shard_map.252
  (144 shorter events, 30.1 us)
Async XLA Ops:
  4.8 14.5 %collective-permute-start.4 = (bf16[1,208,128]{2,1,0:T(8,128)(2,1)}, bf16[1,208,128]{2,1,0:T(8,128)(2,1)S(1)}, u32[]{:S(2)}, u32[]{:S(2)}) collective-permute-start(bf16[1,208,128]{2,1,0:T(8,128)(2,1)} %get-tuple-element.93.refs_0_), channel_id=1, source_target_pairs={{0,8},{1,9},{2,10},{3,11},{4,12},{5,13},{6,14},{7,15},{8,0},{9,1},... | collective-permute-start | bytes 159752 | tf_op jit(solution)/shard_map/ppermute | solution.py:36
  7.9 23.3 %collective-permute-start.14 = (bf16[1,592,128]{2,1,0:T(8,128)(2,1)}, bf16[1,592,128]{2,1,0:T(8,128)(2,1)S(1)}, u32[]{:S(2)}, u32[]{:S(2)}) collective-permute-start(bf16[1,592,128]{2,1,0:T(8,128)(2,1)} %get-tuple-element.96.refs_0_), channel_id=1, source_target_pairs={{0,8},{1,9},{2,10},{3,11},{4,12},{5,13},{6,14},{7,15},{8,0},{9,1},... | collective-permute-start | bytes 454664 | tf_op jit(solution)/shard_map/ppermute | solution.py:36
  13.7 37.4 %collective-permute-start = (bf16[4,64,512]{2,1,0:T(8,128)(2,1)}, bf16[4,64,512]{2,1,0:T(8,128)(2,1)S(1)}, u32[]{:S(2)}, u32[]{:S(2)}) collective-permute-start(bf16[4,64,512]{2,1,0:T(8,128)(2,1)} %get-tuple-element.86), channel_id=1, source_target_pairs={{30,0},{0,2},{2,4},{4,6},{6,8},{8,10},{10,12},{12,14},{14,16},{16,... | collective-permute-start | bytes 786440 | tf_op jit(solution)/shard_map/ppermute | solution.py:32
  13.7 37.4 %collective-permute-start.1 = (bf16[4,64,512]{2,1,0:T(8,128)(2,1)}, bf16[4,64,512]{2,1,0:T(8,128)(2,1)S(1)}, u32[]{:S(2)}, u32[]{:S(2)}) collective-permute-start(bf16[4,64,512]{2,1,0:T(8,128)(2,1)} %get-tuple-element.88), channel_id=1, source_target_pairs={{2,0},{4,2},{6,4},{8,6},{10,8},{12,10},{14,12},{16,14},{18,16},{20... | collective-permute-start | bytes 786440 | tf_op jit(solution)/shard_map/ppermute | solution.py:32
  18.1 11.7 %collective-permute-start.5 = (bf16[1,208,128]{2,1,0:T(8,128)(2,1)}, bf16[1,208,128]{2,1,0:T(8,128)(2,1)S(1)}, u32[]{:S(2)}, u32[]{:S(2)}) collective-permute-start(bf16[1,208,128]{2,1,0:T(8,128)(2,1)} %get-tuple-element.93.refs_0_), channel_id=1, source_target_pairs={{0,16},{1,17},{2,18},{3,19},{4,20},{5,21},{6,22},{7,23},{8,24},{9,... | collective-permute-start | bytes 159752 | tf_op jit(solution)/shard_map/ppermute | solution.py:36
  19.3 12.9 %collective-permute-start.15 = (bf16[1,592,128]{2,1,0:T(8,128)(2,1)}, bf16[1,592,128]{2,1,0:T(8,128)(2,1)S(1)}, u32[]{:S(2)}, u32[]{:S(2)}) collective-permute-start(bf16[1,592,128]{2,1,0:T(8,128)(2,1)} %get-tuple-element.96.refs_0_), channel_id=1, source_target_pairs={{0,16},{1,17},{2,18},{3,19},{4,20},{5,21},{6,22},{7,23},{8,24},{9,... | collective-permute-start | bytes 454664 | tf_op jit(solution)/shard_map/ppermute | solution.py:36
  31.3 21.8 %collective-permute-start.2 = (bf16[4,64,512]{2,1,0:T(8,128)(2,1)}, bf16[4,64,512]{2,1,0:T(8,128)(2,1)S(1)}, u32[]{:S(2)}, u32[]{:S(2)}) collective-permute-start(bf16[4,64,512]{2,1,0:T(8,128)(2,1)} %get-tuple-element.90), channel_id=1, source_target_pairs={{24,0},{26,2},{28,4},{30,6},{0,8},{2,10},{4,12},{6,14},{8,16},{10,... | collective-permute-start | bytes 786440 | tf_op jit(solution)/shard_map/ppermute | solution.py:32
  32.2 22.5 %collective-permute-start.3 = (bf16[4,64,512]{2,1,0:T(8,128)(2,1)}, bf16[4,64,512]{2,1,0:T(8,128)(2,1)S(1)}, u32[]{:S(2)}, u32[]{:S(2)}) collective-permute-start(bf16[4,64,512]{2,1,0:T(8,128)(2,1)} %get-tuple-element.92), channel_id=1, source_target_pairs={{8,0},{10,2},{12,4},{14,6},{16,8},{18,10},{20,12},{22,14},{24,16},... | collective-permute-start | bytes 786440 | tf_op jit(solution)/shard_map/ppermute | solution.py:32
  49.6 40.3 %collective-permute-start.17 = (bf16[4,592,128]{2,1,0:T(8,128)(2,1)S(1)}, bf16[4,592,128]{2,1,0:T(8,128)(2,1)S(1)}, u32[]{:S(2)}, u32[]{:S(2)}) collective-permute-start(bf16[4,592,128]{2,1,0:T(8,128)(2,1)S(1)} %shard_map.242.refs_5_), channel_id=1, source_target_pairs={{0,1},{1,0},{2,3},{3,2},{4,5},{5,4},{6,7},{7,6},{8,9},{9,8},{10,11... | collective-permute-start | bytes 1818632 | tf_op jit(solution)/shard_map/ppermute | solution.py:36
  51.1 38.8 %collective-permute-start.18 = (bf16[4,592,128]{2,1,0:T(8,128)(2,1)S(1)}, bf16[4,592,128]{2,1,0:T(8,128)(2,1)S(1)}, u32[]{:S(2)}, u32[]{:S(2)}) collective-permute-start(bf16[4,592,128]{2,1,0:T(8,128)(2,1)S(1)} %shard_map.242.refs_5_), channel_id=1, source_target_pairs={{0,4},{1,5},{2,6},{3,7},{4,0},{5,1},{6,2},{7,3},{8,12},{9,13},{10,... | collective-permute-start | bytes 1818632 | tf_op jit(solution)/shard_map/ppermute | solution.py:36
  51.1 39.2 %collective-permute-start.19 = (bf16[4,592,128]{2,1,0:T(8,128)(2,1)S(1)}, bf16[4,592,128]{2,1,0:T(8,128)(2,1)}, u32[]{:S(2)}, u32[]{:S(2)}) collective-permute-start(bf16[4,592,128]{2,1,0:T(8,128)(2,1)S(1)} %shard_map.242.refs_5_), channel_id=1, source_target_pairs={{0,5},{1,4},{2,7},{3,6},{4,1},{5,0},{6,3},{7,2},{8,13},{9,12},{10,... | collective-permute-start | bytes 1818632 | tf_op jit(solution)/shard_map/ppermute | solution.py:36
  53.1 29.3 %collective-permute-start.7 = (bf16[4,208,128]{2,1,0:T(8,128)(2,1)S(1)}, bf16[4,208,128]{2,1,0:T(8,128)(2,1)S(1)}, u32[]{:S(2)}, u32[]{:S(2)}) collective-permute-start(bf16[4,208,128]{2,1,0:T(8,128)(2,1)S(1)} %shard_map.240.refs_8_), channel_id=1, source_target_pairs={{0,1},{1,0},{2,3},{3,2},{4,5},{5,4},{6,7},{7,6},{8,9},{9,8},{10,11... | collective-permute-start | bytes 638984 | tf_op jit(solution)/shard_map/ppermute | solution.py:36
  54.7 29.8 %collective-permute-start.8 = (bf16[4,208,128]{2,1,0:T(8,128)(2,1)S(1)}, bf16[4,208,128]{2,1,0:T(8,128)(2,1)S(1)}, u32[]{:S(2)}, u32[]{:S(2)}) collective-permute-start(bf16[4,208,128]{2,1,0:T(8,128)(2,1)S(1)} %shard_map.240.refs_8_), channel_id=1, source_target_pairs={{0,4},{1,5},{2,6},{3,7},{4,0},{5,1},{6,2},{7,3},{8,12},{9,13},{10,... | collective-permute-start | bytes 638984 | tf_op jit(solution)/shard_map/ppermute | solution.py:36
  89.3 30.3 %collective-permute-start.20 = (bf16[4,592,128]{2,1,0:T(8,128)(2,1)S(1)}, bf16[4,592,128]{2,1,0:T(8,128)(2,1)}, u32[]{:S(2)}, u32[]{:S(2)}) collective-permute-start(bf16[4,592,128]{2,1,0:T(8,128)(2,1)S(1)} %shard_map.242.refs_5_), channel_id=1, source_target_pairs={{0,2},{1,3},{2,0},{3,1},{4,6},{5,7},{6,4},{7,5},{8,10},{9,11},{10,... | collective-permute-start | bytes 1818632 | tf_op jit(solution)/shard_map/ppermute | solution.py:36
  89.8 29.8 %collective-permute-start.21 = (bf16[4,592,128]{2,1,0:T(8,128)(2,1)S(1)}, bf16[4,592,128]{2,1,0:T(8,128)(2,1)}, u32[]{:S(2)}, u32[]{:S(2)}) collective-permute-start(bf16[4,592,128]{2,1,0:T(8,128)(2,1)S(1)} %collective-permute-done.17.refs_6_), channel_id=1, source_target_pairs={{0,2},{1,3},{2,0},{3,1},{4,6},{5,7},{6,4},{7,5},{8,10},{9,11},{10,... | collective-permute-start | bytes 1818632 | tf_op jit(solution)/shard_map/ppermute | solution.py:36
  89.9 29.7 %collective-permute-start.22 = (bf16[4,592,128]{2,1,0:T(8,128)(2,1)S(1)}, bf16[4,592,128]{2,1,0:T(8,128)(2,1)}, u32[]{:S(2)}, u32[]{:S(2)}) collective-permute-start(bf16[4,592,128]{2,1,0:T(8,128)(2,1)S(1)} %collective-permute-done.18.refs_7_), channel_id=1, source_target_pairs={{0,2},{1,3},{2,0},{3,1},{4,6},{5,7},{6,4},{7,5},{8,10},{9,11},{10,... | collective-permute-start | bytes 1818632 | tf_op jit(solution)/shard_map/ppermute | solution.py:36
  90.3 29.3 %collective-permute-start.23 = (bf16[4,592,128]{2,1,0:T(8,128)(2,1)}, bf16[4,592,128]{2,1,0:T(8,128)(2,1)}, u32[]{:S(2)}, u32[]{:S(2)}) collective-permute-start(bf16[4,592,128]{2,1,0:T(8,128)(2,1)} %collective-permute-done.19.refs_8_), channel_id=1, source_target_pairs={{0,2},{1,3},{2,0},{3,1},{4,6},{5,7},{6,4},{7,5},{8,10},{9,11},{10,... | collective-permute-start | bytes 1818632 | tf_op jit(solution)/shard_map/ppermute | solution.py:36
  160.9 11.4 %collective-permute-start.24 = (bf16[16,592,128]{2,1,0:T(8,128)(2,1)}, bf16[16,592,128]{2,1,0:T(8,128)(2,1)S(1)}, u32[]{:S(2)}, u32[]{:S(2)}) collective-permute-start(bf16[16,592,128]{2,1,0:T(8,128)(2,1)} %get-tuple-element.101), channel_id=1, source_target_pairs={{0,2},{1,3},{2,0},{3,1},{4,6},{5,7},{6,4},{7,5},{8,10},{9,11},{10,... | collective-permute-start | bytes 7274504 | tf_op jit(solution)/shard_map/ppermute | solution.py:36
  199.4 35.9 %collective-permute-start.25 = (bf16[4,592,128]{2,1,0:T(8,128)(2,1)S(1)}, bf16[4,592,128]{2,1,0:T(8,128)(2,1)S(1)}, u32[]{:S(2)}, u32[]{:S(2)}) collective-permute-start(bf16[4,592,128]{2,1,0:T(8,128)(2,1)S(1)} %get-tuple-element.103), channel_id=1, source_target_pairs={{0,1},{1,0},{2,3},{3,2},{4,5},{5,4},{6,7},{7,6},{8,9},{9,8},{10,11... | collective-permute-start | bytes 1818632 | tf_op jit(solution)/shard_map/ppermute | solution.py:36
  200.9 35.2 %collective-permute-start.26 = (bf16[4,592,128]{2,1,0:T(8,128)(2,1)S(1)}, bf16[4,592,128]{2,1,0:T(8,128)(2,1)S(1)}, u32[]{:S(2)}, u32[]{:S(2)}) collective-permute-start(bf16[4,592,128]{2,1,0:T(8,128)(2,1)S(1)} %get-tuple-element.104), channel_id=1, source_target_pairs={{0,4},{1,5},{2,6},{3,7},{4,0},{5,1},{6,2},{7,3},{8,12},{9,13},{10,... | collective-permute-start | bytes 1818632 | tf_op jit(solution)/shard_map/ppermute | solution.py:36
  200.9 36.5 %collective-permute-start.27 = (bf16[4,592,128]{2,1,0:T(8,128)(2,1)S(1)}, bf16[4,592,128]{2,1,0:T(8,128)(2,1)S(1)}, u32[]{:S(2)}, u32[]{:S(2)}) collective-permute-start(bf16[4,592,128]{2,1,0:T(8,128)(2,1)S(1)} %get-tuple-element.105), channel_id=1, source_target_pairs={{0,5},{1,4},{2,7},{3,6},{4,1},{5,0},{6,3},{7,2},{8,13},{9,12},{10,... | collective-permute-start | bytes 1818632 | tf_op jit(solution)/shard_map/ppermute | solution.py:36
  206.8 32.5 %collective-permute-start.36 = (bf16[4,224,128]{2,1,0:T(8,128)(2,1)S(1)}, bf16[4,224,128]{2,1,0:T(8,128)(2,1)S(1)}, u32[]{:S(2)}, u32[]{:S(2)}) collective-permute-start(bf16[4,224,128]{2,1,0:T(8,128)(2,1)S(1)} %get-tuple-element.141), channel_id=1, source_target_pairs={{0,1},{1,0},{2,3},{3,2},{4,5},{5,4},{6,7},{7,6},{8,9},{9,8},{10,11... | collective-permute-start | bytes 688136 | tf_op jit(solution)/shard_map/ppermute | solution.py:36
  211.5 30.3 %collective-permute-start.37 = (bf16[4,224,128]{2,1,0:T(8,128)(2,1)S(1)}, bf16[4,224,128]{2,1,0:T(8,128)(2,1)S(1)}, u32[]{:S(2)}, u32[]{:S(2)}) collective-permute-start(bf16[4,224,128]{2,1,0:T(8,128)(2,1)S(1)} %get-tuple-element.142), channel_id=1, source_target_pairs={{0,4},{1,5},{2,6},{3,7},{4,0},{5,1},{6,2},{7,3},{8,12},{9,13},{10,... | collective-permute-start | bytes 688136 | tf_op jit(solution)/shard_map/ppermute | solution.py:36
  235.3 11.0 %collective-permute-start.38 = (bf16[4,224,128]{2,1,0:T(8,128)(2,1)S(1)}, bf16[4,224,128]{2,1,0:T(8,128)(2,1)S(1)}, u32[]{:S(2)}, u32[]{:S(2)}) collective-permute-start(bf16[4,224,128]{2,1,0:T(8,128)(2,1)S(1)} %get-tuple-element.143), channel_id=1, source_target_pairs={{0,5},{1,4},{2,7},{3,6},{4,1},{5,0},{6,3},{7,2},{8,13},{9,12},{10,... | collective-permute-start | bytes 688136 | tf_op jit(solution)/shard_map/ppermute | solution.py:36
  236.1 12.9 %collective-permute-start.30 = (bf16[4,64,512]{2,1,0:T(8,128)(2,1)S(1)}, bf16[4,64,512]{2,1,0:T(8,128)(2,1)S(1)}, u32[]{:S(2)}, u32[]{:S(2)}) collective-permute-start(bf16[4,64,512]{2,1,0:T(8,128)(2,1)S(1)} %get-tuple-element.133), channel_id=1, source_target_pairs={{8,0},{10,2},{12,4},{14,6},{16,8},{18,10},{20,12},{22,14},{24,16},... | collective-permute-start | bytes 786440 | tf_op jit(solution)/shard_map/ppermute | solution.py:32
  237.4 17.3 %collective-permute-start.31 = (bf16[4,64,512]{2,1,0:T(8,128)(2,1)S(1)}, bf16[4,64,512]{2,1,0:T(8,128)(2,1)S(1)}, u32[]{:S(2)}, u32[]{:S(2)}) collective-permute-start(bf16[4,64,512]{2,1,0:T(8,128)(2,1)S(1)} %get-tuple-element.134), channel_id=1, source_target_pairs={{24,0},{26,2},{28,4},{30,6},{0,8},{2,10},{4,12},{6,14},{8,16},{10,... | collective-permute-start | bytes 786440 | tf_op jit(solution)/shard_map/ppermute | solution.py:32
  239.3 18.4 %collective-permute-start.32 = (bf16[1,592,128]{2,1,0:T(8,128)(2,1)S(1)}, bf16[1,592,128]{2,1,0:T(8,128)(2,1)S(1)}, u32[]{:S(2)}, u32[]{:S(2)}) collective-permute-start(bf16[1,592,128]{2,1,0:T(8,128)(2,1)S(1)} %get-tuple-element.135), channel_id=1, source_target_pairs={{0,8},{1,9},{2,10},{3,11},{4,12},{5,13},{6,14},{7,15},{8,0},{9,1},... | collective-permute-start | bytes 454664 | tf_op jit(solution)/shard_map/ppermute | solution.py:36
  241.8 35.3 %collective-permute-start.33 = (bf16[1,592,128]{2,1,0:T(8,128)(2,1)S(1)}, bf16[1,592,128]{2,1,0:T(8,128)(2,1)}, u32[]{:S(2)}, u32[]{:S(2)}) collective-permute-start(bf16[1,592,128]{2,1,0:T(8,128)(2,1)S(1)} %get-tuple-element.136), channel_id=1, source_target_pairs={{0,16},{1,17},{2,18},{3,19},{4,20},{5,21},{6,22},{7,23},{8,24},{9,... | collective-permute-start | bytes 454664 | tf_op jit(solution)/shard_map/ppermute | solution.py:36
  246.3 30.8 %collective-permute-start.34 = (bf16[1,592,128]{2,1,0:T(8,128)(2,1)S(1)}, bf16[1,592,128]{2,1,0:T(8,128)(2,1)}, u32[]{:S(2)}, u32[]{:S(2)}) collective-permute-start(bf16[1,592,128]{2,1,0:T(8,128)(2,1)S(1)} %get-tuple-element.137), channel_id=1, source_target_pairs={{0,24},{1,25},{2,26},{3,27},{4,28},{5,29},{6,30},{7,31},{8,16},{9,... | collective-permute-start | bytes 454664 | tf_op jit(solution)/shard_map/ppermute | solution.py:36
  249.0 28.2 %collective-permute-start.39 = (bf16[1,224,128]{2,1,0:T(8,128)(2,1)}, bf16[1,224,128]{2,1,0:T(8,128)(2,1)}, u32[]{:S(2)}, u32[]{:S(2)}) collective-permute-start(bf16[1,224,128]{2,1,0:T(8,128)(2,1)} %get-tuple-element.145), channel_id=1, source_target_pairs={{0,8},{1,9},{2,10},{3,11},{4,12},{5,13},{6,14},{7,15},{8,0},{9,1},... | collective-permute-start | bytes 172040 | tf_op jit(solution)/shard_map/ppermute | solution.py:36
  254.7 22.5 %collective-permute-start.40 = (bf16[1,224,128]{2,1,0:T(8,128)(2,1)}, bf16[1,224,128]{2,1,0:T(8,128)(2,1)}, u32[]{:S(2)}, u32[]{:S(2)}) collective-permute-start(bf16[1,224,128]{2,1,0:T(8,128)(2,1)} %get-tuple-element.146), channel_id=1, source_target_pairs={{0,16},{1,17},{2,18},{3,19},{4,20},{5,21},{6,22},{7,23},{8,24},{9,... | collective-permute-start | bytes 172040 | tf_op jit(solution)/shard_map/ppermute | solution.py:36
  258.4 18.8 %collective-permute-start.41 = (bf16[1,224,128]{2,1,0:T(8,128)(2,1)S(1)}, bf16[1,224,128]{2,1,0:T(8,128)(2,1)}, u32[]{:S(2)}, u32[]{:S(2)}) collective-permute-start(bf16[1,224,128]{2,1,0:T(8,128)(2,1)S(1)} %get-tuple-element.147), channel_id=1, source_target_pairs={{0,24},{1,25},{2,26},{3,27},{4,28},{5,29},{6,30},{7,31},{8,16},{9,... | collective-permute-start | bytes 172040 | tf_op jit(solution)/shard_map/ppermute | solution.py:36
  (48 other events, 1031.5 us)

commit v2 on v1

--- a/solution.py
+++ b/solution.py
@@ -395,79 +395,107 @@
     return pl.BlockSpec(memory_space=pltpu.SMEM)
 
 
-def attend_kernel(*refs, pieces):
-    nodes_ref, h0, h1, h2, h3, bias_ref = refs[:6]
-    buffers, sems = refs[-7:-1], refs[-1]
-    act_buf, q_buf, k_buf, v_buf, p_buf, att_buf = buffers
-    s, last = pl.program_id(0), pl.num_programs(0) - 1
+def activate(rows, mod):
+    hat, _ = layer_normalize(rows.astype(F32))
+    return (hat * mod[0:1] + mod[1:2]).astype(BF16)
+
+
+def project_kernel(*refs, pieces):
+    nodes_ref = refs[0]
+    s = pl.program_id(0)
     if pieces:
-        me_ref, code_ref = refs[6:8]
-        shards = refs[8 : 8 + pieces]
-        wq_ref, wk_ref, wv_ref, mod_ref = refs[8 + pieces : 12 + pieces]
-        raw = refs[18 + pieces]
-        outs = refs[12 + pieces : 18 + pieces]
+        me_ref, code_ref = refs[1:3]
+        shards = refs[3 : 3 + pieces]
+        wq_ref, wk_ref, wv_ref, mod_ref = refs[3 + pieces : 7 + pieces]
+        act_ref, q_ref, k_ref, v_ref, raw = refs[7 + pieces :]
 
         @pl.when(s == 0)
         def _():
             place_first(me_ref, shards, code_ref, wq_ref, wk_ref, wv_ref, mod_ref, raw)
 
-        at = s
+        mod = mod_ref[s]
     else:
-        mod_ref, wq_ref, wk_ref, wv_ref = refs[6:10]
-        outs = refs[10:16]
-        at = 0
+        mod_ref, wq_ref, wk_ref, wv_ref, act_ref, q_ref, k_ref, v_ref = refs[1:]
+        mod = mod_ref[0]
+    act = activate(nodes_ref[0], mod)
+    act_ref[0] = act
+    q_ref[0] = product(act, wq_ref[...]).astype(BF16)
+    k_ref[0] = product(act, wk_ref[...]).astype(BF16)
+    v_ref[0] = product(act, wv_ref[...]).astype(BF16)
+
+
+def project(nodes, weights=None, shards=None):
+    samples, count, width = nodes.shape
+    tile = per_sample((count, width))
+    in_specs, args = [tile], [nodes]
+    out_specs, out_shape, scratch, first = [], [], [], 0
+    if shards is None:
+        wq, wk, wv, mod = weights
+        in_specs += [per_sample((4, width))] + [once((width, width))] * 3
+        args += [mod, wq, wk, wv]
+    else:
+        me, code, *pieces = shards
+        first = len(pieces)
+        in_specs += [smem(), once(code.shape)] + [once(x.shape) for x in pieces]
+        args += [me, code] + pieces
+        square = jax.ShapeDtypeStruct((width, width), BF16)
+        out_shape += [square] * 3 + [jax.ShapeDtypeStruct((samples, 4, width), F32)]
+        out_specs += [once(x.shape) for x in out_shape]
+        scratch = [pltpu.VMEM((samples, sum(x.shape[0] for x in pieces), 128), F32)]
+    return pl.pallas_call(
+        lambda *refs: project_kernel(*refs, pieces=first),
+        grid=(samples,),
+        in_specs=in_specs,
+        out_specs=out_specs + [tile] * 4,
+        out_shape=out_shape + [jax.ShapeDtypeStruct(nodes.shape, BF16)] * 4,
+        scratch_shapes=scratch,
+        compiler_params=params(60),
+    )(*args)
+
+
+def attend_kernel(*refs):
+    h0, h1, h2, h3, bias_ref, mod_ref, wk_ref, wv_ref, own_act, q_ref, own_k, own_v = refs[:12]
+    outs, buffers, sems = refs[12:17], refs[17:22], refs[22]
+    act_buf, k_buf, v_buf, p_buf, att_buf = buffers
+    s, last = pl.program_id(0), pl.num_programs(0) - 1
     heads_count = p_buf.shape[1]
     slot = lax.rem(s, 2)
 
     def copies(sample, place, arrays, some_heads):
         made = [(buffers[i].at[place], outs[i].at[sample], sems.at[place, i]) for i in arrays]
         for h in some_heads:
-            made.append((p_buf.at[place, h], outs[4].at[sample, h], sems.at[place, 6 + h]))
+            made.append((p_buf.at[place, h], outs[3].at[sample, h], sems.at[place, 5 + h]))
         return [pltpu.make_async_copy(*parts) for parts in made]
 
     def wait_for(sample, place):
-        for copy in copies(sample, place, (0, 1, 2, 3, 5), range(heads_count)):
+        for copy in copies(sample, place, (0, 1, 2, 4), range(heads_count)):
             copy.wait()
 
     @pl.when(s > 1)
     def _():
         wait_for(s - 2, slot)
 
-    count, _ = nodes_ref.shape[1:]
+    count = q_ref.shape[1]
     each = h0.shape[1]
-    scale, shift = mod_ref[at, 0:1, :], mod_ref[at, 1:2, :]
-
-    def activate(rows):
-        hat, _ = layer_normalize(rows.astype(F32))
-        return (hat * scale + shift).astype(BF16)
-
-    act_buf[slot, 0:count, :] = activate(nodes_ref[0])
+    for buf, own in ((act_buf, own_act), (k_buf, own_k), (v_buf, own_v)):
+        buf[slot, 0:count, :] = own[0]
     for d, ref in enumerate((h0, h1, h2, h3)):
         begin = count + d * each
-        act_buf[slot, begin : begin + each, :] = activate(ref[0])
-    act = act_buf[slot]
-    for copy in copies(s, slot, (0,), ()):
+        act_buf[slot, begin : begin + each, :] = activate(ref[0], mod_ref[0])
+    far = act_buf[slot, count:, :]
+    k_buf[slot, count:, :] = product(far, wk_ref[...]).astype(BF16)
+    v_buf[slot, count:, :] = product(far, wv_ref[...]).astype(BF16)
+    for copy in copies(s, slot, (0, 1, 2), ()):
         copy.start()
     factor = math.log2(math.e) * HEAD ** (-0.5)
     heads = [slice(h * HEAD, (h + 1) * HEAD) for h in range(heads_count)]
 
-    def project(h):
-        if h % 2 or h >= heads_count:
-            return
-        cols = slice(h * HEAD, min(h + 2, heads_count) * HEAD)
-        q_buf[slot, :, cols] = product(act[0:count], wq_ref[:, cols]).astype(BF16)
-        k_buf[slot, :, cols] = product(act, wk_ref[:, cols]).astype(BF16)
-        v_buf[slot, :, cols] = product(act, wv_ref[:, cols]).astype(BF16)
-
     def score(cols):
-        return product_t(k_buf[slot, :, cols], q_buf[slot, :, cols])
-
-    early = max(heads_count - 3, 0)
-    project(0)
+        return product_t(k_buf[slot, :, cols], q_ref[0, :, cols])
+
     following = score(heads[0])
     for h, cols in enumerate(heads):
         scores = following
-        project(h + 2)
         if h + 1 < heads_count:
             following = score(heads[h + 1])
         scores = scores * factor + bias_ref[...]
@@ -477,10 +505,10 @@
         probs = (expo * (1.0 / total)).astype(BF16)
         p_buf[slot, h] = probs
         att_buf[slot, :, cols] = product(v_buf[slot, :, cols].T, probs).T.astype(BF16)
-        if h == early:
-            for copy in copies(s, slot, (1, 2, 3), range(early + 1)):
+        if h == heads_count // 2 - 1:
+            for copy in copies(s, slot, (), range(h + 1)):
                 copy.start()
-    for copy in copies(s, slot, (5,), range(early + 1, heads_count)):
+    for copy in copies(s, slot, (4,), range(heads_count // 2, heads_count)):
         copy.start()
 
     @pl.when(s == last)
@@ -492,43 +520,27 @@
             wait_for(s - 1, 1 - slot)
 
 
-def attend(nodes, halos, bias, weights=None, shards=None):
-    samples, count, width = nodes.shape
+def attend(halos, bias, mod, wk, wv, own):
+    own_act, queries, own_k, own_v = own
+    samples, count, width = queries.shape
     table = bias.shape[0]
     heads = width // HEAD
     each = halos[0].shape[1]
-    square = jax.ShapeDtypeStruct((width, width), BF16)
-    mod_shape = jax.ShapeDtypeStruct((samples, 4, width), F32)
-    tile = per_sample
-    in_specs = [tile((count, width))] + [tile((each, width))] * 4 + [once((table, count))]
-    args = [nodes, *halos, bias]
-    out_specs, out_shape, scratch = [], [], []
-    if shards is None:
-        wq, wk, wv, mod = weights
-        in_specs += [tile((4, width))] + [once((width, width))] * 3
-        args += [mod, wq, wk, wv]
-    else:
-        me, code, *pieces = shards
-        in_specs += [smem(), once(code.shape)] + [once(x.shape) for x in pieces]
-        args += [me, code] + pieces
-        out_specs += [once((width, width))] * 3 + [once(mod_shape.shape)]
-        out_shape += [square] * 3 + [mod_shape]
-        devices = sum(x.shape[0] for x in pieces)
-        scratch = [pltpu.VMEM((samples, devices, 128), F32)]
-    tables = [(table, width), (count, width), (table, width), (table, width)]
-    tables += [(heads, table, count), (count, width)]
-    first = 0 if shards is None else len(shards) - 2
-    return pl.pallas_call(
-        lambda *refs: attend_kernel(*refs, pieces=first),
+    tables = [(table, width)] * 3 + [(heads, table, count), (count, width)]
+    act, keys, values, probs, attended = pl.pallas_call(
+        attend_kernel,
         grid=(samples,),
-        in_specs=in_specs,
-        out_specs=out_specs + [anywhere()] * len(tables),
-        out_shape=out_shape + [jax.ShapeDtypeStruct((samples,) + t, BF16) for t in tables],
-        scratch_shapes=scratch
-        + [pltpu.VMEM((2,) + t, BF16) for t in tables]
-        + [pltpu.SemaphoreType.DMA((2, 6 + heads))],
+        in_specs=[per_sample((each, width))] * 4
+        + [once((table, count)), per_sample((4, width))]
+        + [once((width, width))] * 2
+        + [per_sample((count, width))] * 4,
+        out_specs=[anywhere()] * len(tables),
+        out_shape=[jax.ShapeDtypeStruct((samples,) + t, BF16) for t in tables],
+        scratch_shapes=[pltpu.VMEM((2,) + t, BF16) for t in tables]
+        + [pltpu.SemaphoreType.DMA((2, 5 + heads))],
         compiler_params=params(60),
-    )(*args)
+    )(*halos, bias, mod, wk, wv, own_act, queries, own_k, own_v)
+    return [act, queries, keys, values, probs], attended
 
 
 def feed_kernel(*refs, shards):
@@ -1077,11 +1089,10 @@
     held = join([first] + far)
     low_first = [held] + swaps([held] * 3, plane)
     high_first = cores(low_first)
+    wq, wk, wv, mod, *own = project(nodes, shards=[me, noise_code] + low_first + high_first)
     held_second = join([second] + far_second)
     low_second = [held_second] + swaps([held_second] * 3, plane)
-    wq, wk, wv, mod, *saved, attended = attend(
-        nodes, halos, bias, shards=[me, noise_code] + low_first + high_first
-    )
+    saved, attended = attend(halos, bias, mod, wk, wv, own)
     high_second = cores(low_second)
     part, gmid, gatt, gmod, hid, down_whole, low_feed, high_feed = feed(
         me,
@@ -1159,7 +1170,8 @@
     sends = begin(nodes, send_rows)
     halos = [from_behind(block, offset) for block, offset in zip(sends, offsets)]
     (wq, wk, wv, mod), weights = gather_plain(*first, *second)
-    *saved, attended = attend(nodes, halos, bias, weights=(wq, wk, wv, mod))
+    own = project(nodes, weights=(wq, wk, wv, mod))
+    saved, attended = attend(halos, bias, mod, wk, wv, own)
     part, gmid, gatt, gmod, hid, *sums = feed(
         me, nodes, attended, cotangent, mod, hidden, devices, weights=weights
     )

time: 280 us -> 283 us (1.011)
  Pallas kernels: 122 us -> 127 us
  waiting for transfers between devices: 73 us -> 70 us
    ppermute x34, starting transfers between devices: 60.9 us -> 54.4 us  [swap(): return lax.ppermute(block, AXES, [(i, i ^ bits) for i in range(devices)])]
    ppermute x8, starting transfers between devices: 10.8 us -> 16.8 us  [from_behind(): lax.ppermute(block, 'patch', [((i - distance) % count, i) for i in range(...]
    pallas_call x1 -> x2, Pallas kernels: 23.2 us -> 28 us  [the longest x1 18.6 us: attend(): pl.pallas_call(attend_kernel, grid=(samples,), in_specs=[per_sample((each...]
    ppermute x34, waiting for transfers between devices: 64.7 us -> 60.4 us  [swap(): return lax.ppermute(block, AXES, [(i, i ^ bits) for i in range(devices)])]
    unnamed x76 -> x80, local copies, waits for them, and re-layouts: 11.4 us -> 13.1 us
  transfers between devices with their start and end apart: 42 -> 42, of which waited for: 15 -> 14; matrix products, arithmetic and copies ran while one was open for 0% -> 0% of each run, Pallas kernels for 17% -> 19%
where the time goes in v2:
time: 283 us
  Pallas kernels  127 us (45%)
  starting transfers between devices  71.2 us (25%)
  waiting for transfers between devices  70 us (25%)
  local copies, waits for them, and re-layouts  13.2 us (5%)
    ppermute x34, waiting for transfers between devices, swap(): return lax.ppermute(block, AXES, [(i, i ^ bits) for i in range(devices)])  60.4 us
    ppermute x34, starting transfers between devices, swap(): return lax.ppermute(block, AXES, [(i, i ^ bits) for i in range(devices)])  54.4 us
    pallas_call x1, Pallas kernels, feed(): pl.pallas_call(lambda *refs: feed_kernel(*refs, shards=len(shards or ()))...  41.2 us
    pallas_call x2, Pallas kernels, attend_back(): pl.pallas_call(lambda *refs: attend_back_kernel(*refs, started=bool(carri...  36 us
    pallas_call x1, Pallas kernels, attend(): pl.pallas_call(attend_kernel, grid=(samples,), in_specs=[per_sample((each...  18.6 us
    ppermute x8, starting transfers between devices, from_behind(): lax.ppermute(block, 'patch', [((i - distance) % count, i) for i in range(...  16.8 us
    unnamed x80, local copies, waits for them, and re-layouts  13.1 us
    ppermute x8, waiting for transfers between devices, from_behind(): lax.ppermute(block, 'patch', [((i - distance) % count, i) for i in range(...  9.68 us
  transfers between devices with their start and end apart: 42, of which 14 were waited for; matrix products, arithmetic and copies ran while one was open for 0% of the time, Pallas kernels for 19%

profile of v2, /device:TPU:0, one launch (start us, length us, event | category | flops | bytes accessed | tf_op | source)
XLA Modules:
  0.0 282.6 jit_solution(8315669703057802879)
XLA Ops:
  0.6 4.2 %shard_map.238 = (bf16[4,64,512]{2,1,0:T(8,128)(2,1)}, bf16[4,64,512]{2,1,0:T(8,128)(2,1)}, bf16[4,64,512]{2,1,0:T(8,128)(2,1)}, bf16[4,64,512]{2,1,0:T(8,128)(2...) custom-call(bf16[4,512,512]{2,1,0:T(8,128)(2,1)} %nodes_ref.1, s32[4,64]{1,0:T(4,128)} %refs_1_.4, ...), custom_call_target="tpu_custom_call" | custom-call | tf_op jit(solution)/shard_map/pallas_call | solution.py:205
  4.8 3.1 %collective-permute-start.14 = (bf16[1,592,128]{2,1,0:T(8,128)(2,1)}, bf16[1,592,128]{2,1,0:T(8,128)(2,1)S(1)}, u32[]{:S(2)}, u32[]{:S(2)}) collective-permute-start(bf16[1,592,128]{2,1,0:T(8,128)(2,1)} %get-tuple-element.105.refs_0_), channel_id=1, source_target_pairs={{0,8},{1,9},{2,10},{3,11},{4,12},{5,13},{6,14},{7,15},{8,0},{9,1},... | collective-permute-start | bytes 454664 | tf_op jit(solution)/shard_map/ppermute | solution.py:36
  8.7 3.7 %shard_map.239.refs_4_ = f32[768,512]{1,0:T(8,128)S(1)} custom-call(s32[16,512]{1,0:T(8,128)S(1)} %bitcast.8), custom_call_target="tpu_custom_call" | custom-call | tf_op jit(solution)/shard_map/pallas_call | solution.py:143
  13.6 4.4 %collective-permute-start.1 = (bf16[4,64,512]{2,1,0:T(8,128)(2,1)}, bf16[4,64,512]{2,1,0:T(8,128)(2,1)S(1)}, u32[]{:S(2)}, u32[]{:S(2)}) collective-permute-start(bf16[4,64,512]{2,1,0:T(8,128)(2,1)} %get-tuple-element.91), channel_id=1, source_target_pairs={{2,0},{4,2},{6,4},{8,6},{10,8},{12,10},{14,12},{16,14},{18,16},{20... | collective-permute-start | bytes 786440 | tf_op jit(solution)/shard_map/ppermute | solution.py:32
  20.6 7.7 %collective-permute-done.5.refs_2_ = bf16[1,208,128]{2,1,0:T(8,128)(2,1)S(1)} collective-permute-done((bf16[1,208,128]{2,1,0:T(8,128)(2,1)}, bf16[1,208,128]{2,1,0:T(8,128)(2,1)S(1)}, u32[]{:S(2)}, u32[]{:S(2)}) %collective-permute-start.5) | collective-permute-done | bytes 53280 | tf_op jit(solution)/shard_map/ppermute | solution.py:36
  28.3 3.2 %collective-permute-start.2 = (bf16[4,64,512]{2,1,0:T(8,128)(2,1)}, bf16[4,64,512]{2,1,0:T(8,128)(2,1)S(1)}, u32[]{:S(2)}, u32[]{:S(2)}) collective-permute-start(bf16[4,64,512]{2,1,0:T(8,128)(2,1)} %get-tuple-element.93), channel_id=1, source_target_pairs={{24,0},{26,2},{28,4},{30,6},{0,8},{2,10},{4,12},{6,14},{8,16},{10,... | collective-permute-start | bytes 786440 | tf_op jit(solution)/shard_map/ppermute | solution.py:32
  32.9 14.0 %collective-permute-done.15.refs_2_ = bf16[1,592,128]{2,1,0:T(8,128)(2,1)S(1)} collective-permute-done((bf16[1,592,128]{2,1,0:T(8,128)(2,1)}, bf16[1,592,128]{2,1,0:T(8,128)(2,1)S(1)}, u32[]{:S(2)}, u32[]{:S(2)}) %collective-permute-start.15) | collective-permute-done | bytes 151584 | tf_op jit(solution)/shard_map/ppermute | solution.py:36
  47.9 2.1 collective-permute-start.17
  52.1 2.9 %collective-permute-done.7.refs_4_ = bf16[4,208,128]{2,1,0:T(8,128)(2,1)S(1)} collective-permute-done((bf16[4,208,128]{2,1,0:T(8,128)(2,1)S(1)}, bf16[4,208,128]{2,1,0:T(8,128)(2,1)S(1)}, u32[]{:S(2)}, u32[]{:S(2)}) %collective-permute-start.7) | collective-permute-done | bytes 213024 | tf_op jit(solution)/shard_map/ppermute | solution.py:36
  55.0 26.1 %collective-permute-done.8.refs_5_ = bf16[4,208,128]{2,1,0:T(8,128)(2,1)S(1)} collective-permute-done((bf16[4,208,128]{2,1,0:T(8,128)(2,1)S(1)}, bf16[4,208,128]{2,1,0:T(8,128)(2,1)S(1)}, u32[]{:S(2)}, u32[]{:S(2)}) %collective-permute-start.8) | collective-permute-done | bytes 213024 | tf_op jit(solution)/shard_map/ppermute | solution.py:36
  81.1 3.2 %collective-permute-done.9.refs_6_ = bf16[4,208,128]{2,1,0:T(8,128)(2,1)S(1)} collective-permute-done((bf16[4,208,128]{2,1,0:T(8,128)(2,1)S(1)}, bf16[4,208,128]{2,1,0:T(8,128)(2,1)S(1)}, u32[]{:S(2)}, u32[]{:S(2)}) %collective-permute-start.9) | collective-permute-done | bytes 213024 | tf_op jit(solution)/shard_map/ppermute | solution.py:36
  87.0 3.8 %collective-permute-done.13.refs_10_ = bf16[4,208,128]{2,1,0:T(8,128)(2,1)S(1)} collective-permute-done((bf16[4,208,128]{2,1,0:T(8,128)(2,1)S(1)}, bf16[4,208,128]{2,1,0:T(8,128)(2,1)S(1)}, u32[]{:S(2)}, u32[]{:S(2)}) %collective-permute-start.13) | collective-permute-done | bytes 213024 | tf_op jit(solution)/shard_map/ppermute | solution.py:36
  91.5 9.4 %shard_map.241 = (bf16[512,512]{1,0:T(8,128)(2,1)}, bf16[512,512]{1,0:T(8,128)(2,1)}, bf16[512,512]{1,0:T(8,128)(2,1)}, f32[4,4,512]{2,1,0:T(4,128)}, bf16[4,512...) custom-call(bf16[4,512,512]{2,1,0:T(8,128)(2,1)} %nodes_ref.1, ...), custom_call_target="tpu_custom_call" | custom-call | tf_op jit(solution)/shard_map/pallas_call | solution.py:445
  102.0 18.6 %shard_map.242 = (bf16[4,768,512]{2,1,0:T(8,128)(2,1)}, bf16[4,768,512]{2,1,0:T(8,128)(2,1)}, bf16[4,768,512]{2,1,0:T(8,128)(2,1)}, bf16[4,4,768,512]{3,2,1,0:T(8,128)(2,1)}, bf16[4,512,512]{2,1,0:T(8,128)(2,1)}) custom-call(bf16[4,64,512]{2,1,0:T(8,128)(2,1)} %copy-done.9, bf16[4,64,512]{2,1,0:T(8,128)(2,1)} %copy-done.11, bf16[4,64,512]{2,1,0:T(8,128)(2,1)} %copy-done.13, ...), custom_call_target="tpu_custom_call" | custom-call | tf_op jit(solution)/shard_map/pallas_call | solution.py:530
  120.8 41.2 %shard_map.244 = (f32[4,512,512]{2,1,0:T(8,128)}, f32[4,512,512]{2,1,0:T(8,128)}, bf16[4,512,512]{2,1,0:T(8,128)(2,1)}, f32[4,2,512]{2,1,0:T(2,128)}, bf16[4,512...) custom-call(s32[1]{0:T(128)} %bitcast.refs_1_.refs_0_, ...), custom_call_target="tpu_custom_call" | custom-call | tf_op jit(solution)/shard_map/pallas_call | solution.py:739
  162.9 10.3 %shard_map.248 = (f32[4,512,512]{2,1,0:T(8,128)}, bf16[4,64,512]{2,1,0:T(8,128)(2,1)S(1)}, bf16[4,64,512]{2,1,0:T(8,128)(2,1)S(1)}, bf16[4,64,512]{2,1,0:T(8,128...) custom-call(s32[1]{0:T(128)} %bitcast.refs_1_.refs_0_, ...), custom_call_target="tpu_custom_call" | custom-call | tf_op jit(solution)/shard_map/pallas_call | solution.py:978
  174.2 25.7 %shard_map.249 = (f32[4,512,512]{2,1,0:T(8,128)}, bf16[4,64,512]{2,1,0:T(8,128)(2,1)S(1)}, bf16[4,64,512]{2,1,0:T(8,128)(2,1)S(1)}, bf16[4,64,512]{2,1,0:T(8,128...) custom-call(s32[1]{0:T(128)} %bitcast.refs_1_.refs_0_, ...), custom_call_target="tpu_custom_call", output_to_operand_aliasing={{0}: (24, {}), {1}: (25, {}), {2}: (26, {}), {3}: (27, {}),... | custom-call | tf_op jit(solution)/shard_map/pallas_call | solution.py:978
  200.8 1.7 collective-permute-start.26
  203.9 4.4 %collective-permute-start.28 = (bf16[4,64,512]{2,1,0:T(8,128)(2,1)S(1)}, bf16[4,64,512]{2,1,0:T(8,128)(2,1)S(1)}, u32[]{:S(2)}, u32[]{:S(2)}) collective-permute-start(bf16[4,64,512]{2,1,0:T(8,128)(2,1)S(1)} %get-tuple-element.137), channel_id=1, source_target_pairs={{2,0},{4,2},{6,4},{8,6},{10,8},{12,10},{14,12},{16,14},{18,16},{20... | collective-permute-start | bytes 786440 | tf_op jit(solution)/shard_map/ppermute | solution.py:32
  208.6 3.7 %collective-permute-done.28.b0 = bf16[4,64,512]{2,1,0:T(8,128)(2,1)S(1)} collective-permute-done((bf16[4,64,512]{2,1,0:T(8,128)(2,1)S(1)}, bf16[4,64,512]{2,1,0:T(8,128)(2,1)S(1)}, u32[]{:S(2)}, u32[]{:S(2)}) %collective-permute-start.28) | collective-permute-done | bytes 262176 | tf_op jit(solution)/shard_map/ppermute | solution.py:32
  212.9 4.0 %collective-permute-done.29.b1 = bf16[4,64,512]{2,1,0:T(8,128)(2,1)S(1)} collective-permute-done((bf16[4,64,512]{2,1,0:T(8,128)(2,1)S(1)}, bf16[4,64,512]{2,1,0:T(8,128)(2,1)S(1)}, u32[]{:S(2)}, u32[]{:S(2)}) %collective-permute-start.29) | collective-permute-done | bytes 262176 | tf_op jit(solution)/shard_map/ppermute | solution.py:32
  216.9 19.6 %collective-permute-start.37 = (bf16[4,224,128]{2,1,0:T(8,128)(2,1)S(1)}, bf16[4,224,128]{2,1,0:T(8,128)(2,1)S(1)}, u32[]{:S(2)}, u32[]{:S(2)}) collective-permute-start(bf16[4,224,128]{2,1,0:T(8,128)(2,1)S(1)} %get-tuple-element.148), channel_id=1, source_target_pairs={{0,4},{1,5},{2,6},{3,7},{4,0},{5,1},{6,2},{7,3},{8,12},{9,13},{10,... | collective-permute-start | bytes 688136 | tf_op jit(solution)/shard_map/ppermute | solution.py:36
  237.3 4.7 %collective-permute-start.30 = (bf16[4,64,512]{2,1,0:T(8,128)(2,1)S(1)}, bf16[4,64,512]{2,1,0:T(8,128)(2,1)S(1)}, u32[]{:S(2)}, u32[]{:S(2)}) collective-permute-start(bf16[4,64,512]{2,1,0:T(8,128)(2,1)S(1)} %get-tuple-element.139), channel_id=1, source_target_pairs={{8,0},{10,2},{12,4},{14,6},{16,8},{18,10},{20,12},{22,14},{24,16},... | collective-permute-start | bytes 786440 | tf_op jit(solution)/shard_map/ppermute | solution.py:32
  242.6 4.6 %collective-permute-start.33 = (bf16[1,592,128]{2,1,0:T(8,128)(2,1)S(1)}, bf16[1,592,128]{2,1,0:T(8,128)(2,1)}, u32[]{:S(2)}, u32[]{:S(2)}) collective-permute-start(bf16[1,592,128]{2,1,0:T(8,128)(2,1)S(1)} %get-tuple-element.142), channel_id=1, source_target_pairs={{0,16},{1,17},{2,18},{3,19},{4,20},{5,21},{6,22},{7,23},{8,24},{9,... | collective-permute-start | bytes 454664 | tf_op jit(solution)/shard_map/ppermute | solution.py:36
  248.2 4.5 %collective-permute-start.34 = (bf16[1,592,128]{2,1,0:T(8,128)(2,1)S(1)}, bf16[1,592,128]{2,1,0:T(8,128)(2,1)}, u32[]{:S(2)}, u32[]{:S(2)}) collective-permute-start(bf16[1,592,128]{2,1,0:T(8,128)(2,1)S(1)} %get-tuple-element.143), channel_id=1, source_target_pairs={{0,24},{1,25},{2,26},{3,27},{4,28},{5,29},{6,30},{7,31},{8,16},{9,... | collective-permute-start | bytes 454664 | tf_op jit(solution)/shard_map/ppermute | solution.py:36
  255.6 3.2 %collective-permute-start.40 = (bf16[1,224,128]{2,1,0:T(8,128)(2,1)}, bf16[1,224,128]{2,1,0:T(8,128)(2,1)}, u32[]{:S(2)}, u32[]{:S(2)}) collective-permute-start(bf16[1,224,128]{2,1,0:T(8,128)(2,1)} %get-tuple-element.152), channel_id=1, source_target_pairs={{0,16},{1,17},{2,18},{3,19},{4,20},{5,21},{6,22},{7,23},{8,24},{9,... | collective-permute-start | bytes 172040 | tf_op jit(solution)/shard_map/ppermute | solution.py:36
  259.9 4.8 %collective-permute-start.41 = (bf16[1,224,128]{2,1,0:T(8,128)(2,1)S(1)}, bf16[1,224,128]{2,1,0:T(8,128)(2,1)}, u32[]{:S(2)}, u32[]{:S(2)}) collective-permute-start(bf16[1,224,128]{2,1,0:T(8,128)(2,1)S(1)} %get-tuple-element.153), channel_id=1, source_target_pairs={{0,24},{1,25},{2,26},{3,27},{4,28},{5,29},{6,30},{7,31},{8,16},{9,... | collective-permute-start | bytes 172040 | tf_op jit(solution)/shard_map/ppermute | solution.py:36
  264.8 2.2 copy-done.1
  267.0 4.2 %shard_map.250 = f32[4,512,512]{2,1,0:T(8,128)} custom-call(bf16[4,512,512]{2,1,0:T(8,128)(2,1)S(1)} %copy-done, f32[4,512,512]{2,1,0:T(8,128)S(1)} %copy-done.1, bf16[4,64,512]{2,1,0:T(8,128)(2,1)S(1)} %collective-permute-done.28.b0, bf16[4,64,512]{2,1,0:T(8,128)(2,1)S(1)} %collective-permute-done.29.b1, ...), custom_call_target="tpu_custom_call" | custom-call | tf_op jit(solution)/shard_map/pallas_call | solution.py:1018
  271.2 3.4 %copy-done.2 = bf16[4,512,2048]{2,1,0:T(8,128)(2,1)S(1)} copy-done((bf16[4,512,2048]{2,1,0:T(8,128)(2,1)S(1)}, bf16[4,512,2048]{2,1,0:T(8,128)(2,1)}, u32[]{:S(2)}) %copy-start.2) | copy-done | bytes 8388632
  274.6 5.8 %shard_map.247 = bf16[4,512,512]{2,1,0:T(8,128)(2,1)} custom-call(bf16[4,512,2048]{2,1,0:T(8,128)(2,1)S(1)} %copy-done.2, bf16[2048,512]{1,0:T(8,128)(2,1)S(1)} %copy-done.18, f32[4,512,512]{2,1,0:T(8,128)S(1)} %copy-done.6), custom_call_target="tpu_custom_call" | custom-call | tf_op jit(solution)/shard_map/pallas_call | solution.py:769
  280.4 2.0 shard_map.253
  (149 shorter events, 24.8 us)
Async XLA Ops:
  4.8 26.7 %collective-permute-start.14 = (bf16[1,592,128]{2,1,0:T(8,128)(2,1)}, bf16[1,592,128]{2,1,0:T(8,128)(2,1)S(1)}, u32[]{:S(2)}, u32[]{:S(2)}) collective-permute-start(bf16[1,592,128]{2,1,0:T(8,128)(2,1)} %get-tuple-element.105.refs_0_), channel_id=1, source_target_pairs={{0,8},{1,9},{2,10},{3,11},{4,12},{5,13},{6,14},{7,15},{8,0},{9,1},... | collective-permute-start | bytes 454664 | tf_op jit(solution)/shard_map/ppermute | solution.py:36
  7.9 11.3 %collective-permute-start.4 = (bf16[1,208,128]{2,1,0:T(8,128)(2,1)}, bf16[1,208,128]{2,1,0:T(8,128)(2,1)S(1)}, u32[]{:S(2)}, u32[]{:S(2)}) collective-permute-start(bf16[1,208,128]{2,1,0:T(8,128)(2,1)} %get-tuple-element.96.refs_0_), channel_id=1, source_target_pairs={{0,8},{1,9},{2,10},{3,11},{4,12},{5,13},{6,14},{7,15},{8,0},{9,1},... | collective-permute-start | bytes 159752 | tf_op jit(solution)/shard_map/ppermute | solution.py:36
  13.6 36.3 %collective-permute-start = (bf16[4,64,512]{2,1,0:T(8,128)(2,1)}, bf16[4,64,512]{2,1,0:T(8,128)(2,1)S(1)}, u32[]{:S(2)}, u32[]{:S(2)}) collective-permute-start(bf16[4,64,512]{2,1,0:T(8,128)(2,1)} %get-tuple-element.89), channel_id=1, source_target_pairs={{30,0},{0,2},{2,4},{4,6},{6,8},{8,10},{10,12},{12,14},{14,16},{16,... | collective-permute-start | bytes 786440 | tf_op jit(solution)/shard_map/ppermute | solution.py:32
  13.6 36.3 %collective-permute-start.1 = (bf16[4,64,512]{2,1,0:T(8,128)(2,1)}, bf16[4,64,512]{2,1,0:T(8,128)(2,1)S(1)}, u32[]{:S(2)}, u32[]{:S(2)}) collective-permute-start(bf16[4,64,512]{2,1,0:T(8,128)(2,1)} %get-tuple-element.91), channel_id=1, source_target_pairs={{2,0},{4,2},{6,4},{8,6},{10,8},{12,10},{14,12},{16,14},{18,16},{20... | collective-permute-start | bytes 786440 | tf_op jit(solution)/shard_map/ppermute | solution.py:32
  28.3 18.6 %collective-permute-start.15 = (bf16[1,592,128]{2,1,0:T(8,128)(2,1)}, bf16[1,592,128]{2,1,0:T(8,128)(2,1)S(1)}, u32[]{:S(2)}, u32[]{:S(2)}) collective-permute-start(bf16[1,592,128]{2,1,0:T(8,128)(2,1)} %get-tuple-element.105.refs_0_), channel_id=1, source_target_pairs={{0,16},{1,17},{2,18},{3,19},{4,20},{5,21},{6,22},{7,23},{8,24},{9,... | collective-permute-start | bytes 454664 | tf_op jit(solution)/shard_map/ppermute | solution.py:36
  28.3 23.3 %collective-permute-start.2 = (bf16[4,64,512]{2,1,0:T(8,128)(2,1)}, bf16[4,64,512]{2,1,0:T(8,128)(2,1)S(1)}, u32[]{:S(2)}, u32[]{:S(2)}) collective-permute-start(bf16[4,64,512]{2,1,0:T(8,128)(2,1)} %get-tuple-element.93), channel_id=1, source_target_pairs={{24,0},{26,2},{28,4},{30,6},{0,8},{2,10},{4,12},{6,14},{8,16},{10,... | collective-permute-start | bytes 786440 | tf_op jit(solution)/shard_map/ppermute | solution.py:32
  31.5 15.4 %collective-permute-start.16 = (bf16[1,592,128]{2,1,0:T(8,128)(2,1)}, bf16[1,592,128]{2,1,0:T(8,128)(2,1)S(1)}, u32[]{:S(2)}, u32[]{:S(2)}) collective-permute-start(bf16[1,592,128]{2,1,0:T(8,128)(2,1)} %get-tuple-element.105.refs_0_), channel_id=1, source_target_pairs={{0,24},{1,25},{2,26},{3,27},{4,28},{5,29},{6,30},{7,31},{8,16},{9,... | collective-permute-start | bytes 454664 | tf_op jit(solution)/shard_map/ppermute | solution.py:36
  47.9 38.1 %collective-permute-start.17 = (bf16[4,592,128]{2,1,0:T(8,128)(2,1)S(1)}, bf16[4,592,128]{2,1,0:T(8,128)(2,1)S(1)}, u32[]{:S(2)}, u32[]{:S(2)}) collective-permute-start(bf16[4,592,128]{2,1,0:T(8,128)(2,1)S(1)} %shard_map.243.refs_5_), channel_id=1, source_target_pairs={{0,1},{1,0},{2,3},{3,2},{4,5},{5,4},{6,7},{7,6},{8,9},{9,8},{10,11... | collective-permute-start | bytes 1818632 | tf_op jit(solution)/shard_map/ppermute | solution.py:36
  49.9 36.4 %collective-permute-start.18 = (bf16[4,592,128]{2,1,0:T(8,128)(2,1)S(1)}, bf16[4,592,128]{2,1,0:T(8,128)(2,1)S(1)}, u32[]{:S(2)}, u32[]{:S(2)}) collective-permute-start(bf16[4,592,128]{2,1,0:T(8,128)(2,1)S(1)} %shard_map.243.refs_5_), channel_id=1, source_target_pairs={{0,4},{1,5},{2,6},{3,7},{4,0},{5,1},{6,2},{7,3},{8,12},{9,13},{10,... | collective-permute-start | bytes 1818632 | tf_op jit(solution)/shard_map/ppermute | solution.py:36
  50.0 36.5 %collective-permute-start.19 = (bf16[4,592,128]{2,1,0:T(8,128)(2,1)S(1)}, bf16[4,592,128]{2,1,0:T(8,128)(2,1)}, u32[]{:S(2)}, u32[]{:S(2)}) collective-permute-start(bf16[4,592,128]{2,1,0:T(8,128)(2,1)S(1)} %shard_map.243.refs_5_), channel_id=1, source_target_pairs={{0,5},{1,4},{2,7},{3,6},{4,1},{5,0},{6,3},{7,2},{8,13},{9,12},{10,... | collective-permute-start | bytes 1818632 | tf_op jit(solution)/shard_map/ppermute | solution.py:36
  51.5 29.6 %collective-permute-start.8 = (bf16[4,208,128]{2,1,0:T(8,128)(2,1)S(1)}, bf16[4,208,128]{2,1,0:T(8,128)(2,1)S(1)}, u32[]{:S(2)}, u32[]{:S(2)}) collective-permute-start(bf16[4,208,128]{2,1,0:T(8,128)(2,1)S(1)} %shard_map.240.refs_3_), channel_id=1, source_target_pairs={{0,4},{1,5},{2,6},{3,7},{4,0},{5,1},{6,2},{7,3},{8,12},{9,13},{10,... | collective-permute-start | bytes 638984 | tf_op jit(solution)/shard_map/ppermute | solution.py:36
  55.0 29.4 %collective-permute-start.9 = (bf16[4,208,128]{2,1,0:T(8,128)(2,1)S(1)}, bf16[4,208,128]{2,1,0:T(8,128)(2,1)S(1)}, u32[]{:S(2)}, u32[]{:S(2)}) collective-permute-start(bf16[4,208,128]{2,1,0:T(8,128)(2,1)S(1)} %shard_map.240.refs_3_), channel_id=1, source_target_pairs={{0,5},{1,4},{2,7},{3,6},{4,1},{5,0},{6,3},{7,2},{8,13},{9,12},{10,... | collective-permute-start | bytes 638984 | tf_op jit(solution)/shard_map/ppermute | solution.py:36
  85.8 34.8 %collective-permute-start.20 = (bf16[4,592,128]{2,1,0:T(8,128)(2,1)S(1)}, bf16[4,592,128]{2,1,0:T(8,128)(2,1)}, u32[]{:S(2)}, u32[]{:S(2)}) collective-permute-start(bf16[4,592,128]{2,1,0:T(8,128)(2,1)S(1)} %shard_map.243.refs_5_), channel_id=1, source_target_pairs={{0,2},{1,3},{2,0},{3,1},{4,6},{5,7},{6,4},{7,5},{8,10},{9,11},{10,... | collective-permute-start | bytes 1818632 | tf_op jit(solution)/shard_map/ppermute | solution.py:36
  86.0 34.6 %collective-permute-start.21 = (bf16[4,592,128]{2,1,0:T(8,128)(2,1)S(1)}, bf16[4,592,128]{2,1,0:T(8,128)(2,1)}, u32[]{:S(2)}, u32[]{:S(2)}) collective-permute-start(bf16[4,592,128]{2,1,0:T(8,128)(2,1)S(1)} %collective-permute-done.17.refs_6_), channel_id=1, source_target_pairs={{0,2},{1,3},{2,0},{3,1},{4,6},{5,7},{6,4},{7,5},{8,10},{9,11},{10,... | collective-permute-start | bytes 1818632 | tf_op jit(solution)/shard_map/ppermute | solution.py:36
  86.4 34.3 %collective-permute-start.22 = (bf16[4,592,128]{2,1,0:T(8,128)(2,1)S(1)}, bf16[4,592,128]{2,1,0:T(8,128)(2,1)}, u32[]{:S(2)}, u32[]{:S(2)}) collective-permute-start(bf16[4,592,128]{2,1,0:T(8,128)(2,1)S(1)} %collective-permute-done.18.refs_7_), channel_id=1, source_target_pairs={{0,2},{1,3},{2,0},{3,1},{4,6},{5,7},{6,4},{7,5},{8,10},{9,11},{10,... | collective-permute-start | bytes 1818632 | tf_op jit(solution)/shard_map/ppermute | solution.py:36
  86.5 34.1 %collective-permute-start.23 = (bf16[4,592,128]{2,1,0:T(8,128)(2,1)}, bf16[4,592,128]{2,1,0:T(8,128)(2,1)}, u32[]{:S(2)}, u32[]{:S(2)}) collective-permute-start(bf16[4,592,128]{2,1,0:T(8,128)(2,1)} %collective-permute-done.19.refs_8_), channel_id=1, source_target_pairs={{0,2},{1,3},{2,0},{3,1},{4,6},{5,7},{6,4},{7,5},{8,10},{9,11},{10,... | collective-permute-start | bytes 1818632 | tf_op jit(solution)/shard_map/ppermute | solution.py:36
  90.8 10.5 %collective-permute-start.3 = (bf16[4,64,512]{2,1,0:T(8,128)(2,1)}, bf16[4,64,512]{2,1,0:T(8,128)(2,1)S(1)}, u32[]{:S(2)}, u32[]{:S(2)}) collective-permute-start(bf16[4,64,512]{2,1,0:T(8,128)(2,1)} %get-tuple-element.95), channel_id=1, source_target_pairs={{8,0},{10,2},{12,4},{14,6},{16,8},{18,10},{20,12},{22,14},{24,16},... | collective-permute-start | bytes 786440 | tf_op jit(solution)/shard_map/ppermute | solution.py:32
  162.0 11.2 %collective-permute-start.24 = (bf16[16,592,128]{2,1,0:T(8,128)(2,1)}, bf16[16,592,128]{2,1,0:T(8,128)(2,1)S(1)}, u32[]{:S(2)}, u32[]{:S(2)}) collective-permute-start(bf16[16,592,128]{2,1,0:T(8,128)(2,1)} %get-tuple-element.110), channel_id=1, source_target_pairs={{0,2},{1,3},{2,0},{3,1},{4,6},{5,7},{6,4},{7,5},{8,10},{9,11},{10,... | collective-permute-start | bytes 7274504 | tf_op jit(solution)/shard_map/ppermute | solution.py:36
  200.4 36.1 %collective-permute-start.25 = (bf16[4,592,128]{2,1,0:T(8,128)(2,1)S(1)}, bf16[4,592,128]{2,1,0:T(8,128)(2,1)S(1)}, u32[]{:S(2)}, u32[]{:S(2)}) collective-permute-start(bf16[4,592,128]{2,1,0:T(8,128)(2,1)S(1)} %get-tuple-element.112), channel_id=1, source_target_pairs={{0,1},{1,0},{2,3},{3,2},{4,5},{5,4},{6,7},{7,6},{8,9},{9,8},{10,11... | collective-permute-start | bytes 1818632 | tf_op jit(solution)/shard_map/ppermute | solution.py:36
  200.8 36.5 %collective-permute-start.26 = (bf16[4,592,128]{2,1,0:T(8,128)(2,1)S(1)}, bf16[4,592,128]{2,1,0:T(8,128)(2,1)S(1)}, u32[]{:S(2)}, u32[]{:S(2)}) collective-permute-start(bf16[4,592,128]{2,1,0:T(8,128)(2,1)S(1)} %get-tuple-element.113), channel_id=1, source_target_pairs={{0,4},{1,5},{2,6},{3,7},{4,0},{5,1},{6,2},{7,3},{8,12},{9,13},{10,... | collective-permute-start | bytes 1818632 | tf_op jit(solution)/shard_map/ppermute | solution.py:36
  202.6 39.5 %collective-permute-start.27 = (bf16[4,592,128]{2,1,0:T(8,128)(2,1)S(1)}, bf16[4,592,128]{2,1,0:T(8,128)(2,1)S(1)}, u32[]{:S(2)}, u32[]{:S(2)}) collective-permute-start(bf16[4,592,128]{2,1,0:T(8,128)(2,1)S(1)} %get-tuple-element.114), channel_id=1, source_target_pairs={{0,5},{1,4},{2,7},{3,6},{4,1},{5,0},{6,3},{7,2},{8,13},{9,12},{10,... | collective-permute-start | bytes 1818632 | tf_op jit(solution)/shard_map/ppermute | solution.py:36
  212.2 30.1 %collective-permute-start.36 = (bf16[4,224,128]{2,1,0:T(8,128)(2,1)S(1)}, bf16[4,224,128]{2,1,0:T(8,128)(2,1)S(1)}, u32[]{:S(2)}, u32[]{:S(2)}) collective-permute-start(bf16[4,224,128]{2,1,0:T(8,128)(2,1)S(1)} %get-tuple-element.147), channel_id=1, source_target_pairs={{0,1},{1,0},{2,3},{3,2},{4,5},{5,4},{6,7},{7,6},{8,9},{9,8},{10,11... | collective-permute-start | bytes 688136 | tf_op jit(solution)/shard_map/ppermute | solution.py:36
  216.9 25.6 %collective-permute-start.37 = (bf16[4,224,128]{2,1,0:T(8,128)(2,1)S(1)}, bf16[4,224,128]{2,1,0:T(8,128)(2,1)S(1)}, u32[]{:S(2)}, u32[]{:S(2)}) collective-permute-start(bf16[4,224,128]{2,1,0:T(8,128)(2,1)S(1)} %get-tuple-element.148), channel_id=1, source_target_pairs={{0,4},{1,5},{2,6},{3,7},{4,0},{5,1},{6,2},{7,3},{8,12},{9,13},{10,... | collective-permute-start | bytes 688136 | tf_op jit(solution)/shard_map/ppermute | solution.py:36
  236.6 11.7 %collective-permute-start.38 = (bf16[4,224,128]{2,1,0:T(8,128)(2,1)S(1)}, bf16[4,224,128]{2,1,0:T(8,128)(2,1)S(1)}, u32[]{:S(2)}, u32[]{:S(2)}) collective-permute-start(bf16[4,224,128]{2,1,0:T(8,128)(2,1)S(1)} %get-tuple-element.149), channel_id=1, source_target_pairs={{0,5},{1,4},{2,7},{3,6},{4,1},{5,0},{6,3},{7,2},{8,13},{9,12},{10,... | collective-permute-start | bytes 688136 | tf_op jit(solution)/shard_map/ppermute | solution.py:36
  237.3 16.7 %collective-permute-start.30 = (bf16[4,64,512]{2,1,0:T(8,128)(2,1)S(1)}, bf16[4,64,512]{2,1,0:T(8,128)(2,1)S(1)}, u32[]{:S(2)}, u32[]{:S(2)}) collective-permute-start(bf16[4,64,512]{2,1,0:T(8,128)(2,1)S(1)} %get-tuple-element.139), channel_id=1, source_target_pairs={{8,0},{10,2},{12,4},{14,6},{16,8},{18,10},{20,12},{22,14},{24,16},... | collective-permute-start | bytes 786440 | tf_op jit(solution)/shard_map/ppermute | solution.py:32
  242.0 13.5 %collective-permute-start.31 = (bf16[4,64,512]{2,1,0:T(8,128)(2,1)S(1)}, bf16[4,64,512]{2,1,0:T(8,128)(2,1)S(1)}, u32[]{:S(2)}, u32[]{:S(2)}) collective-permute-start(bf16[4,64,512]{2,1,0:T(8,128)(2,1)S(1)} %get-tuple-element.140), channel_id=1, source_target_pairs={{24,0},{26,2},{28,4},{30,6},{0,8},{2,10},{4,12},{6,14},{8,16},{10,... | collective-permute-start | bytes 786440 | tf_op jit(solution)/shard_map/ppermute | solution.py:32
  242.4 16.9 %collective-permute-start.32 = (bf16[1,592,128]{2,1,0:T(8,128)(2,1)S(1)}, bf16[1,592,128]{2,1,0:T(8,128)(2,1)S(1)}, u32[]{:S(2)}, u32[]{:S(2)}) collective-permute-start(bf16[1,592,128]{2,1,0:T(8,128)(2,1)S(1)} %get-tuple-element.141), channel_id=1, source_target_pairs={{0,8},{1,9},{2,10},{3,11},{4,12},{5,13},{6,14},{7,15},{8,0},{9,1},... | collective-permute-start | bytes 454664 | tf_op jit(solution)/shard_map/ppermute | solution.py:36
  242.6 37.8 %collective-permute-start.33 = (bf16[1,592,128]{2,1,0:T(8,128)(2,1)S(1)}, bf16[1,592,128]{2,1,0:T(8,128)(2,1)}, u32[]{:S(2)}, u32[]{:S(2)}) collective-permute-start(bf16[1,592,128]{2,1,0:T(8,128)(2,1)S(1)} %get-tuple-element.142), channel_id=1, source_target_pairs={{0,16},{1,17},{2,18},{3,19},{4,20},{5,21},{6,22},{7,23},{8,24},{9,... | collective-permute-start | bytes 454664 | tf_op jit(solution)/shard_map/ppermute | solution.py:36
  248.2 32.1 %collective-permute-start.34 = (bf16[1,592,128]{2,1,0:T(8,128)(2,1)S(1)}, bf16[1,592,128]{2,1,0:T(8,128)(2,1)}, u32[]{:S(2)}, u32[]{:S(2)}) collective-permute-start(bf16[1,592,128]{2,1,0:T(8,128)(2,1)S(1)} %get-tuple-element.143), channel_id=1, source_target_pairs={{0,24},{1,25},{2,26},{3,27},{4,28},{5,29},{6,30},{7,31},{8,16},{9,... | collective-permute-start | bytes 454664 | tf_op jit(solution)/shard_map/ppermute | solution.py:36
  254.0 26.4 %collective-permute-start.39 = (bf16[1,224,128]{2,1,0:T(8,128)(2,1)}, bf16[1,224,128]{2,1,0:T(8,128)(2,1)}, u32[]{:S(2)}, u32[]{:S(2)}) collective-permute-start(bf16[1,224,128]{2,1,0:T(8,128)(2,1)} %get-tuple-element.151), channel_id=1, source_target_pairs={{0,8},{1,9},{2,10},{3,11},{4,12},{5,13},{6,14},{7,15},{8,0},{9,1},... | collective-permute-start | bytes 172040 | tf_op jit(solution)/shard_map/ppermute | solution.py:36
  255.6 24.8 %collective-permute-start.40 = (bf16[1,224,128]{2,1,0:T(8,128)(2,1)}, bf16[1,224,128]{2,1,0:T(8,128)(2,1)}, u32[]{:S(2)}, u32[]{:S(2)}) collective-permute-start(bf16[1,224,128]{2,1,0:T(8,128)(2,1)} %get-tuple-element.152), channel_id=1, source_target_pairs={{0,16},{1,17},{2,18},{3,19},{4,20},{5,21},{6,22},{7,23},{8,24},{9,... | collective-permute-start | bytes 172040 | tf_op jit(solution)/shard_map/ppermute | solution.py:36
  259.9 20.5 %collective-permute-start.41 = (bf16[1,224,128]{2,1,0:T(8,128)(2,1)S(1)}, bf16[1,224,128]{2,1,0:T(8,128)(2,1)}, u32[]{:S(2)}, u32[]{:S(2)}) collective-permute-start(bf16[1,224,128]{2,1,0:T(8,128)(2,1)S(1)} %get-tuple-element.153), channel_id=1, source_target_pairs={{0,24},{1,25},{2,26},{3,27},{4,28},{5,29},{6,30},{7,31},{8,16},{9,... | collective-permute-start | bytes 172040 | tf_op jit(solution)/shard_map/ppermute | solution.py:36
  (50 other events, 1012.3 us)

commit v3 on v2

--- a/solution.py
+++ b/solution.py
@@ -654,7 +654,7 @@
             down_copy.wait()
         for c in range(wide):
             cols = slice(c * width, (c + 1) * width)
-            down_rows[cols, :] = down_acc[:, cols].T
+            down_rows[cols, :] = down_acc[:, cols].astype(down_rows.dtype).T
         if len(sums) > 2:
             for ref, value in zip(sums, (up_acc, down_rows, wo_acc, bu_acc, bd_acc)):
                 ref[...] = value[...]
@@ -692,7 +692,7 @@
             quarter = half // 4
             for q in range(4):
                 some = slice(q * quarter, (q + 1) * quarter)
-                lax.fori_loop(some.start, some.stop, pack, 0, unroll=2)
+                lax.fori_loop(some.start, some.stop, pack, 0, unroll=4)
                 leaving.append(
                     pltpu.make_async_copy(
                         ref.at[some], sums[part].at[some], out_sems.at[part, q]
@@ -712,7 +712,7 @@
         pltpu.VMEM((width, width), F32),
         pltpu.VMEM((1, hidden), F32),
         pltpu.VMEM((1, width), F32),
-        pltpu.VMEM((hidden, width), F32),
+        pltpu.VMEM((hidden, width), BF16 if shards else F32),
         pltpu.VMEM((2, count, hidden), BF16),
         pltpu.SemaphoreType.DMA((2,)),
         pltpu.SemaphoreType.DMA((1,)),

time: 283 us -> 282 us (level)
  no operation moved by 1% of the time
where the time goes in v3:
time: 282 us
  Pallas kernels  126 us (45%)
  starting transfers between devices  71.2 us (25%)
  waiting for transfers between devices  70 us (25%)
  local copies, waits for them, and re-layouts  13.2 us (5%)
    ppermute x34, waiting for transfers between devices, swap(): return lax.ppermute(block, AXES, [(i, i ^ bits) for i in range(devices)])  60.4 us
    ppermute x34, starting transfers between devices, swap(): return lax.ppermute(block, AXES, [(i, i ^ bits) for i in range(devices)])  54.4 us
    pallas_call x1, Pallas kernels, feed(): pl.pallas_call(lambda *refs: feed_kernel(*refs, shards=len(shards or ()))...  40.7 us
    pallas_call x2, Pallas kernels, attend_back(): pl.pallas_call(lambda *refs: attend_back_kernel(*refs, started=bool(carri...  36 us
    pallas_call x1, Pallas kernels, attend(): pl.pallas_call(attend_kernel, grid=(samples,), in_specs=[per_sample((each...  18.6 us
    ppermute x8, starting transfers between devices, from_behind(): lax.ppermute(block, 'patch', [((i - distance) % count, i) for i in range(...  16.8 us
    unnamed x80, local copies, waits for them, and re-layouts  13.1 us
    ppermute x8, waiting for transfers between devices, from_behind(): lax.ppermute(block, 'patch', [((i - distance) % count, i) for i in range(...  9.68 us
  transfers between devices with their start and end apart: 42, of which 14 were waited for; matrix products, arithmetic and copies ran while one was open for 0% of the time, Pallas kernels for 19%

profile of v3, /device:TPU:0, one launch (start us, length us, event | category | flops | bytes accessed | tf_op | source)
XLA Modules:
  0.0 282.0 jit_solution(3522531985618890061)
XLA Ops:
  0.6 4.2 %shard_map.238 = (bf16[4,64,512]{2,1,0:T(8,128)(2,1)}, bf16[4,64,512]{2,1,0:T(8,128)(2,1)}, bf16[4,64,512]{2,1,0:T(8,128)(2,1)}, bf16[4,64,512]{2,1,0:T(8,128)(2...) custom-call(bf16[4,512,512]{2,1,0:T(8,128)(2,1)} %nodes_ref.1, s32[4,64]{1,0:T(4,128)} %refs_1_.4, ...), custom_call_target="tpu_custom_call" | custom-call | tf_op jit(solution)/shard_map/pallas_call | solution.py:205
  4.8 3.1 %collective-permute-start.14 = (bf16[1,592,128]{2,1,0:T(8,128)(2,1)}, bf16[1,592,128]{2,1,0:T(8,128)(2,1)S(1)}, u32[]{:S(2)}, u32[]{:S(2)}) collective-permute-start(bf16[1,592,128]{2,1,0:T(8,128)(2,1)} %get-tuple-element.105.refs_0_), channel_id=1, source_target_pairs={{0,8},{1,9},{2,10},{3,11},{4,12},{5,13},{6,14},{7,15},{8,0},{9,1},... | collective-permute-start | bytes 454664 | tf_op jit(solution)/shard_map/ppermute | solution.py:36
  8.7 3.7 %shard_map.239.refs_4_ = f32[768,512]{1,0:T(8,128)S(1)} custom-call(s32[16,512]{1,0:T(8,128)S(1)} %bitcast.8), custom_call_target="tpu_custom_call" | custom-call | tf_op jit(solution)/shard_map/pallas_call | solution.py:143
  13.6 4.4 %collective-permute-start.1 = (bf16[4,64,512]{2,1,0:T(8,128)(2,1)}, bf16[4,64,512]{2,1,0:T(8,128)(2,1)S(1)}, u32[]{:S(2)}, u32[]{:S(2)}) collective-permute-start(bf16[4,64,512]{2,1,0:T(8,128)(2,1)} %get-tuple-element.91), channel_id=1, source_target_pairs={{2,0},{4,2},{6,4},{8,6},{10,8},{12,10},{14,12},{16,14},{18,16},{20... | collective-permute-start | bytes 786440 | tf_op jit(solution)/shard_map/ppermute | solution.py:32
  20.6 7.7 %collective-permute-done.5.refs_2_ = bf16[1,208,128]{2,1,0:T(8,128)(2,1)S(1)} collective-permute-done((bf16[1,208,128]{2,1,0:T(8,128)(2,1)}, bf16[1,208,128]{2,1,0:T(8,128)(2,1)S(1)}, u32[]{:S(2)}, u32[]{:S(2)}) %collective-permute-start.5) | collective-permute-done | bytes 53280 | tf_op jit(solution)/shard_map/ppermute | solution.py:36
  28.3 3.2 %collective-permute-start.2 = (bf16[4,64,512]{2,1,0:T(8,128)(2,1)}, bf16[4,64,512]{2,1,0:T(8,128)(2,1)S(1)}, u32[]{:S(2)}, u32[]{:S(2)}) collective-permute-start(bf16[4,64,512]{2,1,0:T(8,128)(2,1)} %get-tuple-element.93), channel_id=1, source_target_pairs={{24,0},{26,2},{28,4},{30,6},{0,8},{2,10},{4,12},{6,14},{8,16},{10,... | collective-permute-start | bytes 786440 | tf_op jit(solution)/shard_map/ppermute | solution.py:32
  32.9 14.0 %collective-permute-done.15.refs_2_ = bf16[1,592,128]{2,1,0:T(8,128)(2,1)S(1)} collective-permute-done((bf16[1,592,128]{2,1,0:T(8,128)(2,1)}, bf16[1,592,128]{2,1,0:T(8,128)(2,1)S(1)}, u32[]{:S(2)}, u32[]{:S(2)}) %collective-permute-start.15) | collective-permute-done | bytes 151584 | tf_op jit(solution)/shard_map/ppermute | solution.py:36
  47.9 2.1 collective-permute-start.17
  52.1 2.9 %collective-permute-done.7.refs_4_ = bf16[4,208,128]{2,1,0:T(8,128)(2,1)S(1)} collective-permute-done((bf16[4,208,128]{2,1,0:T(8,128)(2,1)S(1)}, bf16[4,208,128]{2,1,0:T(8,128)(2,1)S(1)}, u32[]{:S(2)}, u32[]{:S(2)}) %collective-permute-start.7) | collective-permute-done | bytes 213024 | tf_op jit(solution)/shard_map/ppermute | solution.py:36
  55.0 26.1 %collective-permute-done.8.refs_5_ = bf16[4,208,128]{2,1,0:T(8,128)(2,1)S(1)} collective-permute-done((bf16[4,208,128]{2,1,0:T(8,128)(2,1)S(1)}, bf16[4,208,128]{2,1,0:T(8,128)(2,1)S(1)}, u32[]{:S(2)}, u32[]{:S(2)}) %collective-permute-start.8) | collective-permute-done | bytes 213024 | tf_op jit(solution)/shard_map/ppermute | solution.py:36
  81.1 3.2 %collective-permute-done.9.refs_6_ = bf16[4,208,128]{2,1,0:T(8,128)(2,1)S(1)} collective-permute-done((bf16[4,208,128]{2,1,0:T(8,128)(2,1)S(1)}, bf16[4,208,128]{2,1,0:T(8,128)(2,1)S(1)}, u32[]{:S(2)}, u32[]{:S(2)}) %collective-permute-start.9) | collective-permute-done | bytes 213024 | tf_op jit(solution)/shard_map/ppermute | solution.py:36
  87.0 3.8 %collective-permute-done.13.refs_10_ = bf16[4,208,128]{2,1,0:T(8,128)(2,1)S(1)} collective-permute-done((bf16[4,208,128]{2,1,0:T(8,128)(2,1)S(1)}, bf16[4,208,128]{2,1,0:T(8,128)(2,1)S(1)}, u32[]{:S(2)}, u32[]{:S(2)}) %collective-permute-start.13) | collective-permute-done | bytes 213024 | tf_op jit(solution)/shard_map/ppermute | solution.py:36
  91.5 9.4 %shard_map.241 = (bf16[512,512]{1,0:T(8,128)(2,1)}, bf16[512,512]{1,0:T(8,128)(2,1)}, bf16[512,512]{1,0:T(8,128)(2,1)}, f32[4,4,512]{2,1,0:T(4,128)}, bf16[4,512...) custom-call(bf16[4,512,512]{2,1,0:T(8,128)(2,1)} %nodes_ref.1, ...), custom_call_target="tpu_custom_call" | custom-call | tf_op jit(solution)/shard_map/pallas_call | solution.py:445
  102.0 18.6 %shard_map.242 = (bf16[4,768,512]{2,1,0:T(8,128)(2,1)}, bf16[4,768,512]{2,1,0:T(8,128)(2,1)}, bf16[4,768,512]{2,1,0:T(8,128)(2,1)}, bf16[4,4,768,512]{3,2,1,0:T(8,128)(2,1)}, bf16[4,512,512]{2,1,0:T(8,128)(2,1)}) custom-call(bf16[4,64,512]{2,1,0:T(8,128)(2,1)} %copy-done.9, bf16[4,64,512]{2,1,0:T(8,128)(2,1)} %copy-done.11, bf16[4,64,512]{2,1,0:T(8,128)(2,1)} %copy-done.13, ...), custom_call_target="tpu_custom_call" | custom-call | tf_op jit(solution)/shard_map/pallas_call | solution.py:530
  120.8 40.7 %shard_map.244 = (f32[4,512,512]{2,1,0:T(8,128)}, f32[4,512,512]{2,1,0:T(8,128)}, bf16[4,512,512]{2,1,0:T(8,128)(2,1)}, f32[4,2,512]{2,1,0:T(2,128)}, bf16[4,512...) custom-call(s32[1]{0:T(128)} %bitcast.refs_1_.refs_0_, ...), custom_call_target="tpu_custom_call" | custom-call | tf_op jit(solution)/shard_map/pallas_call | solution.py:739
  162.3 10.3 %shard_map.248 = (f32[4,512,512]{2,1,0:T(8,128)}, bf16[4,64,512]{2,1,0:T(8,128)(2,1)S(1)}, bf16[4,64,512]{2,1,0:T(8,128)(2,1)S(1)}, bf16[4,64,512]{2,1,0:T(8,128...) custom-call(s32[1]{0:T(128)} %bitcast.refs_1_.refs_0_, ...), custom_call_target="tpu_custom_call" | custom-call | tf_op jit(solution)/shard_map/pallas_call | solution.py:978
  173.6 25.7 %shard_map.249 = (f32[4,512,512]{2,1,0:T(8,128)}, bf16[4,64,512]{2,1,0:T(8,128)(2,1)S(1)}, bf16[4,64,512]{2,1,0:T(8,128)(2,1)S(1)}, bf16[4,64,512]{2,1,0:T(8,128...) custom-call(s32[1]{0:T(128)} %bitcast.refs_1_.refs_0_, ...), custom_call_target="tpu_custom_call", output_to_operand_aliasing={{0}: (24, {}), {1}: (25, {}), {2}: (26, {}), {3}: (27, {}),... | custom-call | tf_op jit(solution)/shard_map/pallas_call | solution.py:978
  200.3 1.7 collective-permute-start.26
  203.3 4.4 %collective-permute-start.28 = (bf16[4,64,512]{2,1,0:T(8,128)(2,1)S(1)}, bf16[4,64,512]{2,1,0:T(8,128)(2,1)S(1)}, u32[]{:S(2)}, u32[]{:S(2)}) collective-permute-start(bf16[4,64,512]{2,1,0:T(8,128)(2,1)S(1)} %get-tuple-element.137), channel_id=1, source_target_pairs={{2,0},{4,2},{6,4},{8,6},{10,8},{12,10},{14,12},{16,14},{18,16},{20... | collective-permute-start | bytes 786440 | tf_op jit(solution)/shard_map/ppermute | solution.py:32
  208.0 3.7 %collective-permute-done.28.b0 = bf16[4,64,512]{2,1,0:T(8,128)(2,1)S(1)} collective-permute-done((bf16[4,64,512]{2,1,0:T(8,128)(2,1)S(1)}, bf16[4,64,512]{2,1,0:T(8,128)(2,1)S(1)}, u32[]{:S(2)}, u32[]{:S(2)}) %collective-permute-start.28) | collective-permute-done | bytes 262176 | tf_op jit(solution)/shard_map/ppermute | solution.py:32
  212.3 4.0 %collective-permute-done.29.b1 = bf16[4,64,512]{2,1,0:T(8,128)(2,1)S(1)} collective-permute-done((bf16[4,64,512]{2,1,0:T(8,128)(2,1)S(1)}, bf16[4,64,512]{2,1,0:T(8,128)(2,1)S(1)}, u32[]{:S(2)}, u32[]{:S(2)}) %collective-permute-start.29) | collective-permute-done | bytes 262176 | tf_op jit(solution)/shard_map/ppermute | solution.py:32
  216.4 19.6 %collective-permute-start.37 = (bf16[4,224,128]{2,1,0:T(8,128)(2,1)S(1)}, bf16[4,224,128]{2,1,0:T(8,128)(2,1)S(1)}, u32[]{:S(2)}, u32[]{:S(2)}) collective-permute-start(bf16[4,224,128]{2,1,0:T(8,128)(2,1)S(1)} %get-tuple-element.148), channel_id=1, source_target_pairs={{0,4},{1,5},{2,6},{3,7},{4,0},{5,1},{6,2},{7,3},{8,12},{9,13},{10,... | collective-permute-start | bytes 688136 | tf_op jit(solution)/shard_map/ppermute | solution.py:36
  236.8 4.7 %collective-permute-start.30 = (bf16[4,64,512]{2,1,0:T(8,128)(2,1)S(1)}, bf16[4,64,512]{2,1,0:T(8,128)(2,1)S(1)}, u32[]{:S(2)}, u32[]{:S(2)}) collective-permute-start(bf16[4,64,512]{2,1,0:T(8,128)(2,1)S(1)} %get-tuple-element.139), channel_id=1, source_target_pairs={{8,0},{10,2},{12,4},{14,6},{16,8},{18,10},{20,12},{22,14},{24,16},... | collective-permute-start | bytes 786440 | tf_op jit(solution)/shard_map/ppermute | solution.py:32
  242.0 4.6 %collective-permute-start.33 = (bf16[1,592,128]{2,1,0:T(8,128)(2,1)S(1)}, bf16[1,592,128]{2,1,0:T(8,128)(2,1)}, u32[]{:S(2)}, u32[]{:S(2)}) collective-permute-start(bf16[1,592,128]{2,1,0:T(8,128)(2,1)S(1)} %get-tuple-element.142), channel_id=1, source_target_pairs={{0,16},{1,17},{2,18},{3,19},{4,20},{5,21},{6,22},{7,23},{8,24},{9,... | collective-permute-start | bytes 454664 | tf_op jit(solution)/shard_map/ppermute | solution.py:36
  247.7 4.5 %collective-permute-start.34 = (bf16[1,592,128]{2,1,0:T(8,128)(2,1)S(1)}, bf16[1,592,128]{2,1,0:T(8,128)(2,1)}, u32[]{:S(2)}, u32[]{:S(2)}) collective-permute-start(bf16[1,592,128]{2,1,0:T(8,128)(2,1)S(1)} %get-tuple-element.143), channel_id=1, source_target_pairs={{0,24},{1,25},{2,26},{3,27},{4,28},{5,29},{6,30},{7,31},{8,16},{9,... | collective-permute-start | bytes 454664 | tf_op jit(solution)/shard_map/ppermute | solution.py:36
  255.0 3.2 %collective-permute-start.40 = (bf16[1,224,128]{2,1,0:T(8,128)(2,1)}, bf16[1,224,128]{2,1,0:T(8,128)(2,1)}, u32[]{:S(2)}, u32[]{:S(2)}) collective-permute-start(bf16[1,224,128]{2,1,0:T(8,128)(2,1)} %get-tuple-element.152), channel_id=1, source_target_pairs={{0,16},{1,17},{2,18},{3,19},{4,20},{5,21},{6,22},{7,23},{8,24},{9,... | collective-permute-start | bytes 172040 | tf_op jit(solution)/shard_map/ppermute | solution.py:36
  259.3 4.8 %collective-permute-start.41 = (bf16[1,224,128]{2,1,0:T(8,128)(2,1)S(1)}, bf16[1,224,128]{2,1,0:T(8,128)(2,1)}, u32[]{:S(2)}, u32[]{:S(2)}) collective-permute-start(bf16[1,224,128]{2,1,0:T(8,128)(2,1)S(1)} %get-tuple-element.153), channel_id=1, source_target_pairs={{0,24},{1,25},{2,26},{3,27},{4,28},{5,29},{6,30},{7,31},{8,16},{9,... | collective-permute-start | bytes 172040 | tf_op jit(solution)/shard_map/ppermute | solution.py:36
  264.3 2.2 copy-done.1
  266.5 4.2 %shard_map.250 = f32[4,512,512]{2,1,0:T(8,128)} custom-call(bf16[4,512,512]{2,1,0:T(8,128)(2,1)S(1)} %copy-done, f32[4,512,512]{2,1,0:T(8,128)S(1)} %copy-done.1, bf16[4,64,512]{2,1,0:T(8,128)(2,1)S(1)} %collective-permute-done.28.b0, bf16[4,64,512]{2,1,0:T(8,128)(2,1)S(1)} %collective-permute-done.29.b1, ...), custom_call_target="tpu_custom_call" | custom-call | tf_op jit(solution)/shard_map/pallas_call | solution.py:1018
  270.6 3.4 %copy-done.2 = bf16[4,512,2048]{2,1,0:T(8,128)(2,1)S(1)} copy-done((bf16[4,512,2048]{2,1,0:T(8,128)(2,1)S(1)}, bf16[4,512,2048]{2,1,0:T(8,128)(2,1)}, u32[]{:S(2)}) %copy-start.2) | copy-done | bytes 8388632
  274.0 5.8 %shard_map.247 = bf16[4,512,512]{2,1,0:T(8,128)(2,1)} custom-call(bf16[4,512,2048]{2,1,0:T(8,128)(2,1)S(1)} %copy-done.2, bf16[2048,512]{1,0:T(8,128)(2,1)S(1)} %copy-done.18, f32[4,512,512]{2,1,0:T(8,128)S(1)} %copy-done.6), custom_call_target="tpu_custom_call" | custom-call | tf_op jit(solution)/shard_map/pallas_call | solution.py:769
  279.8 2.0 shard_map.253
  (149 shorter events, 24.8 us)
Async XLA Ops:
  4.8 26.7 %collective-permute-start.14 = (bf16[1,592,128]{2,1,0:T(8,128)(2,1)}, bf16[1,592,128]{2,1,0:T(8,128)(2,1)S(1)}, u32[]{:S(2)}, u32[]{:S(2)}) collective-permute-start(bf16[1,592,128]{2,1,0:T(8,128)(2,1)} %get-tuple-element.105.refs_0_), channel_id=1, source_target_pairs={{0,8},{1,9},{2,10},{3,11},{4,12},{5,13},{6,14},{7,15},{8,0},{9,1},... | collective-permute-start | bytes 454664 | tf_op jit(solution)/shard_map/ppermute | solution.py:36
  7.9 11.3 %collective-permute-start.4 = (bf16[1,208,128]{2,1,0:T(8,128)(2,1)}, bf16[1,208,128]{2,1,0:T(8,128)(2,1)S(1)}, u32[]{:S(2)}, u32[]{:S(2)}) collective-permute-start(bf16[1,208,128]{2,1,0:T(8,128)(2,1)} %get-tuple-element.96.refs_0_), channel_id=1, source_target_pairs={{0,8},{1,9},{2,10},{3,11},{4,12},{5,13},{6,14},{7,15},{8,0},{9,1},... | collective-permute-start | bytes 159752 | tf_op jit(solution)/shard_map/ppermute | solution.py:36
  13.6 36.3 %collective-permute-start = (bf16[4,64,512]{2,1,0:T(8,128)(2,1)}, bf16[4,64,512]{2,1,0:T(8,128)(2,1)S(1)}, u32[]{:S(2)}, u32[]{:S(2)}) collective-permute-start(bf16[4,64,512]{2,1,0:T(8,128)(2,1)} %get-tuple-element.89), channel_id=1, source_target_pairs={{30,0},{0,2},{2,4},{4,6},{6,8},{8,10},{10,12},{12,14},{14,16},{16,... | collective-permute-start | bytes 786440 | tf_op jit(solution)/shard_map/ppermute | solution.py:32
  13.6 36.3 %collective-permute-start.1 = (bf16[4,64,512]{2,1,0:T(8,128)(2,1)}, bf16[4,64,512]{2,1,0:T(8,128)(2,1)S(1)}, u32[]{:S(2)}, u32[]{:S(2)}) collective-permute-start(bf16[4,64,512]{2,1,0:T(8,128)(2,1)} %get-tuple-element.91), channel_id=1, source_target_pairs={{2,0},{4,2},{6,4},{8,6},{10,8},{12,10},{14,12},{16,14},{18,16},{20... | collective-permute-start | bytes 786440 | tf_op jit(solution)/shard_map/ppermute | solution.py:32
  28.3 18.6 %collective-permute-start.15 = (bf16[1,592,128]{2,1,0:T(8,128)(2,1)}, bf16[1,592,128]{2,1,0:T(8,128)(2,1)S(1)}, u32[]{:S(2)}, u32[]{:S(2)}) collective-permute-start(bf16[1,592,128]{2,1,0:T(8,128)(2,1)} %get-tuple-element.105.refs_0_), channel_id=1, source_target_pairs={{0,16},{1,17},{2,18},{3,19},{4,20},{5,21},{6,22},{7,23},{8,24},{9,... | collective-permute-start | bytes 454664 | tf_op jit(solution)/shard_map/ppermute | solution.py:36
  28.3 23.3 %collective-permute-start.2 = (bf16[4,64,512]{2,1,0:T(8,128)(2,1)}, bf16[4,64,512]{2,1,0:T(8,128)(2,1)S(1)}, u32[]{:S(2)}, u32[]{:S(2)}) collective-permute-start(bf16[4,64,512]{2,1,0:T(8,128)(2,1)} %get-tuple-element.93), channel_id=1, source_target_pairs={{24,0},{26,2},{28,4},{30,6},{0,8},{2,10},{4,12},{6,14},{8,16},{10,... | collective-permute-start | bytes 786440 | tf_op jit(solution)/shard_map/ppermute | solution.py:32
  31.5 15.4 %collective-permute-start.16 = (bf16[1,592,128]{2,1,0:T(8,128)(2,1)}, bf16[1,592,128]{2,1,0:T(8,128)(2,1)S(1)}, u32[]{:S(2)}, u32[]{:S(2)}) collective-permute-start(bf16[1,592,128]{2,1,0:T(8,128)(2,1)} %get-tuple-element.105.refs_0_), channel_id=1, source_target_pairs={{0,24},{1,25},{2,26},{3,27},{4,28},{5,29},{6,30},{7,31},{8,16},{9,... | collective-permute-start | bytes 454664 | tf_op jit(solution)/shard_map/ppermute | solution.py:36
  47.9 38.1 %collective-permute-start.17 = (bf16[4,592,128]{2,1,0:T(8,128)(2,1)S(1)}, bf16[4,592,128]{2,1,0:T(8,128)(2,1)S(1)}, u32[]{:S(2)}, u32[]{:S(2)}) collective-permute-start(bf16[4,592,128]{2,1,0:T(8,128)(2,1)S(1)} %shard_map.243.refs_5_), channel_id=1, source_target_pairs={{0,1},{1,0},{2,3},{3,2},{4,5},{5,4},{6,7},{7,6},{8,9},{9,8},{10,11... | collective-permute-start | bytes 1818632 | tf_op jit(solution)/shard_map/ppermute | solution.py:36
  49.9 36.4 %collective-permute-start.18 = (bf16[4,592,128]{2,1,0:T(8,128)(2,1)S(1)}, bf16[4,592,128]{2,1,0:T(8,128)(2,1)S(1)}, u32[]{:S(2)}, u32[]{:S(2)}) collective-permute-start(bf16[4,592,128]{2,1,0:T(8,128)(2,1)S(1)} %shard_map.243.refs_5_), channel_id=1, source_target_pairs={{0,4},{1,5},{2,6},{3,7},{4,0},{5,1},{6,2},{7,3},{8,12},{9,13},{10,... | collective-permute-start | bytes 1818632 | tf_op jit(solution)/shard_map/ppermute | solution.py:36
  50.0 36.5 %collective-permute-start.19 = (bf16[4,592,128]{2,1,0:T(8,128)(2,1)S(1)}, bf16[4,592,128]{2,1,0:T(8,128)(2,1)}, u32[]{:S(2)}, u32[]{:S(2)}) collective-permute-start(bf16[4,592,128]{2,1,0:T(8,128)(2,1)S(1)} %shard_map.243.refs_5_), channel_id=1, source_target_pairs={{0,5},{1,4},{2,7},{3,6},{4,1},{5,0},{6,3},{7,2},{8,13},{9,12},{10,... | collective-permute-start | bytes 1818632 | tf_op jit(solution)/shard_map/ppermute | solution.py:36
  51.5 29.6 %collective-permute-start.8 = (bf16[4,208,128]{2,1,0:T(8,128)(2,1)S(1)}, bf16[4,208,128]{2,1,0:T(8,128)(2,1)S(1)}, u32[]{:S(2)}, u32[]{:S(2)}) collective-permute-start(bf16[4,208,128]{2,1,0:T(8,128)(2,1)S(1)} %shard_map.240.refs_3_), channel_id=1, source_target_pairs={{0,4},{1,5},{2,6},{3,7},{4,0},{5,1},{6,2},{7,3},{8,12},{9,13},{10,... | collective-permute-start | bytes 638984 | tf_op jit(solution)/shard_map/ppermute | solution.py:36
  55.0 29.4 %collective-permute-start.9 = (bf16[4,208,128]{2,1,0:T(8,128)(2,1)S(1)}, bf16[4,208,128]{2,1,0:T(8,128)(2,1)S(1)}, u32[]{:S(2)}, u32[]{:S(2)}) collective-permute-start(bf16[4,208,128]{2,1,0:T(8,128)(2,1)S(1)} %shard_map.240.refs_3_), channel_id=1, source_target_pairs={{0,5},{1,4},{2,7},{3,6},{4,1},{5,0},{6,3},{7,2},{8,13},{9,12},{10,... | collective-permute-start | bytes 638984 | tf_op jit(solution)/shard_map/ppermute | solution.py:36
  85.8 34.8 %collective-permute-start.20 = (bf16[4,592,128]{2,1,0:T(8,128)(2,1)S(1)}, bf16[4,592,128]{2,1,0:T(8,128)(2,1)}, u32[]{:S(2)}, u32[]{:S(2)}) collective-permute-start(bf16[4,592,128]{2,1,0:T(8,128)(2,1)S(1)} %shard_map.243.refs_5_), channel_id=1, source_target_pairs={{0,2},{1,3},{2,0},{3,1},{4,6},{5,7},{6,4},{7,5},{8,10},{9,11},{10,... | collective-permute-start | bytes 1818632 | tf_op jit(solution)/shard_map/ppermute | solution.py:36
  86.0 34.6 %collective-permute-start.21 = (bf16[4,592,128]{2,1,0:T(8,128)(2,1)S(1)}, bf16[4,592,128]{2,1,0:T(8,128)(2,1)}, u32[]{:S(2)}, u32[]{:S(2)}) collective-permute-start(bf16[4,592,128]{2,1,0:T(8,128)(2,1)S(1)} %collective-permute-done.17.refs_6_), channel_id=1, source_target_pairs={{0,2},{1,3},{2,0},{3,1},{4,6},{5,7},{6,4},{7,5},{8,10},{9,11},{10,... | collective-permute-start | bytes 1818632 | tf_op jit(solution)/shard_map/ppermute | solution.py:36
  86.4 34.3 %collective-permute-start.22 = (bf16[4,592,128]{2,1,0:T(8,128)(2,1)S(1)}, bf16[4,592,128]{2,1,0:T(8,128)(2,1)}, u32[]{:S(2)}, u32[]{:S(2)}) collective-permute-start(bf16[4,592,128]{2,1,0:T(8,128)(2,1)S(1)} %collective-permute-done.18.refs_7_), channel_id=1, source_target_pairs={{0,2},{1,3},{2,0},{3,1},{4,6},{5,7},{6,4},{7,5},{8,10},{9,11},{10,... | collective-permute-start | bytes 1818632 | tf_op jit(solution)/shard_map/ppermute | solution.py:36
  86.5 34.1 %collective-permute-start.23 = (bf16[4,592,128]{2,1,0:T(8,128)(2,1)}, bf16[4,592,128]{2,1,0:T(8,128)(2,1)}, u32[]{:S(2)}, u32[]{:S(2)}) collective-permute-start(bf16[4,592,128]{2,1,0:T(8,128)(2,1)} %collective-permute-done.19.refs_8_), channel_id=1, source_target_pairs={{0,2},{1,3},{2,0},{3,1},{4,6},{5,7},{6,4},{7,5},{8,10},{9,11},{10,... | collective-permute-start | bytes 1818632 | tf_op jit(solution)/shard_map/ppermute | solution.py:36
  90.8 10.5 %collective-permute-start.3 = (bf16[4,64,512]{2,1,0:T(8,128)(2,1)}, bf16[4,64,512]{2,1,0:T(8,128)(2,1)S(1)}, u32[]{:S(2)}, u32[]{:S(2)}) collective-permute-start(bf16[4,64,512]{2,1,0:T(8,128)(2,1)} %get-tuple-element.95), channel_id=1, source_target_pairs={{8,0},{10,2},{12,4},{14,6},{16,8},{18,10},{20,12},{22,14},{24,16},... | collective-permute-start | bytes 786440 | tf_op jit(solution)/shard_map/ppermute | solution.py:32
  161.4 11.2 %collective-permute-start.24 = (bf16[16,592,128]{2,1,0:T(8,128)(2,1)}, bf16[16,592,128]{2,1,0:T(8,128)(2,1)S(1)}, u32[]{:S(2)}, u32[]{:S(2)}) collective-permute-start(bf16[16,592,128]{2,1,0:T(8,128)(2,1)} %get-tuple-element.110), channel_id=1, source_target_pairs={{0,2},{1,3},{2,0},{3,1},{4,6},{5,7},{6,4},{7,5},{8,10},{9,11},{10,... | collective-permute-start | bytes 7274504 | tf_op jit(solution)/shard_map/ppermute | solution.py:36
  199.8 36.1 %collective-permute-start.25 = (bf16[4,592,128]{2,1,0:T(8,128)(2,1)S(1)}, bf16[4,592,128]{2,1,0:T(8,128)(2,1)S(1)}, u32[]{:S(2)}, u32[]{:S(2)}) collective-permute-start(bf16[4,592,128]{2,1,0:T(8,128)(2,1)S(1)} %get-tuple-element.112), channel_id=1, source_target_pairs={{0,1},{1,0},{2,3},{3,2},{4,5},{5,4},{6,7},{7,6},{8,9},{9,8},{10,11... | collective-permute-start | bytes 1818632 | tf_op jit(solution)/shard_map/ppermute | solution.py:36
  200.3 36.5 %collective-permute-start.26 = (bf16[4,592,128]{2,1,0:T(8,128)(2,1)S(1)}, bf16[4,592,128]{2,1,0:T(8,128)(2,1)S(1)}, u32[]{:S(2)}, u32[]{:S(2)}) collective-permute-start(bf16[4,592,128]{2,1,0:T(8,128)(2,1)S(1)} %get-tuple-element.113), channel_id=1, source_target_pairs={{0,4},{1,5},{2,6},{3,7},{4,0},{5,1},{6,2},{7,3},{8,12},{9,13},{10,... | collective-permute-start | bytes 1818632 | tf_op jit(solution)/shard_map/ppermute | solution.py:36
  202.0 39.5 %collective-permute-start.27 = (bf16[4,592,128]{2,1,0:T(8,128)(2,1)S(1)}, bf16[4,592,128]{2,1,0:T(8,128)(2,1)S(1)}, u32[]{:S(2)}, u32[]{:S(2)}) collective-permute-start(bf16[4,592,128]{2,1,0:T(8,128)(2,1)S(1)} %get-tuple-element.114), channel_id=1, source_target_pairs={{0,5},{1,4},{2,7},{3,6},{4,1},{5,0},{6,3},{7,2},{8,13},{9,12},{10,... | collective-permute-start | bytes 1818632 | tf_op jit(solution)/shard_map/ppermute | solution.py:36
  211.7 30.1 %collective-permute-start.36 = (bf16[4,224,128]{2,1,0:T(8,128)(2,1)S(1)}, bf16[4,224,128]{2,1,0:T(8,128)(2,1)S(1)}, u32[]{:S(2)}, u32[]{:S(2)}) collective-permute-start(bf16[4,224,128]{2,1,0:T(8,128)(2,1)S(1)} %get-tuple-element.147), channel_id=1, source_target_pairs={{0,1},{1,0},{2,3},{3,2},{4,5},{5,4},{6,7},{7,6},{8,9},{9,8},{10,11... | collective-permute-start | bytes 688136 | tf_op jit(solution)/shard_map/ppermute | solution.py:36
  216.4 25.6 %collective-permute-start.37 = (bf16[4,224,128]{2,1,0:T(8,128)(2,1)S(1)}, bf16[4,224,128]{2,1,0:T(8,128)(2,1)S(1)}, u32[]{:S(2)}, u32[]{:S(2)}) collective-permute-start(bf16[4,224,128]{2,1,0:T(8,128)(2,1)S(1)} %get-tuple-element.148), channel_id=1, source_target_pairs={{0,4},{1,5},{2,6},{3,7},{4,0},{5,1},{6,2},{7,3},{8,12},{9,13},{10,... | collective-permute-start | bytes 688136 | tf_op jit(solution)/shard_map/ppermute | solution.py:36
  236.0 11.7 %collective-permute-start.38 = (bf16[4,224,128]{2,1,0:T(8,128)(2,1)S(1)}, bf16[4,224,128]{2,1,0:T(8,128)(2,1)S(1)}, u32[]{:S(2)}, u32[]{:S(2)}) collective-permute-start(bf16[4,224,128]{2,1,0:T(8,128)(2,1)S(1)} %get-tuple-element.149), channel_id=1, source_target_pairs={{0,5},{1,4},{2,7},{3,6},{4,1},{5,0},{6,3},{7,2},{8,13},{9,12},{10,... | collective-permute-start | bytes 688136 | tf_op jit(solution)/shard_map/ppermute | solution.py:36
  236.8 16.7 %collective-permute-start.30 = (bf16[4,64,512]{2,1,0:T(8,128)(2,1)S(1)}, bf16[4,64,512]{2,1,0:T(8,128)(2,1)S(1)}, u32[]{:S(2)}, u32[]{:S(2)}) collective-permute-start(bf16[4,64,512]{2,1,0:T(8,128)(2,1)S(1)} %get-tuple-element.139), channel_id=1, source_target_pairs={{8,0},{10,2},{12,4},{14,6},{16,8},{18,10},{20,12},{22,14},{24,16},... | collective-permute-start | bytes 786440 | tf_op jit(solution)/shard_map/ppermute | solution.py:32
  241.5 13.5 %collective-permute-start.31 = (bf16[4,64,512]{2,1,0:T(8,128)(2,1)S(1)}, bf16[4,64,512]{2,1,0:T(8,128)(2,1)S(1)}, u32[]{:S(2)}, u32[]{:S(2)}) collective-permute-start(bf16[4,64,512]{2,1,0:T(8,128)(2,1)S(1)} %get-tuple-element.140), channel_id=1, source_target_pairs={{24,0},{26,2},{28,4},{30,6},{0,8},{2,10},{4,12},{6,14},{8,16},{10,... | collective-permute-start | bytes 786440 | tf_op jit(solution)/shard_map/ppermute | solution.py:32
  241.8 16.9 %collective-permute-start.32 = (bf16[1,592,128]{2,1,0:T(8,128)(2,1)S(1)}, bf16[1,592,128]{2,1,0:T(8,128)(2,1)S(1)}, u32[]{:S(2)}, u32[]{:S(2)}) collective-permute-start(bf16[1,592,128]{2,1,0:T(8,128)(2,1)S(1)} %get-tuple-element.141), channel_id=1, source_target_pairs={{0,8},{1,9},{2,10},{3,11},{4,12},{5,13},{6,14},{7,15},{8,0},{9,1},... | collective-permute-start | bytes 454664 | tf_op jit(solution)/shard_map/ppermute | solution.py:36
  242.0 37.8 %collective-permute-start.33 = (bf16[1,592,128]{2,1,0:T(8,128)(2,1)S(1)}, bf16[1,592,128]{2,1,0:T(8,128)(2,1)}, u32[]{:S(2)}, u32[]{:S(2)}) collective-permute-start(bf16[1,592,128]{2,1,0:T(8,128)(2,1)S(1)} %get-tuple-element.142), channel_id=1, source_target_pairs={{0,16},{1,17},{2,18},{3,19},{4,20},{5,21},{6,22},{7,23},{8,24},{9,... | collective-permute-start | bytes 454664 | tf_op jit(solution)/shard_map/ppermute | solution.py:36
  247.7 32.1 %collective-permute-start.34 = (bf16[1,592,128]{2,1,0:T(8,128)(2,1)S(1)}, bf16[1,592,128]{2,1,0:T(8,128)(2,1)}, u32[]{:S(2)}, u32[]{:S(2)}) collective-permute-start(bf16[1,592,128]{2,1,0:T(8,128)(2,1)S(1)} %get-tuple-element.143), channel_id=1, source_target_pairs={{0,24},{1,25},{2,26},{3,27},{4,28},{5,29},{6,30},{7,31},{8,16},{9,... | collective-permute-start | bytes 454664 | tf_op jit(solution)/shard_map/ppermute | solution.py:36
  253.5 26.4 %collective-permute-start.39 = (bf16[1,224,128]{2,1,0:T(8,128)(2,1)}, bf16[1,224,128]{2,1,0:T(8,128)(2,1)}, u32[]{:S(2)}, u32[]{:S(2)}) collective-permute-start(bf16[1,224,128]{2,1,0:T(8,128)(2,1)} %get-tuple-element.151), channel_id=1, source_target_pairs={{0,8},{1,9},{2,10},{3,11},{4,12},{5,13},{6,14},{7,15},{8,0},{9,1},... | collective-permute-start | bytes 172040 | tf_op jit(solution)/shard_map/ppermute | solution.py:36
  255.0 24.8 %collective-permute-start.40 = (bf16[1,224,128]{2,1,0:T(8,128)(2,1)}, bf16[1,224,128]{2,1,0:T(8,128)(2,1)}, u32[]{:S(2)}, u32[]{:S(2)}) collective-permute-start(bf16[1,224,128]{2,1,0:T(8,128)(2,1)} %get-tuple-element.152), channel_id=1, source_target_pairs={{0,16},{1,17},{2,18},{3,19},{4,20},{5,21},{6,22},{7,23},{8,24},{9,... | collective-permute-start | bytes 172040 | tf_op jit(solution)/shard_map/ppermute | solution.py:36
  259.3 20.5 %collective-permute-start.41 = (bf16[1,224,128]{2,1,0:T(8,128)(2,1)S(1)}, bf16[1,224,128]{2,1,0:T(8,128)(2,1)}, u32[]{:S(2)}, u32[]{:S(2)}) collective-permute-start(bf16[1,224,128]{2,1,0:T(8,128)(2,1)S(1)} %get-tuple-element.153), channel_id=1, source_target_pairs={{0,24},{1,25},{2,26},{3,27},{4,28},{5,29},{6,30},{7,31},{8,16},{9,... | collective-permute-start | bytes 172040 | tf_op jit(solution)/shard_map/ppermute | solution.py:36
  (50 other events, 1007.3 us)
